TPU v7x, 32 devices: a whole 2x2x4 slice. The times are simulated.
32 devices in a mesh: dp: 8 (over y, x, core), tensor: 4 (over z).
Axes of the slice: x: 2, y: 2, z: 4, core: 2. Of those that a mesh axis runs over, the one named last changes fastest.
Arguments:
- tokens: bfloat16 [16384, 768], P(('dp', 'tensor')), may hold values from -6 to 6
- starts: int32 [8, 8], P('dp'), may hold values from 0 to 2047, as said below
- w_qkv: bfloat16 [768, 2304], P(None, 'tensor'), may hold values from -0.21875 to 0.21875
- b_qkv: bfloat16 [2304], P('tensor'), may hold values from -3 to 3
- w_out: bfloat16 [768, 768], P('tensor'), may hold values from -2 to 2
- b_out: bfloat16 [768], replicated, may hold values from -3 to 3
- gain_one: bfloat16 [768], replicated, may hold values from 0.099609375 to 1.8984375
- shift_one: bfloat16 [768], replicated, may hold values from -3 to 3
- w_in: bfloat16 [768, 3072], P(None, 'tensor'), may hold values from -0.21875 to 0.21875
- b_in: bfloat16 [3072], P('tensor'), may hold values from -3 to 3
- w_two: bfloat16 [3072, 768], P('tensor'), may hold values from -0.21875 to 0.21875
- b_two: bfloat16 [768], replicated, may hold values from -3 to 3
- gain_two: bfloat16 [768], replicated, may hold values from 0.099609375 to 1.8984375
- shift_two: bfloat16 [768], replicated, may hold values from -3 to 3
- cotangent: bfloat16 [16384, 768], P(('dp', 'tensor')), may hold values from -6 to 6
Outputs:
- block_out: bfloat16 [16384, 768], P(('dp', 'tensor'))
- d_tokens: bfloat16 [16384, 768], P(('dp', 'tensor'))
- d_w_qkv: float32 [768, 2304], P(None, 'tensor')
- d_b_qkv: float32 [2304], P('tensor')
- d_w_out: float32 [768, 768], P('tensor')
- d_b_out: float32 [768], replicated
- d_gain_one: float32 [768], replicated
- d_shift_one: float32 [768], replicated
- d_w_in: float32 [768, 3072], P(None, 'tensor')
- d_b_in: float32 [3072], P('tensor')
- d_w_two: float32 [3072, 768], P('tensor')
- d_b_two: float32 [768], replicated
- d_gain_two: float32 [768], replicated
- d_shift_two: float32 [768], replicated
Inputs may be any that keep to these rules, and one draw needn't show every extreme that they name: Each row holds exactly 8 documents: its first start is 0 and its starts rise strictly. In the first row the last document is a single token.
All inputs are finite; a program needn't handle non-finite values.
Results may differ from a plain program's by a relative error of at most 0.014.
Values may be sent and summed in bfloat16 or wider, within the bound.
No kernel may reach another device: no remote copies, remote signals or barrier semaphores. Data moves between devices by JAX's collectives and lax.ppermute only.
A program may use at most 192 MiB of HBM per device.

v0:
```python
import functools
import math

import jax
import jax.numpy as jnp
from jax import lax
from jax.experimental import pallas as pl
from jax.experimental.pallas import tpu as pltpu
from jax.sharding import PartitionSpec as P

HEAD = 64
ROW_LEN = 2048
DOCS = 8
F32 = jnp.float32
BF16 = jnp.bfloat16
NN = ((1,), (0,))
NT = ((1,), (1,))
TN = ((0,), (0,))
STATE = 80
COST = 0.2 * 1.15e9
VMEM = pl.BlockSpec(memory_space=pltpu.VMEM)
SMEM = pl.BlockSpec(memory_space=pltpu.SMEM)
ANY = pl.BlockSpec(memory_space=pl.ANY)


def dot(left, right, dims=NN):
    return lax.dot_general(left, right, (dims, ((), ())), preferred_element_type=F32)


def call(body, outs, specs, scratch=(), limit=6, after=(), cost=0):
    n = len(specs)

    def waiting_body(*refs):
        body(*refs[:n], *refs[n + len(after):])

    return lambda *operands: pl.pallas_call(
        waiting_body,
        out_shape=outs,
        in_specs=list(specs) + [ANY] * len(after),
        out_specs=jax.tree.map(lambda _: VMEM, outs),
        scratch_shapes=scratch,
        cost_estimate=pl.CostEstimate(flops=1 + int(cost * COST), bytes_accessed=1, transcendentals=0),
        compiler_params=pltpu.CompilerParams(vmem_limit_bytes=limit << 20),
    )(*operands, *after)


def shaped(shape, dtype):
    return jax.ShapeDtypeStruct(shape, dtype)


class Places:
    def __init__(self, dp, tensor):
        self.dp, self.tensor = dp, tensor
        self.row = lax.axis_index("dp")
        self.z = lax.axis_index("tensor")
        self.piece = self.row & 7

    def swap(self, value, mask):
        return lax.ppermute(value, "dp", [(d, d ^ mask) for d in range(self.dp)])

    def turn(self, value, step):
        size = self.tensor
        return lax.ppermute(value, "tensor", [(k, (k + step) % size) for k in range(size)])

    def onward(self, value, step):
        size = self.tensor
        pairs = [(k, k + step) for k in range(size) if 0 <= k + step < size]
        return lax.ppermute(value, "tensor", pairs)


CORE, X, Y = 1, 2, 4
BUFFERS = ((0, (0, 2)), (0, (4, 6)), (0, (1, 3)), (0, (5, 7)), (2, (0, 4)), (2, (2, 6)), (2, (1, 5)), (2, (3, 7)))


def stacked(*groups, after=()):
    sizes = [len(group) for group in groups]

    def body(*refs):
        sources, targets = list(refs[:sum(sizes)]), refs[sum(sizes):]
        for size, target in zip(sizes, targets, strict=True):
            for k in range(size):
                target[k] = sources.pop(0)[...]

    outs = tuple(shaped((len(group),) + group[0].shape, group[0].dtype) for group in groups)
    flat = [value for group in groups for value in group]
    return call(body, outs, [VMEM] * len(flat), after=after)(*flat)


def mix_pieces_kernel(first, second, third, fourth, a, b, bias_qkv, bias_in):
    rows, wide = a.shape[1], bias_qkv.shape[2]
    for j, part in enumerate((first, second, third, fourth)):
        (a, b)[j // 2][j % 2] = part[0:rows]
        extra = part[rows:].astype(F32)
        bias_qkv[j] = extra[0:1, :wide]
        bias_in[j] = extra[1:2]


def swap_halves(places, a, b):
    return places.swap(a, X), places.swap(b, Y)


def gather_rest(places, a, b, a2, b2):
    near, far = stacked((a, b)), stacked((a2, b2))
    return a, a2, b, b2, places.swap(near[0], CORE), places.swap(far[0], CORE)


def start_placing(piece, buffers, targets, sems):
    copies = []
    a, a2, b, b2, near, far = buffers
    buffers = (a, a2, near.at[0], far.at[0], b, b2, near.at[1], far.at[1])
    for buffer, (shard, pieces) in zip(buffers, BUFFERS, strict=True):
        for k, other in enumerate(pieces):
            for at, target, first_row, rows in targets:
                spot = pl.multiple_of(first_row + (piece ^ other) * rows, 8)
                copies.append(pltpu.make_async_copy(
                    buffer.at[k, :, at:at + rows, :],
                    target.at[shard:shard + 2, pl.ds(spot, rows), :],
                    sems.at[len(copies)],
                ))
    for copy in copies:
        copy.start()
    half = len(copies) // 2
    return copies[:half], copies[half:]


def wait_all(copies):
    for copy in copies:
        copy.wait()


def doubled(part):
    return jnp.concatenate([part, part], axis=1)


def with_one(value):
    lanes = lax.broadcasted_iota(jnp.int32, (value.shape[0], 2 * HEAD), 1)
    return jnp.where(lanes < HEAD, doubled(value.astype(F32)), (lanes == HEAD).astype(F32)).astype(BF16)


def head_parts(mixed_ref, shard, head):
    at = head * 3 * HEAD
    return tuple(mixed_ref[shard, :, at + t * HEAD:at + (t + 1) * HEAD] for t in range(3))


def causal_blocks(count):
    half = count // 2
    return ((0, half, 0, half), (half, count, 0, count))


def mix_kernel(info, tokens, bias, key_table, *refs):
    buffers, (mixed_out, state_out, weight), sems = refs[:6], refs[6:9], refs[9]
    wide = mixed_out.shape[2]
    tall = weight.shape[1] - wide
    halves = start_placing(
        info[0], buffers, ((0, weight, 0, wide // 8), (wide // 8, weight, wide, tall // 8)), sems)

    def shard_step(j, carry):
        mixed = dot(tokens[...], weight[j, 0:wide], NT) + bias[j]
        lanes = lax.broadcasted_iota(jnp.int32, mixed.shape, 1)
        mixed_out[j] = jnp.where(lanes % 192 >= 128, mixed, jnp.maximum(mixed, 0.0)).astype(BF16)
        for h in range(3):
            _, key, value = head_parts(mixed_out, j, h)
            feats = (doubled(key).astype(F32) * key_table[...]).astype(BF16)
            state_out[j, h] = dot(with_one(value), feats, TN)[:STATE].astype(BF16)
        return carry

    for k, half in enumerate(halves):
        wait_all(half)
        lax.fori_loop(2 * k, 2 * k + 2, shard_step, 0)


def local_kernel(mixed, mask, sums_out):
    def shard_step(j, carry):
        for h in range(3):
            query, key, value = head_parts(mixed, j, h)
            value = with_one(value)
            for r0, r1, c0, c1 in causal_blocks(mask.shape[0]):
                scores = (dot(query[r0:r1], key[c0:c1], NT) * mask[r0:r1, c0:c1]).astype(BF16)
                sums_out[j, h, r0:r1] = dot(scores, value[c0:c1])
        return carry

    lax.fori_loop(0, mixed.shape[0], shard_step, 0)


def norm_parts(rows_in):
    centred = rows_in - jnp.mean(rows_in, axis=-1, keepdims=True)
    spread = jnp.mean(centred * centred, axis=-1, keepdims=True)
    scale = lax.rsqrt(spread + 1e-05)
    return centred * scale, scale


def norm_back(grad, normed, scale, gain):
    e = grad * gain
    d_rows = scale * (
        e
        - jnp.mean(e, axis=-1, keepdims=True)
        - normed * jnp.mean(e * normed, axis=-1, keepdims=True)
    )
    return d_rows, jnp.sum(grad * normed, axis=0, keepdims=True), jnp.sum(grad, axis=0, keepdims=True)


def join_kernel(info, sums, arrived1, arrived2, arrived3, mixed, query_table, tokens, weight, b_out, gain, shift,
                attended, carried, dens, first, normed_out, scale_out):
    shards = mixed.shape[0]
    for j in range(shards):
        total = None
        for step, arrived in enumerate((arrived1, arrived2, arrived3), 1):
            linked = info[step].astype(F32) * arrived[(j - step) % shards].astype(F32)
            total = linked if total is None else total + linked
        carried[j] = total.astype(BF16)

    def shard_step(j, branch):
        lanes = lax.broadcasted_iota(jnp.int32, (tokens.shape[0], 128), 1)
        kept = jnp.zeros((tokens.shape[0], 128), F32)
        for h in range(3):
            query = head_parts(mixed, j, h)[0]
            feats = (doubled(query).astype(F32) * query_table[...]).astype(BF16)
            total = sums[j, h][:, :STATE] + dot(feats, carried[j, h], NT)
            den = total[:, HEAD:HEAD + 1]
            inverse = 1.0 / jnp.maximum(den, 1.0)
            attended[j, :, h * HEAD:(h + 1) * HEAD] = (total[:, :HEAD] * inverse).astype(BF16)
            kept = jnp.where(lanes == h, inverse, kept)
            kept = jnp.where(lanes == 8 + h, jnp.where(den > 1.0, inverse, 0.0), kept)
        dens[j] = kept
        return branch + dot(attended[j], weight[j, weight.shape[1] - 192:])

    branch = lax.fori_loop(0, shards, shard_step, jnp.zeros(tokens.shape, F32))
    normed, scale = norm_parts(tokens[...].astype(F32) + branch + b_out[...])
    normed_out[...] = normed
    scale_out[...] = jnp.broadcast_to(scale, scale_out.shape)
    first[...] = (normed * gain[...] + shift[...]).astype(BF16)


def gelu_parts(v):
    k = math.sqrt(2 / math.pi)
    square = v * v
    t = jnp.tanh(v * (k + k * 0.044715 * square))
    half = 0.5 * v
    bent = half * t
    slope = (0.5 + 0.5 * t) + (half - bent * t) * (k + 3 * k * 0.044715 * square)
    return half + bent, slope


def rows_ordered(turned, piece, order):
    rows = turned.shape[0] // 8
    return jnp.concatenate(
        [turned[pl.ds(pl.multiple_of((piece ^ other) * rows, rows), rows), :] for other in order], axis=0)


ROUTES = ((0, 4, 2, 6), (0, 2, 4, 6))


def order_rows(ordered, turned, piece):
    for route, order in enumerate(ROUTES):
        for sends in range(2):
            ordered[2 * route + sends] = rows_ordered(turned, piece, tuple(other + sends for other in order))


def columns(j, width):
    return pl.ds(pl.multiple_of(j * width, 128), width)


def feed_kernel(info, first, bias, b_two, gain, shift, cotangent, *refs):
    buffers = refs[:6]
    slope, block_out, d_second_out, d_r2_out, vectors, *grads = refs[6:13]
    w_in, w_two, active, turned, ordered, total, sems = refs[13:]
    shards, width = w_in.shape[0], w_in.shape[2]
    rows = width // 8
    halves = start_placing(info[0], buffers, ((0, w_in, 0, rows), (rows, w_two, 0, rows)), sems)
    total[...] = jnp.broadcast_to(b_two[...], total.shape)

    def forward_step(j, carry):
        half = first.shape[0] // 2
        spans = slice(0, half), slice(half, 2 * half)
        hidden = [dot(first[span], w_in[j]) + bias[j] for span in spans]
        for span, part in zip(spans, hidden, strict=True):
            act, bend = gelu_parts(part)
            act = act.astype(BF16)
            active[j, span] = act
            slope[j, span] = bend.astype(BF16)
            total[span] += dot(act, w_two[j])
        return carry

    for k, half in enumerate(halves):
        wait_all(half)
        lax.fori_loop(2 * k, 2 * k + 2, forward_step, 0)
    normed, scale = norm_parts(first[...].astype(F32) + total[...])
    block_out[...] = (normed * gain[...] + shift[...]).astype(BF16)
    d_r2, d_gain, d_shift = norm_back(cotangent[...].astype(F32), normed, scale, gain[...])
    d_r2_out[...] = d_r2
    d_second = d_r2.astype(BF16)
    d_second_out[...] = d_second
    turned[...] = d_second.T
    vectors[0:1] = d_gain
    vectors[1:2] = d_shift
    vectors[2:3] = jnp.sum(d_second.astype(F32), axis=0, keepdims=True)
    vectors[3:] = jnp.zeros((5, vectors.shape[1]), F32)
    order_rows(ordered, turned, info[0])

    def grad_step(j, carry):
        for sends in range(2):
            grads[sends][:, columns(j, width)] = dot(ordered[2 * (j // 2) + sends], active[j]).astype(BF16)
        return carry

    lax.fori_loop(0, shards, grad_step, 0)


def feed_back_kernel(info, first, d_second, slope, *refs):
    buffers = refs[:6]
    d_hidden, d_bias, *grads = refs[6:10]
    w_two, turned, ordered, sems = refs[10:]
    shards, width = w_two.shape[0], w_two.shape[2]
    rows = width // 8
    halves = start_placing(info[0], buffers, ((rows, w_two, 0, rows),), sems)
    turned[...] = first[...].T
    order_rows(ordered, turned, info[0])

    def step(j, carry):
        d_active = dot(d_second[...], w_two[j], NT)
        d_h = (d_active * slope[j].astype(F32)).astype(BF16)
        d_hidden[j] = d_h
        d_bias[j] = jnp.broadcast_to(jnp.sum(d_h.astype(F32), axis=0, keepdims=True), d_bias.shape[1:])
        for sends in range(2):
            grads[sends][:, columns(j, width)] = dot(ordered[2 * (j // 2) + sends], d_hidden[j]).astype(BF16)
        return carry

    for k, half in enumerate(halves):
        wait_all(half)
        lax.fori_loop(2 * k, 2 * k + 2, step, 0)


def first_back_kernel(info, d_hidden, d_r2, normed, scale, gain, *refs):
    buffers = refs[:6]
    d_r1_out, d_branch_out, vectors = refs[6:9]
    w_in, total, sems = refs[9:]
    rows = w_in.shape[1] // 8
    halves = start_placing(info[0], buffers, ((0, w_in, 0, rows),), sems)
    total[...] = d_r2[...]

    def first_step(j, carry):
        total[...] += dot(d_hidden[j], w_in[j], NT)
        return carry

    for k, half in enumerate(halves):
        wait_all(half)
        lax.fori_loop(2 * k, 2 * k + 2, first_step, 0)
    d_r1, d_gain, d_shift = norm_back(total[...], normed[...], scale[:, 0:1], gain[...])
    d_r1_out[...] = d_r1
    d_branch = d_r1.astype(BF16)
    d_branch_out[...] = d_branch
    vectors[0:1] = d_gain
    vectors[1:2] = d_shift
    vectors[2:3] = jnp.sum(d_branch.astype(F32), axis=0, keepdims=True)
    vectors[3:] = jnp.zeros((5, vectors.shape[1]), F32)


def heads_back_kernel(d_branch, weight, attended, dens, mixed, query_table, d_sums, d_carried):
    def shard_step(j, carry):
        g_all = dot(d_branch[...], weight[j, weight.shape[1] - 192:], NT)
        lanes = lax.broadcasted_iota(jnp.int32, (d_branch.shape[0], 128), 1)
        for h in range(3):
            g = g_all[:, h * HEAD:(h + 1) * HEAD]
            o = attended[j, :, h * HEAD:(h + 1) * HEAD].astype(F32)
            inverse, inverse_if = dens[j, :, h:h + 1], dens[j, :, 8 + h:9 + h]
            d_den = -jnp.sum(g * o, axis=-1, keepdims=True) * inverse_if
            d_num = doubled(g * inverse)
            both = jnp.where(lanes < HEAD, d_num, jnp.where(lanes == HEAD, d_den, 0.0)).astype(BF16)
            d_sums[j, h] = both
            query = head_parts(mixed, j, h)[0]
            feats = (doubled(query).astype(F32) * query_table[...]).astype(BF16)
            d_carried[j, h] = dot(both, feats, TN)[:STATE].astype(BF16)
        return carry

    lax.fori_loop(0, mixed.shape[0], shard_step, 0)


def local_back_kernel(mixed, d_sums, mask, mask_t, d_mixed):
    def shard_step(j, carry):
        for h in range(3):
            query, key, value = head_parts(mixed, j, h)
            value = with_one(value)
            grad = d_sums[j, h]
            at = h * 3 * HEAD
            for r0, r1, c0, c1 in causal_blocks(mask.shape[0]):
                d_scores = (dot(grad[r0:r1], value[c0:c1], NT) * mask[r0:r1, c0:c1]).astype(BF16)
                d_mixed[j, r0:r1, at:at + HEAD] = dot(d_scores, key[c0:c1])
            half = mask.shape[0] // 2
            for c0, c1, r0 in ((0, half, 0), (half, 2 * half, half)):
                turned = mask_t[c0:c1, r0:]
                d_scores = (dot(value[c0:c1], grad[r0:], NT) * turned).astype(BF16)
                d_mixed[j, c0:c1, at + HEAD:at + 2 * HEAD] = dot(d_scores, query[r0:])
                scores = (dot(key[c0:c1], query[r0:], NT) * turned).astype(BF16)
                d_mixed[j, c0:c1, at + 2 * HEAD:at + 3 * HEAD] = dot(scores, grad[r0:])[:, :HEAD]
        return carry

    lax.fori_loop(0, mixed.shape[0], shard_step, 0)


def mix_back_kernel(base, info, mixed, local, d_sums, carried, arrived1, arrived2, arrived3, query_table, key_table,
                    tokens, attended, d_branch, *refs):
    last = base > 0
    sources, refs = (refs[:4], refs[4:]) if last else ((), refs)
    d_mixed, d_bias, *grads = refs[:4]
    turned, turned_branch, state, held, middles = refs[-5:]
    shards, wide = mixed.shape[0], mixed.shape[2]
    width = d_mixed.shape[2]
    turned[...] = tokens[...].T
    turned_branch[...] = d_branch[...].T
    for k in range(2):
        total = None
        for step, arrived in enumerate((arrived1, arrived2, arrived3), 1):
            linked = info[3 + step].astype(F32) * arrived[(base + k + step) % shards].astype(F32)
            total = linked if total is None else total + linked
        state[k] = total.astype(BF16)

    def folded(both):
        return both[:, :HEAD] + both[:, HEAD:]

    def shard_step(k, carry):
        j = base + k
        parts = []
        for h in range(3):
            query, key, value = head_parts(mixed, j, h)
            at = h * 3 * HEAD
            spans = [slice(at + t * HEAD, at + (t + 1) * HEAD) for t in range(3)]
            d_query = folded(dot(d_sums[j, h][:, :STATE], carried[j, h]) * query_table[...])
            d_query = jnp.where(query.astype(F32) > 0, local[j, :, spans[0]] + d_query, 0.0)
            d_key = folded(dot(with_one(value)[:, :STATE], state[k, h]) * key_table[...])
            d_key = jnp.where(key.astype(F32) > 0, local[j, :, spans[1]] + d_key, 0.0)
            feats = (doubled(key).astype(F32) * key_table[...]).astype(BF16)
            d_value = local[j, :, spans[2]] + dot(feats, state[k, h], NT)[:, :HEAD]
            parts += [d_query, d_key, d_value]
        whole = jnp.concatenate(parts + [attended[j].astype(F32)], axis=1).astype(BF16)
        d_mixed[k] = whole
        middles[k] = jnp.concatenate([parts[-1], attended[j][:, :HEAD].astype(F32)], axis=1)
        d_bias[k] = jnp.broadcast_to(jnp.sum(d_mixed[k].astype(F32), axis=0, keepdims=True), d_bias.shape[1:])
        return carry

    lax.fori_loop(0, 2, shard_step, 0)
    rows = grads[0].shape[0]
    low = wide // 128 * 128
    for k in range(2):
        lanes = lax.broadcasted_iota(jnp.int32, (d_mixed.shape[1], 128), 1)
        middle = middles[k]
        left_side = jnp.where(lanes < HEAD, middle, 0.0).astype(BF16)
        right_side = jnp.where(lanes < HEAD, 0.0, middle).astype(BF16)
        left_side = jnp.concatenate([d_mixed[k][:, :low], left_side], axis=1)
        right_side = jnp.concatenate([right_side, d_mixed[k][:, low + 128:]], axis=1)
        for sends in (1, 0):
            out, at = grads[sends], k * width
            order = tuple(other + sends for other in ROUTES[k])
            left = dot(rows_ordered(turned, info[0], order), left_side)
            right = dot(rows_ordered(turned_branch, info[0], order), right_side)
            out[0:rows, at:at + low] = left[:, :low].astype(BF16)
            out[0:rows, at + low:at + low + 128] = (left[:, low:] + right[:, :128]).astype(BF16)
            out[0:rows, at + low + 128:at + width] = right[:, 128:].astype(BF16)
    if last:
        one, two, bias_in, bias_first = sources
        vectors = refs[4]
        held[0:3] = one[0:3]
        held[3:6] = two[0:3]
        for j in range(shards):
            held[6 + 2 * j:7 + 2 * j] = bias_first[j, 0:1] if j < 2 else d_bias[j - 2, 0:1]
            held[7 + 2 * j:8 + 2 * j] = bias_in[j, 0:1]
        held[14:16] = jnp.zeros((2, width), F32)
        low_rows = held[...].astype(BF16)
        vectors[...] = low_rows
        grads[1][rows:, 0:width] = low_rows[0:8]
        grads[1][rows:, width:] = low_rows[8:16]


def tokens_back_kernel(d_mixed_a, d_mixed_b, weight, d_r1, d_tokens):
    wide = weight.shape[1] - 192
    total = d_r1[...]
    for j in range(weight.shape[0]):
        d_mixed = (d_mixed_a, d_mixed_b)[j // 2]
        total = total + dot(d_mixed[j % 2][:, :wide], weight[j, 0:wide])
    d_tokens[...] = total.astype(BF16)


def later(values, others):
    return lax.optimization_barrier((values, others))[0]


def halves_like(rows, width, extra=0):
    keep, send = shaped((rows, width), F32), shaped((rows, width), BF16)
    return keep, send, keep, shaped((rows + extra, width), BF16)


def first_halves_kernel(keep, got, *outs):
    half, width = outs[0].shape
    for k in range(2):
        cols = slice(k * width, (k + 1) * width)
        outs[2 * k][...] = keep[0:half, cols].astype(F32) + got[0:half, cols].astype(F32)
        send = keep[half:2 * half, cols].astype(F32) + got[half:2 * half, cols].astype(F32)
        outs[2 * k + 1][0:half] = send.astype(BF16)


def first_pairs_kernel(keep_a, got_a, keep_b, got_b, mine, *outs):
    half, width = outs[0].shape[0] // 2, outs[0].shape[1]
    for k in range(2):
        cols = slice(k * width, (k + 1) * width)
        for t, (keep, got) in enumerate(((keep_a, got_a), (keep_b, got_b))):
            spots = slice(t * half, (t + 1) * half)
            outs[2 * k][spots] = keep[0:half, cols].astype(F32) + got[0:half, cols].astype(F32)
            send = keep[half:2 * half, cols].astype(F32) + got[half:2 * half, cols].astype(F32)
            outs[2 * k + 1][spots] = send.astype(BF16)
        rows = mine[8 * k:8 * k + 8].astype(F32) + got_b[2 * half:, cols].astype(F32)
        outs[4][8 * k:8 * k + 8] = rows.astype(BF16)
        outs[3][2 * half + 8 * k:2 * half + 8 * k + 8] = rows.astype(BF16)


def next_halves_kernel(keep0, keep1, got0, got1, *outs):
    half = outs[0].shape[0]
    for k, (keep, got) in enumerate(((keep0, got0), (keep1, got1))):
        outs[2 * k][...] = keep[0:half] + got[0:half].astype(F32)
        outs[2 * k + 1][...] = (keep[half:] + got[half:].astype(F32)).astype(BF16)


def ends_kernel(keep0, keep1, got0, got1, end0, end1):
    end0[...] = (keep0[...] + got0[...].astype(F32)).astype(BF16)
    end1[...] = (keep1[...] + got1[...].astype(F32)).astype(BF16)


def feed_last_kernel(keep0, keep1, got0, got1, two0, two1, *outs):
    rows, width = outs[0].shape[0] // 2, outs[0].shape[1]
    for j, out in enumerate(outs):
        keep, got, two = (keep0, got0, two0) if j < 2 else (keep1, got1, two1)
        cols = slice(j % 2 * width, (j % 2 + 1) * width)
        out[0:rows] = (keep[:, cols] + got[:, cols].astype(F32)).astype(BF16)
        out[rows:] = two[:, cols]


def mix_next_kernel(keep0, keep1, got0, got1, mine, *outs):
    half = outs[0].shape[0] // 2
    for k, (keep, got) in enumerate(((keep0, got0), (keep1, got1))):
        for t in range(2):
            at = 2 * t * half
            spots = slice(t * half, (t + 1) * half)
            outs[2 * k][spots] = keep[at:at + half] + got[at:at + half].astype(F32)
            send = keep[at + half:at + 2 * half] + got[at + half:at + 2 * half].astype(F32)
            outs[2 * k + 1][spots] = send.astype(BF16)
    rows = (mine[...].astype(F32) + got1[4 * half:].astype(F32)).astype(BF16)
    outs[4][...] = rows
    outs[3][2 * half:] = rows


def mix_last_kernel(keep0, keep1, got0, got1, mine, *outs):
    half = keep0.shape[0] // 2
    rows = (mine[...].astype(F32) + got1[2 * half:].astype(F32)).astype(BF16)
    for j, out in enumerate(outs):
        keep, got = (keep0, got0) if j % 2 == 0 else (keep1, got1)
        spots = slice(j // 2 * half, (j // 2 + 1) * half)
        out[0:half] = (keep[spots] + got[spots].astype(F32)).astype(BF16)
        out[half:half + 6] = rows[0:6]
        out[half + 6:half + 8] = rows[6 + 2 * j:8 + 2 * j]


def swap_all(places, values, masks):
    return [places.swap(value, mask) for value, mask in zip(values, masks, strict=True)]


def turn_back(places, parts):
    return [parts[0]] + [places.turn(parts[s], -s) for s in range(1, places.tensor)]


def pair_sum(mine, other):
    return (mine.astype(F32) + other.astype(F32)).astype(BF16)


def over_groups(places, total):
    mask = 8
    while mask < places.dp:
        total = total + places.swap(total, mask)
        mask *= 2
    return total


def added(places, values, rows, after=()):
    kind = BF16 if places.dp == 8 else F32

    def body(*refs):
        total = refs[0][0:rows].astype(F32)
        for other in refs[1:-1]:
            total = total + other[0:rows].astype(F32)
        refs[-1][...] = total.astype(kind)

    total = call(body, shaped((rows, values[0].shape[1]), kind), [VMEM] * len(values), after=after)(*values)
    return over_groups(places, total).astype(BF16)


def spread_chips(places, own):
    return [own, places.swap(own, X), places.swap(own, Y), places.swap(own, X + Y)]


def spread_cores(places, four):
    return list(four) + [places.swap(stacked(four)[0], CORE)]


def place_rows(piece, pieces, targets):
    for k in range(8):
        source = pieces[k // 2] if k % 2 == 0 else pieces[4].at[k // 2]
        for t, target in enumerate(targets):
            rows = target.shape[0] // 8
            spot = pl.multiple_of((piece ^ k) * rows, rows)
            target[pl.ds(spot, rows), :] = source[t * rows:(t + 1) * rows].astype(F32)


def finish_feed_kernel(info, own, x, y, xy, core, d_in, d_two, held):
    place_rows(info[0], (own, x, y, xy, core), (d_in, held))
    d_two[...] = held[...].T


def finish_mix_kernel(info, own, x, y, xy, core, d_qkv, d_out, held):
    place_rows(info[0], (own, x, y, xy, core), (held,))
    turned = held[...].T
    d_qkv[...] = turned[0:d_qkv.shape[0]]
    d_out[...] = turned[d_qkv.shape[0]:]


def doc_tables(starts_row, base, count):
    spots = base + jnp.arange(count, dtype=jnp.int32)
    started = (spots[:, None] >= starts_row[None, :]).astype(jnp.int32)
    doc_ids = jnp.sum(started, axis=1) - 1
    onehot = (doc_ids[:, None] == jnp.arange(DOCS, dtype=jnp.int32)[None, :]).astype(jnp.int32)
    finish = jnp.concatenate([starts_row[1:], jnp.full((1,), ROW_LEN, jnp.int32)])
    own_start = jnp.sum(onehot * starts_row[None, :], axis=1)
    own_len = jnp.sum(onehot * (finish - starts_row)[None, :], axis=1)
    angles = 0.5 * math.pi * (spots - own_start).astype(F32) / own_len.astype(F32)
    return angles, doc_ids


def doc_at(starts_row, spot):
    return jnp.sum((spot >= starts_row).astype(jnp.int32)) - 1


def on_device(dp, tensor, tokens, starts, w_qkv, b_qkv, w_out, b_out, gain_one, shift_one, w_in, b_in,
              w_two, b_two, gain_two, shift_two, cotangent):
    places = Places(dp, tensor)
    count, width = tokens.shape
    piece = places.piece
    line = lambda a: a.astype(F32).reshape(1, -1)
    sems = lambda n: pltpu.SemaphoreType.DMA((n,))

    def own_rows(weight):
        rows = weight.shape[0] // 8
        return lax.dynamic_slice_in_dim(weight, piece * rows, rows, 0)

    rows = width // 8
    wide = w_qkv.shape[1]
    bias_rows = jnp.pad(b_qkv.reshape(1, wide), ((0, 7), (0, width - wide))) + jnp.pad(b_in.reshape(1, width), ((1, 6), (0, 0)))
    mix_piece = jnp.concatenate([own_rows(w_qkv.T), own_rows(w_out), bias_rows])
    feed_piece = jnp.concatenate([own_rows(w_in), own_rows(w_two)])
    mix_parts = [mix_piece] + [places.turn(mix_piece, s) for s in range(1, tensor)]
    feed_parts = [feed_piece] + [places.turn(feed_piece, s) for s in range(1, tensor - 1)]
    feed_parts.append(places.turn(later(feed_piece, mix_parts), tensor - 1))
    pair = shaped((2, rows, width), BF16)
    mix_a, mix_b, bias_qkv, bias_in = call(
        mix_pieces_kernel, (pair, pair, shaped((tensor, 1, wide), F32), shaped((tensor, 1, width), F32)), [VMEM] * 4,
    )(*mix_parts)
    near_x, near_y = swap_halves(places, mix_a, mix_b)
    mix_ax, mix_by = stacked((mix_a, near_x), (mix_b, near_y))
    mix_buffers = gather_rest(places, mix_ax, mix_by, places.swap(mix_ax, Y), places.swap(mix_by, X))
    feed_a, feed_b = stacked(feed_parts[:2], feed_parts[2:], after=(mix_ax, mix_by))
    near_x, near_y = swap_halves(places, feed_a, feed_b)

    row = starts[0]
    base = places.z * count
    angles, docs = doc_tables(row, base, count)
    first_doc, last_doc = doc_at(row, base), doc_at(row, base + count - 1)
    links = [doc_at(row, base - (s - 1) * count - 1) == first_doc for s in range(1, tensor)]
    links += [doc_at(row, base + s * count) == last_doc for s in range(1, tensor)]
    info = jnp.stack([piece] + [link.astype(jnp.int32) for link in links] + [piece])
    spot = jnp.arange(count)
    cosine, sines = jnp.cos(angles), jnp.sin(angles)
    turn = cosine[:, None] * cosine[None, :] + sines[:, None] * sines[None, :]
    same = docs[:, None] == docs[None, :]
    mask = jnp.where(same & (spot[:, None] >= spot[None, :]), turn, 0.0)
    mask_t = jnp.where(same & (spot[:, None] <= spot[None, :]), turn, 0.0)
    lanes = jnp.arange(2 * HEAD)[None, :]
    table = jnp.where(lanes < HEAD, cosine[:, None], sines[:, None])
    query_table = jnp.where((docs == first_doc)[:, None], table, 0.0)
    key_table = jnp.where((docs == last_doc)[:, None], table, 0.0)

    states = shaped((tensor, 3, STATE, 2 * HEAD), BF16)
    mixed, state, mix_weight = call(
        mix_kernel,
        (shaped((tensor, count, wide), BF16), states, shaped((tensor, width, width), BF16)),
        [SMEM, VMEM, VMEM, VMEM] + [ANY] * 6, [sems(32)], after=(mask, mask_t), limit=9, cost=8,
    )(info, tokens, bias_qkv, key_table, *mix_buffers)
    per_head = shaped((tensor, 3, count, 2 * HEAD), F32)
    arrived = [places.onward(state, s) for s in range(1, tensor)]
    per_head = shaped((tensor, 3, count, 2 * HEAD), F32)
    feed_ax, feed_by = stacked((feed_a, near_x), (feed_b, near_y), after=(state,))
    near_sums = call(local_kernel, per_head, [VMEM, VMEM], after=(feed_ax, feed_by), limit=6, cost=7)(mixed, mask)
    feed_far = places.swap(feed_ax, Y), places.swap(feed_by, X)
    attended, carried, dens, first, normed, scale = call(
        join_kernel,
        (shaped((tensor, count, 192), BF16), states, shaped((tensor, count, 128), F32), shaped((count, width), BF16),
         shaped((count, width), F32), shaped((count, 128), F32)),
        [SMEM] + [VMEM] * 11, limit=18, cost=100,
    )(info, near_sums, *arrived, mixed, query_table, tokens, mix_weight, line(b_out), line(gain_one), line(shift_one))
    feed_buffers = gather_rest(places, *later((feed_ax, feed_by, *feed_far), first))
    hidden_like = shaped((tensor, count, width), BF16)
    vectors = shaped((8, width), F32)
    grad_like = shaped((4 * rows, tensor * width), BF16)
    square = pltpu.VMEM((tensor, width, width), BF16)
    turned = pltpu.VMEM((width, count), BF16)
    ordered = pltpu.VMEM((4, 4 * rows, count), BF16)
    total_scratch = pltpu.VMEM((count, width), F32)
    slope, block_out, d_second, d_r2, vectors_two, two_keep, two_send = call(
        feed_kernel,
        (hidden_like, shaped((count, width), BF16), shaped((count, width), BF16),
         shaped((count, width), F32), vectors, grad_like, grad_like),
        [SMEM] + [VMEM] * 6 + [ANY] * 6, [square, square, pltpu.VMEM(hidden_like.shape, BF16), turned, ordered, total_scratch, sems(32)], limit=33, cost=19,
    )(info, first, bias_in, line(b_two), line(gain_two), line(shift_two), cotangent, *feed_buffers)

    got = places.swap(two_send, CORE)
    d_hidden, d_bias_in, in_keep, in_send = call(
        feed_back_kernel, (hidden_like, shaped((tensor, 8, width), F32), grad_like, grad_like),
        [SMEM] + [VMEM] * 3 + [ANY] * 6, [square, turned, ordered, sems(16)], limit=19, cost=14,
    )(info, first, d_second, slope, *feed_buffers)
    wide_halves = halves_like(2 * rows, 2 * width)
    keep0, send0, keep1, send1 = call(first_halves_kernel, wide_halves, [VMEM] * 2, after=(in_send,))(two_keep, got)
    got_two, got_in = swap_all(places, (send0, send1), (X, Y)), places.swap(in_send, CORE)
    d_r1, d_branch, vectors_one = call(
        first_back_kernel,
        (shaped((count, width), F32), shaped((count, width), BF16), vectors),
        [SMEM] + [VMEM] * 5 + [ANY] * 6, [square, total_scratch, sems(16)], after=(send0, send1), limit=17, cost=11,
    )(info, d_hidden, d_r2, normed, scale, line(gain_one), *feed_buffers)
    keep0, send0, keep1, send1 = call(
        next_halves_kernel, halves_like(rows, 2 * width), [VMEM] * 4, after=(d_branch,))(keep0, keep1, *got_two)
    got_two = swap_all(places, (send0, send1), (Y, X))
    in0, in_send0, in1, in_send1 = call(
        first_halves_kernel, wide_halves, [VMEM] * 2, after=(send0, send1))(in_keep, got_in)
    got_in = swap_all(places, (in_send0, in_send1), (X, Y))
    d_sums, d_carried = call(
        heads_back_kernel, (shaped((tensor, 3, count, 2 * HEAD), BF16), states), [VMEM] * 6,
        after=(in_send0, in_send1), limit=10, cost=11,
    )(d_branch, mix_weight, attended, dens, mixed, query_table)
    arrived_back = [places.onward(d_carried, -s) for s in range(1, tensor)]
    end = shaped((rows, 2 * width), BF16)
    two_ends = call(ends_kernel, (end, end), [VMEM] * 4, after=(d_carried,))(keep0, keep1, *got_two)
    in0, in_send0, in1, in_send1 = call(
        next_halves_kernel, halves_like(rows, 2 * width), [VMEM] * 4, after=two_ends)(in0, in1, *got_in)
    got_in = swap_all(places, (in_send0, in_send1), (Y, X))
    local = call(
        local_back_kernel, shaped((tensor, count, wide), F32), [VMEM] * 4, after=(in_send0, in_send1), limit=10, cost=15,
    )(mixed, d_sums, mask, mask_t)
    feed_last = call(
        feed_last_kernel, (shaped((2 * rows, width), BF16),) * tensor, [VMEM] * 6, after=(local, *arrived_back),
    )(in0, in1, *got_in, *two_ends)
    feed_own = turn_back(places, feed_last)
    mix_like = shaped((4 * rows, 2 * width), BF16)
    mix_outs = (shaped((2, count, width), BF16), shaped((2, 8, width), F32), mix_like)
    mix_scratch = [turned, turned, pltpu.VMEM((2, 3, STATE, 2 * HEAD), BF16), pltpu.VMEM((16, width), F32), pltpu.VMEM((2, count, 128), F32)]
    mix_inputs = (info, mixed, local, d_sums, carried, *arrived_back, query_table, key_table, tokens, attended, d_branch)
    d_mixed_a, d_bias_a, keep_a, send_a = call(
        functools.partial(mix_back_kernel, 0), mix_outs + (mix_like,), [SMEM] + [VMEM] * 12, mix_scratch,
        after=feed_last, limit=19, cost=11,
    )(*mix_inputs)
    got_a = places.swap(send_a, CORE)
    d_mixed_b, d_bias_b, keep_b, send_b, vector_rows = call(
        functools.partial(mix_back_kernel, 2),
        mix_outs + (shaped((4 * rows + 8, 2 * width), BF16), shaped((16, width), BF16)), [SMEM] + [VMEM] * 16,
        mix_scratch, limit=19, cost=11,
    )(*mix_inputs, vectors_one, vectors_two, d_bias_in, d_bias_a)
    feed_rows = added(places, feed_own, 2 * rows, after=(d_mixed_b,))
    got_a, got_b = later(got_a, feed_rows), places.swap(later(send_b, feed_rows), CORE)
    row_like = shaped((16, width), BF16)
    keep0, send0, keep1, send1, vector_rows = call(
        first_pairs_kernel, halves_like(4 * rows, width, 16) + (row_like,), [VMEM] * 5,
    )(keep_a, got_a, keep_b, got_b, vector_rows)
    got = swap_all(places, (send0, send1), (X, Y))
    d_tokens = call(
        tokens_back_kernel, shaped((count, width), BF16), [VMEM] * 4, after=(send0, send1), limit=9, cost=6,
    )(d_mixed_a, d_mixed_b, mix_weight, d_r1)
    keep0, send0, keep1, send1, vector_rows = call(
        mix_next_kernel, halves_like(2 * rows, width, 16) + (row_like,), [VMEM] * 5, after=(d_tokens,),
    )(keep0, keep1, *got, vector_rows)
    got = swap_all(places, (send0, send1), (Y, X))
    feed_low = later(feed_rows, (send0, send1))
    feed_x, feed_y = swap_all(places, (feed_low, feed_low), (X, Y))
    mix_last = call(
        mix_last_kernel, (shaped((rows + 8, width), BF16),) * tensor, [VMEM] * 5,
    )(keep0, keep1, *got, vector_rows)
    mix_own = turn_back(places, mix_last)
    feed_x, feed_y = later((feed_x, feed_y), mix_last)
    feed_xy = later(places.swap(feed_x, Y), mix_own[1])
    feed_all = spread_cores(places, [feed_low, feed_x, feed_y, feed_xy])

    held = pltpu.VMEM((width, width), F32)
    d_w_in, d_w_two = call(
        finish_feed_kernel, (shaped((width, width), F32),) * 2, [SMEM] + [VMEM] * 5, [held], limit=10, cost=4,
    )(info, *feed_all)
    mix_own = later(mix_own, d_w_in)
    mix_rows = added(places, mix_own, rows)
    d_w_qkv, d_w_out = call(
        finish_mix_kernel, (shaped((wide, width), F32), shaped((192, width), F32)), [SMEM] + [VMEM] * 5, [held], limit=7, cost=3,
    )(info, *spread_cores(places, spread_chips(places, mix_rows)))

    ends = jnp.stack([part[rows:] for part in mix_own])
    ends = lax.dynamic_slice_in_dim(jnp.concatenate([ends, ends]), tensor - places.z, tensor, 0)
    summed = over_groups(places, jnp.sum(ends.astype(F32), axis=0))
    d_gain_one, d_shift_one, d_b_out, d_gain_two, d_shift_two, d_b_two = (summed[k] for k in range(6))
    d_b_qkv, d_b_in = summed[6, :wide], summed[7]
    return (block_out, d_tokens, d_w_qkv.T, d_b_qkv, d_w_out, d_b_out, d_gain_one, d_shift_one, d_w_in, d_b_in,
            d_w_two, d_b_two, d_gain_two, d_shift_two)


def solution(mesh):
    sizes = dict(mesh.shape)
    rows = P(("dp", "tensor"), None)
    wide, tall, cut, whole = P(None, "tensor"), P("tensor", None), P("tensor"), P()
    in_specs = (rows, P("dp", None), wide, cut, tall, whole, whole, whole, wide, cut, tall, whole, whole, whole, rows)
    out_specs = (rows, rows, wide, cut, tall, whole, whole, whole, wide, cut, tall, whole, whole, whole)
    return jax.shard_map(
        functools.partial(on_device, sizes["dp"], sizes["tensor"]),
        mesh=mesh, in_specs=in_specs, out_specs=out_specs, check_vma=False,
    )
```

profile of v0, /device:TPU:0, one launch (start us, length us, event | category | flops | bytes accessed | tf_op | source)
XLA Modules:
  0.0 311.6 jit_solution(13107799062277173213)
XLA Ops:
  2.9 5.1 %collective-permute-start.2 = (bf16[104,768]{1,0:T(8,128)(2,1)S(1)}, bf16[104,768]{1,0:T(8,128)(2,1)S(1)}, u32[]{:S(2)}, u32[]{:S(2)}) collective-permute-start(bf16[104,768]{1,0:T(8,128)(2,1)S(1)} %pad_maximum_fusion.1.refs_0_), channel_id=1, source_target_pairs={{0,3},{1,0},{2,1},{3,2},{4,7},{5,4},{6,5},{7,6},{8,11},{9,8},{10,9... | collective-permute-start | bytes 479240 | tf_op jit(solution)/shard_map/ppermute | solution.py:63
  9.1 3.5 %collective-permute-done.2.refs_3_ = bf16[104,768]{1,0:T(8,128)(2,1)S(1)} collective-permute-done((bf16[104,768]{1,0:T(8,128)(2,1)S(1)}, bf16[104,768]{1,0:T(8,128)(2,1)S(1)}, u32[]{:S(2)}, u32[]{:S(2)}) %collective-permute-start.2) | collective-permute-done | bytes 159776 | tf_op jit(solution)/shard_map/ppermute | solution.py:63
  12.6 9.0 %collective-permute-done.1.refs_2_ = bf16[104,768]{1,0:T(8,128)(2,1)S(1)} collective-permute-done((bf16[104,768]{1,0:T(8,128)(2,1)S(1)}, bf16[104,768]{1,0:T(8,128)(2,1)S(1)}, u32[]{:S(2)}, u32[]{:S(2)}) %collective-permute-start.1) | collective-permute-done | bytes 159776 | tf_op jit(solution)/shard_map/ppermute | solution.py:63
  22.2 1.5 collective-permute-start.3
  23.7 1.5 collective-permute-start.4
  26.3 2.9 collective-permute-start.10
  30.7 1.2 collective-permute-done.4.refs_3_
  32.0 1.6 collective-permute-start.5
  36.7 8.9 %collective-permute-done.5.refs_0_.refs_5_ = bf16[2,2,96,768]{3,2,1,0:T(8,128)(2,1)S(1)} collective-permute-done((bf16[2,2,96,768]{3,2,1,0:T(8,128)(2,1)S(1)}, bf16[2,2,96,768]{3,2,1,0:T(8,128)(2,1)S(1)}, u32[]{:S(2)}, u32[]{:S(2)}) %collective-permute-start.5) | collective-permute-done | bytes 589856 | tf_op jit(solution)/shard_map/ppermute | solution.py:59
  45.6 1.2 collective-permute-done.6.refs_1_.refs_7_
  46.8 1.2 shard_map.257
  48.9 8.8 %collective-permute-done.11.refs_3_ = bf16[192,768]{1,0:T(8,128)(2,1)S(1)} collective-permute-done((bf16[192,768]{1,0:T(8,128)(2,1)S(1)}, bf16[192,768]{1,0:T(8,128)(2,1)S(1)}, u32[]{:S(2)}, u32[]{:S(2)}) %collective-permute-start.11) | collective-permute-done | bytes 294944 | tf_op jit(solution)/shard_map/ppermute | solution.py:63
  64.8 1.5 copy-done.23
  68.1 8.1 %shard_map.258 = (bf16[4,512,576]{2,1,0:T(8,128)(2,1)S(1)}, bf16[4,3,80,128]{3,2,1,0:T(8,128)(2,1)S(1)}, bf16[4,768,768]{2,1,0:T(8,128)(2,1)S(1)}) custom-call(s32[8]{0:T(128)S(1)} %stack.69.refs_0_, bf16[512,768]{1,0:T(8,128)(2,1)S(1)} %copy-done.14, f32[4,1,576]{2,1,0:T(1,128)S(1)} %copy-done.39, f32[512,128]{1,0:T(8,128)S(1)} %get-tuple-element.232.refs_3_.refs_9_, ...), custom_call_target="tpu_custom_call" | custom-call | flops 1840000000 | bytes 1 | tf_op jit(solution)/shard_map/pallas_call | solution.py:36
  76.3 5.3 %collective-permute-start.16 = (bf16[4,3,80,128]{3,2,1,0:T(8,128)(2,1)S(1)}, bf16[4,3,80,128]{3,2,1,0:T(8,128)(2,1)S(1)}, u32[]{:S(2)}, u32[]{:S(2)}) collective-permute-start(bf16[4,3,80,128]{3,2,1,0:T(8,128)(2,1)S(1)} %get-tuple-element.121.refs_4_), channel_id=1, source_target_pairs={{0,3},{4,7},{8,11},{12,15},{16,19},{20,23},{24,27},{28,31}} | collective-permute-start | bytes 737288 | tf_op jit(solution)/shard_map/ppermute | solution.py:68
  81.6 1.3 collective-permute-start.15
  82.9 2.6 collective-permute-start.14
  85.6 1.8 shard_map.260
  88.0 1.5 collective-permute-start.18
  89.5 5.0 %shard_map.261.refs_1_ = f32[4,3,512,128]{3,2,1,0:T(8,128)S(1)} custom-call(bf16[4,512,576]{2,1,0:T(8,128)(2,1)S(1)} %get-tuple-element.117.refs_0_.refs_5_.refs_4_.refs_1_, f32[512,512]{1,0:T(8,128)S(1)} %get-tuple-element.230.refs_10_.refs_1_.refs_2_, bf16[2,2,192,768]{3,2,1,0:T(8,128)(2,1)S(1)} %get-tuple-element.127.refs_2_.refs_0_.refs_7_.refs_4_.refs_6_, ...), custom_call_target="tpu_custom_call" | custom-call | flops 1610000000 | bytes 1 | tf_op jit(solution)/shard_map/pallas_call | solution.py:36
  94.5 2.2 collective-permute-done.14.refs_2_
  96.7 6.6 %shard_map.262 = (bf16[4,512,192]{2,1,0:T(8,128)(2,1)S(1)}, bf16[4,3,80,128]{3,2,1,0:T(8,128)(2,1)S(1)}, f32[4,512,128]{2,1,0:T(8,128)S(1)}, bf16[512,768]{1,0:T...) custom-call(s32[8]{0:T(128)S(1)} %stack.69.refs_0_, f32[4,3,512,128]{3,2,1,0:T(8,128)S(1)} %shard_map.261.refs_1_, ...), custom_call_target="tpu_custom_call" | custom-call | flops 23000000512 | bytes 1 | tf_op jit(solution)/shard_map/pallas_call | solution.py:36
  103.3 1.2 copy-done.26
  106.2 7.7 %collective-permute-done.17.refs_0_.refs_8_.refs_5_.refs_7_ = bf16[2,2,192,768]{3,2,1,0:T(8,128)(2,1)S(1)} collective-permute-done((bf16[2,2,192,768]{3,2,1,0:T(8,128)(2,1)S(1)}, bf16[2,2,192,768]{3,2,1,0:T(8,128)(2,1)S(1)}, u32[]{:S(2)}, u32[]{:S(2)}) %collective-permute-start.17) | collective-permute-done | bytes 1179680 | tf_op jit(solution)/shard_map/ppermute | solution.py:59
  115.3 3.8 %collective-permute-done.20.refs_12_.refs_9_.refs_11_ = bf16[2,2,2,192,768]{4,3,2,1,0:T(8,128)(2,1)S(1)} collective-permute-done((bf16[2,2,2,192,768]{4,3,2,1,0:T(8,128)(2,1)S(1)}, bf16[2,2,2,192,768]{4,3,2,1,0:T(8,128)(2,1)S(1)}, u32[]{:S(2)}, u32[]{:S(2)}) %collective-permute-start.20) | collective-permute-done | bytes 2359328 | tf_op jit(solution)/shard_map/ppermute | solution.py:59
  119.0 3.4 %collective-permute-done.19.refs_11_.refs_8_.refs_10_ = bf16[2,2,2,192,768]{4,3,2,1,0:T(8,128)(2,1)S(1)} collective-permute-done((bf16[2,2,2,192,768]{4,3,2,1,0:T(8,128)(2,1)S(1)}, bf16[2,2,2,192,768]{4,3,2,1,0:T(8,128)(2,1)S(1)}, u32[]{:S(2)}, u32[]{:S(2)}) %collective-permute-start.19) | collective-permute-done | bytes 2359328 | tf_op jit(solution)/shard_map/ppermute | solution.py:59
  122.4 16.0 %shard_map.265 = (bf16[4,512,768]{2,1,0:T(8,128)(2,1)S(1)}, bf16[512,768]{1,0:T(8,128)(2,1)}, bf16[512,768]{1,0:T(8,128)(2,1)S(1)}, f32[512,768]{1,0:T(8,128)S(1...) custom-call(s32[8]{0:T(128)S(1)} %stack.69.refs_0_, ...), custom_call_target="tpu_custom_call" | custom-call | flops 4369999872 | bytes 1 | tf_op jit(solution)/shard_map/pallas_call | solution.py:36
  140.3 1.3 copy-done.3
  141.6 1.7 copy-done.8
  143.2 8.1 %shard_map.266 = (bf16[4,512,768]{2,1,0:T(8,128)(2,1)S(1)}, f32[4,8,768]{2,1,0:T(8,128)S(1)}, bf16[384,3072]{1,0:T(8,128)(2,1)S(1)}, bf16[384,3072]{1,0:T(8,128)(2,1)S(1)}) custom-call(s32[8]{0:T(128)S(1)} %stack.69.refs_0_, bf16[512,768]{1,0:T(8,128)(2,1)S(1)} %get-tuple-element.125.refs_1_, bf16[512,768]{1,0:T(8,128)(2,1)S(1)} %get-tuple-element.132.refs_2_, ...), custom_call_target="tpu_custom_call" | custom-call | flops 3220000000 | bytes 1 | tf_op jit(solution)/shard_map/pallas_call | solution.py:36
  152.3 1.6 collective-permute-start.23
  153.9 1.5 collective-permute-start.24
  155.4 5.8 %shard_map.268 = (f32[512,768]{1,0:T(8,128)S(1)}, bf16[512,768]{1,0:T(8,128)(2,1)S(1)}, f32[8,768]{1,0:T(8,128)S(1)}) custom-call(s32[8]{0:T(128)S(1)} %stack.69.refs_0_, bf16[4,512,768]{2,1,0:T(8,128)(2,1)S(1)} %get-tuple-element.134.refs_1_, f32[512,768]{1,0:T(8,128)S(1)} %copy-done.29, f32[512,768]{1,0:T(8,128)S(1)} %copy-done.27, ...), custom_call_target="tpu_custom_call" | custom-call | flops 2530000128 | bytes 1 | tf_op jit(solution)/shard_map/pallas_call | solution.py:36
  161.2 6.5 %collective-permute-done.23.refs_2_ = bf16[192,1536]{1,0:T(8,128)(2,1)S(1)} collective-permute-done((bf16[192,1536]{1,0:T(8,128)(2,1)S(1)}, bf16[192,1536]{1,0:T(8,128)(2,1)S(1)}, u32[]{:S(2)}, u32[]{:S(2)}) %collective-permute-start.23) | collective-permute-done | bytes 589856 | tf_op jit(solution)/shard_map/ppermute | solution.py:59
  167.7 1.2 collective-permute-done.24.refs_3_
  170.3 1.5 collective-permute-start.26
  172.3 1.5 collective-permute-start.28
  173.8 10.7 %shard_map.271 = (bf16[4,3,512,128]{3,2,1,0:T(8,128)(2,1)S(1)}, bf16[4,3,80,128]{3,2,1,0:T(8,128)(2,1)S(1)}) custom-call(bf16[512,768]{1,0:T(8,128)(2,1)S(1)} %get-tuple-element.143.refs_4_.refs_0_.refs_12_, bf16[4,768,768]{2,1,0:T(8,128)(2,1)S(1)} %get-tuple-element.124.refs_8_.refs_1_.refs_2_, bf16[4,512,192]{2,1,0:T(8,128)(2,1)S(1)} %copy-done.6, ...), custom_call_target="tpu_custom_call" | custom-call | flops 2530000128 | bytes 1 | tf_op jit(solution)/shard_map/pallas_call | solution.py:36
  184.5 1.3 collective-permute-start.31
  185.8 4.8 %collective-permute-done.27.refs_2_ = bf16[96,1536]{1,0:T(8,128)(2,1)S(1)} collective-permute-done((bf16[96,1536]{1,0:T(8,128)(2,1)S(1)}, bf16[96,1536]{1,0:T(8,128)(2,1)S(1)}, u32[]{:S(2)}, u32[]{:S(2)}) %collective-permute-start.27) | collective-permute-done | bytes 294944 | tf_op jit(solution)/shard_map/ppermute | solution.py:59
  190.6 1.3 collective-permute-start.30
  191.9 1.3 collective-permute-start.29
  193.6 1.6 collective-permute-start.32
  195.2 1.4 collective-permute-start.33
  196.6 11.3 %shard_map.274.refs_6_.refs_2_ = f32[4,512,576]{2,1,0:T(8,128)S(1)} custom-call(bf16[4,512,576]{2,1,0:T(8,128)(2,1)S(1)} %get-tuple-element.117.refs_0_.refs_5_.refs_4_.refs_1_, bf16[4,3,512,128]{3,2,1,0:T(8,128)(2,1)S(1)} %get-tuple-element.153.refs_1_.refs_3_, f32[512,512]{1,0:T(8,128)S(1)} %copy-done.13, f32[512,512]{1,0:T(8,128)S(1)} %copy-done.20, ...), custom_call_target="tpu_custom_call" | custom-call | flops 3450000128 | bytes 1 | tf_op jit(solution)/shard_map/pallas_call | solution.py:36
  208.1 5.7 %collective-permute-start.35 = (bf16[192,768]{1,0:T(8,128)(2,1)S(1)}, bf16[192,768]{1,0:T(8,128)(2,1)S(1)}, u32[]{:S(2)}, u32[]{:S(2)}) collective-permute-start(bf16[192,768]{1,0:T(8,128)(2,1)S(1)} %get-tuple-element.167.refs_14_), channel_id=1, source_target_pairs={{0,3},{1,0},{2,1},{3,2},{4,7},{5,4},{6,5},{7,6},{8,11},{9,8},{10,9... | collective-permute-start | bytes 884744 | tf_op jit(solution)/shard_map/ppermute | solution.py:63
  214.4 7.0 %shard_map.276 = (bf16[2,512,768]{2,1,0:T(8,128)(2,1)S(1)}, f32[2,8,768]{2,1,0:T(8,128)S(1)}, bf16[384,1536]{1,0:T(8,128)(2,1)S(1)}, bf16[384,1536]{1,0:T(8,128)(2,1)S(1)}) custom-call(s32[8]{0:T(128)S(1)} %stack.69.refs_0_, bf16[4,512,576]{2,1,0:T(8,128)(2,1)S(1)} %get-tuple-element.117.refs_0_.refs_5_.refs_4_.refs_1_, ...), custom_call_target="tpu_custom_call" | custom-call | flops 2530000128 | bytes 1 | tf_op jit(solution)/shard_map/pallas_call | solution.py:36
  221.5 7.4 %shard_map.277 = (bf16[2,512,768]{2,1,0:T(8,128)(2,1)S(1)}, f32[2,8,768]{2,1,0:T(8,128)}, bf16[384,1536]{1,0:T(8,128)(2,1)S(1)}, bf16[392,1536]{1,0:T(8,128)(2,1)S(1)}, bf16[16,768]{1,0:T(8,128)(2,1)S(1)}) custom-call(s32[8]{0:T(128)S(1)} %stack.69.refs_0_, bf16[4,512,576]{2,1,0:T(8,128)(2,1)S(1)} %get-tuple-element.117.refs_0_.refs_5_.refs_4_.refs_1_, ...), custom_call_target="tpu_custom_call" | custom-call | flops 2530000128 | bytes 1 | tf_op jit(solution)/shard_map/pallas_call | solution.py:36
  228.9 9.4 %collective-permute-done.36.refs_2_ = bf16[192,768]{1,0:T(8,128)(2,1)S(1)} collective-permute-done((bf16[192,768]{1,0:T(8,128)(2,1)S(1)}, bf16[192,768]{1,0:T(8,128)(2,1)S(1)}, u32[]{:S(2)}, u32[]{:S(2)}) %collective-permute-start.36) | collective-permute-done | bytes 294944 | tf_op jit(solution)/shard_map/ppermute | solution.py:63
  239.1 4.1 %collective-permute-done.34.refs_1_ = bf16[384,1536]{1,0:T(8,128)(2,1)S(1)} collective-permute-done((bf16[384,1536]{1,0:T(8,128)(2,1)S(1)}, bf16[384,1536]{1,0:T(8,128)(2,1)S(1)}, u32[]{:S(2)}, u32[]{:S(2)}) %collective-permute-start.34) | collective-permute-done | bytes 1179680 | tf_op jit(solution)/shard_map/ppermute | solution.py:59
  243.7 1.6 collective-permute-start.40
  245.2 3.5 %shard_map.280.refs_5_ = bf16[512,768]{1,0:T(8,128)(2,1)} custom-call(bf16[2,512,768]{2,1,0:T(8,128)(2,1)S(1)} %get-tuple-element.170.refs_0_, bf16[2,512,768]{2,1,0:T(8,128)(2,1)S(1)} %get-tuple-element.175.refs_4_.refs_1_, bf16[4,768,768]{2,1,0:T(8,128)(2,1)S(1)} %get-tuple-element.124.refs_8_.refs_1_.refs_2_, f32[512,768]{1,0:T(8,128)S(1)} %get-tuple-element.176.refs_3_, ...), custom_call_target="tpu_custom_call" | custom-call | flops 1380000000 | bytes 1 | tf_op jit(solution)/shard_map/pallas_call | solution.py:36
  248.7 11.6 %collective-permute-done.39.refs_2_ = bf16[384,768]{1,0:T(8,128)(2,1)S(1)} collective-permute-done((bf16[384,768]{1,0:T(8,128)(2,1)S(1)}, bf16[384,768]{1,0:T(8,128)(2,1)S(1)}, u32[]{:S(2)}, u32[]{:S(2)}) %collective-permute-start.39) | collective-permute-done | bytes 589856 | tf_op jit(solution)/shard_map/ppermute | solution.py:59
  262.7 1.4 collective-permute-start.47
  264.1 1.7 collective-permute-start.46
  265.8 6.2 %collective-permute-done.41.refs_2_ = bf16[192,768]{1,0:T(8,128)(2,1)S(1)} collective-permute-done((bf16[192,768]{1,0:T(8,128)(2,1)S(1)}, bf16[192,768]{1,0:T(8,128)(2,1)S(1)}, u32[]{:S(2)}, u32[]{:S(2)}) %collective-permute-start.41) | collective-permute-done | bytes 294944 | tf_op jit(solution)/shard_map/ppermute | solution.py:59
  272.4 3.9 %collective-permute-done.47.refs_2_.refs_3_ = bf16[192,768]{1,0:T(8,128)(2,1)S(1)} collective-permute-done((bf16[192,768]{1,0:T(8,128)(2,1)S(1)}, bf16[192,768]{1,0:T(8,128)(2,1)S(1)}, u32[]{:S(2)}, u32[]{:S(2)}) %collective-permute-start.47) | collective-permute-done | bytes 294944 | tf_op jit(solution)/shard_map/ppermute | solution.py:59
  277.6 5.3 %collective-permute-done.43.refs_1_ = bf16[104,768]{1,0:T(8,128)(2,1)S(1)} collective-permute-done((bf16[104,768]{1,0:T(8,128)(2,1)S(1)}, bf16[104,768]{1,0:T(8,128)(2,1)S(1)}, u32[]{:S(2)}, u32[]{:S(2)}) %collective-permute-start.43) | collective-permute-done | bytes 159776 | tf_op jit(solution)/shard_map/ppermute | solution.py:63
  286.6 4.4 %shard_map.284 = (f32[768,768]{1,0:T(8,128)}, f32[768,768]{1,0:T(8,128)}) custom-call(s32[8]{0:T(128)S(1)} %stack.69.refs_0_, bf16[192,768]{1,0:T(8,128)(2,1)S(1)} %shard_map.278.refs_0_.refs_1_, bf16[192,768]{1,0:T(8,128)(2,1)S(1)} %collective-permute-done.46.refs_1_.refs_2_, bf16[192,768]{1,0:T(8,128)(2,1)S(1)} %collective-permute-done.47.refs_2_.refs_3_, ...), custom_call_target="tpu_custom_call" | custom-call | flops 920000000 | bytes 1 | tf_op jit(solution)/shard_map/pallas_call | solution.py:36
  291.0 5.5 %collective-permute-done.44.refs_2_ = bf16[104,768]{1,0:T(8,128)(2,1)S(1)} collective-permute-done((bf16[104,768]{1,0:T(8,128)(2,1)S(1)}, bf16[104,768]{1,0:T(8,128)(2,1)S(1)}, u32[]{:S(2)}, u32[]{:S(2)}) %collective-permute-start.44) | collective-permute-done | bytes 159776 | tf_op jit(solution)/shard_map/ppermute | solution.py:63
  296.6 1.6 collective-permute-start.52
  300.2 4.1 %collective-permute-done.52.refs_3_.refs_4_ = bf16[96,768]{1,0:T(8,128)(2,1)S(1)} collective-permute-done((bf16[96,768]{1,0:T(8,128)(2,1)S(1)}, bf16[96,768]{1,0:T(8,128)(2,1)S(1)}, u32[]{:S(2)}, u32[]{:S(2)}) %collective-permute-start.52) | collective-permute-done | bytes 147488 | tf_op jit(solution)/shard_map/ppermute | solution.py:59
  304.3 2.2 collective-permute-done.51.refs_2_.refs_3_
  308.7 2.8 shard_map.287
  (217 shorter events, 36.5 us)
Async XLA Ops:
  2.9 26.2 %copy-start.43 = (s32[1,8]{1,0:T(1,128)S(1)}, s32[1,8]{1,0:T(1,128)}, u32[]{:S(2)}) copy-start(s32[1,8]{1,0:T(1,128)} %param.16) | copy-start | bytes 100
  2.9 9.7 %collective-permute-start.2 = (bf16[104,768]{1,0:T(8,128)(2,1)S(1)}, bf16[104,768]{1,0:T(8,128)(2,1)S(1)}, u32[]{:S(2)}, u32[]{:S(2)}) collective-permute-start(bf16[104,768]{1,0:T(8,128)(2,1)S(1)} %pad_maximum_fusion.1.refs_0_), channel_id=1, source_target_pairs={{0,3},{1,0},{2,1},{3,2},{4,7},{5,4},{6,5},{7,6},{8,11},{9,8},{10,9... | collective-permute-start | bytes 479240 | tf_op jit(solution)/shard_map/ppermute | solution.py:63
  8.1 13.5 %collective-permute-start.1 = (bf16[104,768]{1,0:T(8,128)(2,1)S(1)}, bf16[104,768]{1,0:T(8,128)(2,1)S(1)}, u32[]{:S(2)}, u32[]{:S(2)}) collective-permute-start(bf16[104,768]{1,0:T(8,128)(2,1)S(1)} %pad_maximum_fusion.1.refs_0_), channel_id=1, source_target_pairs={{0,2},{1,3},{2,0},{3,1},{4,6},{5,7},{6,4},{7,5},{8,10},{9,11},{10,... | collective-permute-start | bytes 479240 | tf_op jit(solution)/shard_map/ppermute | solution.py:63
  8.1 13.5 %collective-permute-start = (bf16[104,768]{1,0:T(8,128)(2,1)S(1)}, bf16[104,768]{1,0:T(8,128)(2,1)S(1)}, u32[]{:S(2)}, u32[]{:S(2)}) collective-permute-start(bf16[104,768]{1,0:T(8,128)(2,1)S(1)} %pad_maximum_fusion.1.refs_0_), channel_id=1, source_target_pairs={{0,1},{1,2},{2,3},{3,0},{4,5},{5,6},{6,7},{7,4},{8,9},{9,10},{10,1... | collective-permute-start | bytes 479240 | tf_op jit(solution)/shard_map/ppermute | solution.py:63
  22.2 12.6 %copy-start.41 = (f32[4,1,768]{2,1,0:T(1,128)}, f32[4,1,768]{2,1,0:T(1,128)S(1)}, u32[]{:S(2)}) copy-start(f32[4,1,768]{2,1,0:T(1,128)S(1)} %get-tuple-element.126.refs_2_) | copy-start | bytes 36868
  22.2 8.4 %collective-permute-start.3 = (bf16[2,96,768]{2,1,0:T(8,128)(2,1)S(1)}, bf16[2,96,768]{2,1,0:T(8,128)(2,1)S(1)}, u32[]{:S(2)}, u32[]{:S(2)}) collective-permute-start(bf16[2,96,768]{2,1,0:T(8,128)(2,1)S(1)} %get-tuple-element.113.refs_0_), channel_id=1, source_target_pairs={{0,8},{4,12},{8,0},{12,4},{16,24},{20,28},{24,16},{28,20},{1,9},{5... | collective-permute-start | bytes 884744 | tf_op jit(solution)/shard_map/ppermute | solution.py:59
  23.7 8.2 %collective-permute-start.4 = (bf16[2,96,768]{2,1,0:T(8,128)(2,1)S(1)}, bf16[2,96,768]{2,1,0:T(8,128)(2,1)S(1)}, u32[]{:S(2)}, u32[]{:S(2)}) collective-permute-start(bf16[2,96,768]{2,1,0:T(8,128)(2,1)S(1)} %get-tuple-element.114.refs_2_), channel_id=1, source_target_pairs={{0,16},{4,20},{8,24},{12,28},{16,0},{20,4},{24,8},{28,12},{1,17},{... | collective-permute-start | bytes 884744 | tf_op jit(solution)/shard_map/ppermute | solution.py:59
  26.3 22.6 %collective-permute-start.10 = (bf16[192,768]{1,0:T(8,128)(2,1)S(1)}, bf16[192,768]{1,0:T(8,128)(2,1)S(1)}, u32[]{:S(2)}, u32[]{:S(2)}) collective-permute-start(bf16[192,768]{1,0:T(8,128)(2,1)S(1)} %pad_maximum_fusion.refs_0_), channel_id=1, source_target_pairs={{0,2},{1,3},{2,0},{3,1},{4,6},{5,7},{6,4},{7,5},{8,10},{9,11},{10,... | collective-permute-start | bytes 884744 | tf_op jit(solution)/shard_map/ppermute | solution.py:63
  29.1 19.7 %collective-permute-start.9 = (bf16[192,768]{1,0:T(8,128)(2,1)S(1)}, bf16[192,768]{1,0:T(8,128)(2,1)S(1)}, u32[]{:S(2)}, u32[]{:S(2)}) collective-permute-start(bf16[192,768]{1,0:T(8,128)(2,1)S(1)} %pad_maximum_fusion.refs_0_), channel_id=1, source_target_pairs={{0,1},{1,2},{2,3},{3,0},{4,5},{5,6},{6,7},{7,4},{8,9},{9,10},{10,1... | collective-permute-start | bytes 884744 | tf_op jit(solution)/shard_map/ppermute | solution.py:63
  32.0 13.6 %collective-permute-start.5 = (bf16[2,2,96,768]{3,2,1,0:T(8,128)(2,1)S(1)}, bf16[2,2,96,768]{3,2,1,0:T(8,128)(2,1)S(1)}, u32[]{:S(2)}, u32[]{:S(2)}) collective-permute-start(bf16[2,2,96,768]{3,2,1,0:T(8,128)(2,1)S(1)} %get-tuple-element.115.refs_0_.refs_4_), channel_id=1, source_target_pairs={{0,16},{4,20},{8,24},{12,28},{16,0},{20,4},{24,8},{28,12},{1,17},{... | collective-permute-start | bytes 1769480 | tf_op jit(solution)/shard_map/ppermute | solution.py:59
  33.6 13.3 %collective-permute-start.6 = (bf16[2,2,96,768]{3,2,1,0:T(8,128)(2,1)S(1)}, bf16[2,2,96,768]{3,2,1,0:T(8,128)(2,1)S(1)}, u32[]{:S(2)}, u32[]{:S(2)}) collective-permute-start(bf16[2,2,96,768]{3,2,1,0:T(8,128)(2,1)S(1)} %get-tuple-element.116.refs_1_.refs_6_.refs_5_), channel_id=1, source_target_pairs={{0,8},{4,12},{8,0},{12,4},{16,24},{20,28},{24,16},{28,20},{1,9},{5... | collective-permute-start | bytes 1769480 | tf_op jit(solution)/shard_map/ppermute | solution.py:59
  36.7 28.1 %collective-permute-start.7 = (bf16[2,2,2,96,768]{4,3,2,1,0:T(8,128)(2,1)}, bf16[2,2,2,96,768]{4,3,2,1,0:T(8,128)(2,1)}, u32[]{:S(2)}, u32[]{:S(2)}) collective-permute-start(bf16[2,2,2,96,768]{4,3,2,1,0:T(8,128)(2,1)} %shard_map.256), channel_id=1, source_target_pairs={{0,4},{4,0},{8,12},{12,8},{16,20},{20,16},{24,28},{28,24},{1,5},{5... | collective-permute-start | bytes 3538952 | tf_op jit(solution)/shard_map/ppermute | solution.py:59
  45.6 13.2 %copy-start.22 = (bf16[2,2,96,768]{3,2,1,0:T(8,128)(2,1)}, bf16[2,2,96,768]{3,2,1,0:T(8,128)(2,1)S(1)}, u32[]{:S(2)}) copy-start(bf16[2,2,96,768]{3,2,1,0:T(8,128)(2,1)S(1)} %collective-permute-done.5.refs_0_.refs_5_) | copy-start | bytes 1769476
  48.0 16.8 %collective-permute-start.8 = (bf16[2,2,2,96,768]{4,3,2,1,0:T(8,128)(2,1)}, bf16[2,2,2,96,768]{4,3,2,1,0:T(8,128)(2,1)}, u32[]{:S(2)}, u32[]{:S(2)}) collective-permute-start(bf16[2,2,2,96,768]{4,3,2,1,0:T(8,128)(2,1)} %shard_map.257), channel_id=1, source_target_pairs={{0,4},{4,0},{8,12},{12,8},{16,20},{20,16},{24,28},{28,24},{1,5},{5... | collective-permute-start | bytes 3538952 | tf_op jit(solution)/shard_map/ppermute | solution.py:59
  48.2 9.5 %collective-permute-start.11 = (bf16[192,768]{1,0:T(8,128)(2,1)S(1)}, bf16[192,768]{1,0:T(8,128)(2,1)S(1)}, u32[]{:S(2)}, u32[]{:S(2)}) collective-permute-start(bf16[192,768]{1,0:T(8,128)(2,1)S(1)} %pad_maximum_fusion.refs_0_), channel_id=1, source_target_pairs={{0,3},{1,0},{2,1},{3,2},{4,7},{5,4},{6,5},{7,6},{8,11},{9,8},{10,9... | collective-permute-start | bytes 884744 | tf_op jit(solution)/shard_map/ppermute | solution.py:63
  58.8 26.9 %collective-permute-start.12 = (bf16[2,192,768]{2,1,0:T(8,128)(2,1)}, bf16[2,192,768]{2,1,0:T(8,128)(2,1)}, u32[]{:S(2)}, u32[]{:S(2)}) collective-permute-start(bf16[2,192,768]{2,1,0:T(8,128)(2,1)} %get-tuple-element.119.refs_0_), channel_id=1, source_target_pairs={{0,8},{4,12},{8,0},{12,4},{16,24},{20,28},{24,16},{28,20},{1,9},{5... | collective-permute-start | bytes 1769480 | tf_op jit(solution)/shard_map/ppermute | solution.py:59
  59.3 26.3 %collective-permute-start.13 = (bf16[2,192,768]{2,1,0:T(8,128)(2,1)}, bf16[2,192,768]{2,1,0:T(8,128)(2,1)}, u32[]{:S(2)}, u32[]{:S(2)}) collective-permute-start(bf16[2,192,768]{2,1,0:T(8,128)(2,1)} %get-tuple-element.120.refs_2_), channel_id=1, source_target_pairs={{0,16},{4,20},{8,24},{12,28},{16,0},{20,4},{24,8},{28,12},{1,17},{... | collective-permute-start | bytes 1769480 | tf_op jit(solution)/shard_map/ppermute | solution.py:59
  60.2 16.1 %copy-start.17 = (f32[512,128]{1,0:T(8,128)}, f32[512,128]{1,0:T(8,128)S(1)}, u32[]{:S(2)}) copy-start(f32[512,128]{1,0:T(8,128)S(1)} %get-tuple-element.232.refs_3_.refs_9_) | copy-start | bytes 786436
  64.8 24.7 %copy-start.12 = (f32[512,512]{1,0:T(8,128)}, f32[512,512]{1,0:T(8,128)S(1)}, u32[]{:S(2)}) copy-start(f32[512,512]{1,0:T(8,128)S(1)} %get-tuple-element.230.refs_10_.refs_1_.refs_2_) | copy-start | bytes 3145732
  68.1 17.5 %copy-start.44 = (bf16[768]{0:T(1024)(128)(2,1)S(1)}, bf16[768]{0:T(1024)(128)(2,1)}, u32[]{:S(2)}) copy-start(bf16[768]{0:T(1024)(128)(2,1)} %param.21) | copy-start | bytes 4612
  68.1 17.5 %copy-start.45 = (bf16[768]{0:T(1024)(128)(2,1)S(1)}, bf16[768]{0:T(1024)(128)(2,1)}, u32[]{:S(2)}) copy-start(bf16[768]{0:T(1024)(128)(2,1)} %param.20) | copy-start | bytes 4612
  68.1 17.5 %copy-start.46 = (bf16[768]{0:T(1024)(128)(2,1)S(1)}, bf16[768]{0:T(1024)(128)(2,1)}, u32[]{:S(2)}) copy-start(bf16[768]{0:T(1024)(128)(2,1)} %param.22) | copy-start | bytes 4612
  76.3 18.2 %collective-permute-start.16 = (bf16[4,3,80,128]{3,2,1,0:T(8,128)(2,1)S(1)}, bf16[4,3,80,128]{3,2,1,0:T(8,128)(2,1)S(1)}, u32[]{:S(2)}, u32[]{:S(2)}) collective-permute-start(bf16[4,3,80,128]{3,2,1,0:T(8,128)(2,1)S(1)} %get-tuple-element.121.refs_4_), channel_id=1, source_target_pairs={{0,3},{4,7},{8,11},{12,15},{16,19},{20,23},{24,27},{28,31}} | collective-permute-start | bytes 737288 | tf_op jit(solution)/shard_map/ppermute | solution.py:68
  81.6 12.9 %collective-permute-start.15 = (bf16[4,3,80,128]{3,2,1,0:T(8,128)(2,1)S(1)}, bf16[4,3,80,128]{3,2,1,0:T(8,128)(2,1)S(1)}, u32[]{:S(2)}, u32[]{:S(2)}) collective-permute-start(bf16[4,3,80,128]{3,2,1,0:T(8,128)(2,1)S(1)} %get-tuple-element.121.refs_4_), channel_id=1, source_target_pairs={{0,2},{1,3},{4,6},{5,7},{8,10},{9,11},{12,14},{13,15},{16,18},{17,... | collective-permute-start | bytes 737288 | tf_op jit(solution)/shard_map/ppermute | solution.py:68
  82.9 13.8 %collective-permute-start.14 = (bf16[4,3,80,128]{3,2,1,0:T(8,128)(2,1)S(1)}, bf16[4,3,80,128]{3,2,1,0:T(8,128)(2,1)S(1)}, u32[]{:S(2)}, u32[]{:S(2)}) collective-permute-start(bf16[4,3,80,128]{3,2,1,0:T(8,128)(2,1)S(1)} %get-tuple-element.121.refs_4_), channel_id=1, source_target_pairs={{0,1},{1,2},{2,3},{4,5},{5,6},{6,7},{8,9},{9,10},{10,11},{12,13},{... | collective-permute-start | bytes 737288 | tf_op jit(solution)/shard_map/ppermute | solution.py:68
  87.4 26.5 %collective-permute-start.17 = (bf16[2,2,192,768]{3,2,1,0:T(8,128)(2,1)S(1)}, bf16[2,2,192,768]{3,2,1,0:T(8,128)(2,1)S(1)}, u32[]{:S(2)}, u32[]{:S(2)}) collective-permute-start(bf16[2,2,192,768]{3,2,1,0:T(8,128)(2,1)S(1)} %get-tuple-element.127.refs_2_.refs_0_.refs_7_.refs_4_.refs_6_), channel_id=1, source_target_pairs={{0,16},{4,20},{8,24},{12,28},{16,0},{20,4},{24,8},{28,12},{1,17},{... | collective-permute-start | bytes 3538952 | tf_op jit(solution)/shard_map/ppermute | solution.py:59
  88.0 26.2 %collective-permute-start.18 = (bf16[2,2,192,768]{3,2,1,0:T(8,128)(2,1)S(1)}, bf16[2,2,192,768]{3,2,1,0:T(8,128)(2,1)S(1)}, u32[]{:S(2)}, u32[]{:S(2)}) collective-permute-start(bf16[2,2,192,768]{3,2,1,0:T(8,128)(2,1)S(1)} %get-tuple-element.129.refs_3_.refs_1_.refs_9_.refs_6_.refs_8_), channel_id=1, source_target_pairs={{0,8},{4,12},{8,0},{12,4},{16,24},{20,28},{24,16},{28,20},{1,9},{5... | collective-permute-start | bytes 3538952 | tf_op jit(solution)/shard_map/ppermute | solution.py:59
  114.4 4.6 %collective-permute-start.20 = (bf16[2,2,2,192,768]{4,3,2,1,0:T(8,128)(2,1)S(1)}, bf16[2,2,2,192,768]{4,3,2,1,0:T(8,128)(2,1)S(1)}, u32[]{:S(2)}, u32[]{:S(2)}) collective-permute-start(bf16[2,2,2,192,768]{4,3,2,1,0:T(8,128)(2,1)S(1)} %shard_map.264), channel_id=1, source_target_pairs={{0,4},{4,0},{8,12},{12,8},{16,20},{20,16},{24,28},{28,24},{1,5},{5... | collective-permute-start | bytes 7077896 | tf_op jit(solution)/shard_map/ppermute | solution.py:59
  114.7 7.7 %collective-permute-start.19 = (bf16[2,2,2,192,768]{4,3,2,1,0:T(8,128)(2,1)S(1)}, bf16[2,2,2,192,768]{4,3,2,1,0:T(8,128)(2,1)S(1)}, u32[]{:S(2)}, u32[]{:S(2)}) collective-permute-start(bf16[2,2,2,192,768]{4,3,2,1,0:T(8,128)(2,1)S(1)} %shard_map.263), channel_id=1, source_target_pairs={{0,4},{4,0},{8,12},{12,8},{16,20},{20,16},{24,28},{28,24},{1,5},{5... | collective-permute-start | bytes 7077896 | tf_op jit(solution)/shard_map/ppermute | solution.py:59
  119.0 19.4 %copy-start.7 = (bf16[2,2,2,192,768]{4,3,2,1,0:T(8,128)(2,1)}, bf16[2,2,2,192,768]{4,3,2,1,0:T(8,128)(2,1)S(1)}, u32[]{:S(2)}) copy-start(bf16[2,2,2,192,768]{4,3,2,1,0:T(8,128)(2,1)S(1)} %collective-permute-done.20.refs_12_.refs_9_.refs_11_) | copy-start | bytes 7077892
  122.4 17.9 %copy-start.10 = (bf16[2,2,2,192,768]{4,3,2,1,0:T(8,128)(2,1)}, bf16[2,2,2,192,768]{4,3,2,1,0:T(8,128)(2,1)S(1)}, u32[]{:S(2)}) copy-start(bf16[2,2,2,192,768]{4,3,2,1,0:T(8,128)(2,1)S(1)} %collective-permute-done.19.refs_11_.refs_8_.refs_10_) | copy-start | bytes 7077892
  140.1 11.6 %collective-permute-start.21 = (bf16[384,3072]{1,0:T(8,128)(2,1)}, bf16[384,3072]{1,0:T(8,128)(2,1)S(1)}, u32[]{:S(2)}, u32[]{:S(2)}) collective-permute-start(bf16[384,3072]{1,0:T(8,128)(2,1)} %get-tuple-element.139), channel_id=1, source_target_pairs={{0,4},{4,0},{8,12},{12,8},{16,20},{20,16},{24,28},{28,24},{1,5},{5... | collective-permute-start | bytes 7077896 | tf_op jit(solution)/shard_map/ppermute | solution.py:59
  151.3 17.8 %collective-permute-start.22 = (bf16[384,3072]{1,0:T(8,128)(2,1)S(1)}, bf16[384,3072]{1,0:T(8,128)(2,1)S(1)}, u32[]{:S(2)}, u32[]{:S(2)}) collective-permute-start(bf16[384,3072]{1,0:T(8,128)(2,1)S(1)} %get-tuple-element.140.refs_2_), channel_id=1, source_target_pairs={{0,4},{4,0},{8,12},{12,8},{16,20},{20,16},{24,28},{28,24},{1,5},{5... | collective-permute-start | bytes 7077896 | tf_op jit(solution)/shard_map/ppermute | solution.py:59
  152.3 15.4 %collective-permute-start.23 = (bf16[192,1536]{1,0:T(8,128)(2,1)S(1)}, bf16[192,1536]{1,0:T(8,128)(2,1)S(1)}, u32[]{:S(2)}, u32[]{:S(2)}) collective-permute-start(bf16[192,1536]{1,0:T(8,128)(2,1)S(1)} %get-tuple-element.141.refs_12_), channel_id=1, source_target_pairs={{0,8},{4,12},{8,0},{12,4},{16,24},{20,28},{24,16},{28,20},{1,9},{5... | collective-permute-start | bytes 1769480 | tf_op jit(solution)/shard_map/ppermute | solution.py:59
  153.9 15.1 %collective-permute-start.24 = (bf16[192,1536]{1,0:T(8,128)(2,1)S(1)}, bf16[192,1536]{1,0:T(8,128)(2,1)S(1)}, u32[]{:S(2)}, u32[]{:S(2)}) collective-permute-start(bf16[192,1536]{1,0:T(8,128)(2,1)S(1)} %get-tuple-element.142.refs_13_), channel_id=1, source_target_pairs={{0,16},{4,20},{8,24},{12,28},{16,0},{20,4},{24,8},{28,12},{1,17},{... | collective-permute-start | bytes 1769480 | tf_op jit(solution)/shard_map/ppermute | solution.py:59
  169.7 23.6 %collective-permute-start.25 = (bf16[192,1536]{1,0:T(8,128)(2,1)S(1)}, bf16[192,1536]{1,0:T(8,128)(2,1)S(1)}, u32[]{:S(2)}, u32[]{:S(2)}) collective-permute-start(bf16[192,1536]{1,0:T(8,128)(2,1)S(1)} %get-tuple-element.151.refs_6_), channel_id=1, source_target_pairs={{0,8},{4,12},{8,0},{12,4},{16,24},{20,28},{24,16},{28,20},{1,9},{5... | collective-permute-start | bytes 1769480 | tf_op jit(solution)/shard_map/ppermute | solution.py:59
  170.3 23.1 %collective-permute-start.26 = (bf16[192,1536]{1,0:T(8,128)(2,1)S(1)}, bf16[192,1536]{1,0:T(8,128)(2,1)S(1)}, u32[]{:S(2)}, u32[]{:S(2)}) collective-permute-start(bf16[192,1536]{1,0:T(8,128)(2,1)S(1)} %get-tuple-element.152.refs_7_), channel_id=1, source_target_pairs={{0,16},{4,20},{8,24},{12,28},{16,0},{20,4},{24,8},{28,12},{1,17},{... | collective-permute-start | bytes 1769480 | tf_op jit(solution)/shard_map/ppermute | solution.py:59
  171.8 18.8 %collective-permute-start.27 = (bf16[96,1536]{1,0:T(8,128)(2,1)S(1)}, bf16[96,1536]{1,0:T(8,128)(2,1)S(1)}, u32[]{:S(2)}, u32[]{:S(2)}) collective-permute-start(bf16[96,1536]{1,0:T(8,128)(2,1)S(1)} %get-tuple-element.149.refs_2_), channel_id=1, source_target_pairs={{0,16},{4,20},{8,24},{12,28},{16,0},{20,4},{24,8},{28,12},{1,17},{... | collective-permute-start | bytes 884744 | tf_op jit(solution)/shard_map/ppermute | solution.py:59
  172.3 19.6 %collective-permute-start.28 = (bf16[96,1536]{1,0:T(8,128)(2,1)S(1)}, bf16[96,1536]{1,0:T(8,128)(2,1)S(1)}, u32[]{:S(2)}, u32[]{:S(2)}) collective-permute-start(bf16[96,1536]{1,0:T(8,128)(2,1)S(1)} %get-tuple-element.150.refs_3_), channel_id=1, source_target_pairs={{0,8},{4,12},{8,0},{12,4},{16,24},{20,28},{24,16},{28,20},{1,9},{5... | collective-permute-start | bytes 884744 | tf_op jit(solution)/shard_map/ppermute | solution.py:59
  184.5 23.3 %collective-permute-start.31 = (bf16[4,3,80,128]{3,2,1,0:T(8,128)(2,1)S(1)}, bf16[4,3,80,128]{3,2,1,0:T(8,128)(2,1)S(1)}, u32[]{:S(2)}, u32[]{:S(2)}) collective-permute-start(bf16[4,3,80,128]{3,2,1,0:T(8,128)(2,1)S(1)} %get-tuple-element.158.refs_4_), channel_id=1, source_target_pairs={{3,0},{7,4},{11,8},{15,12},{19,16},{23,20},{27,24},{31,28}} | collective-permute-start | bytes 737288 | tf_op jit(solution)/shard_map/ppermute | solution.py:68
  190.6 17.3 %collective-permute-start.30 = (bf16[4,3,80,128]{3,2,1,0:T(8,128)(2,1)S(1)}, bf16[4,3,80,128]{3,2,1,0:T(8,128)(2,1)S(1)}, u32[]{:S(2)}, u32[]{:S(2)}) collective-permute-start(bf16[4,3,80,128]{3,2,1,0:T(8,128)(2,1)S(1)} %get-tuple-element.158.refs_4_), channel_id=1, source_target_pairs={{2,0},{3,1},{6,4},{7,5},{10,8},{11,9},{14,12},{15,13},{18,16},{19,... | collective-permute-start | bytes 737288 | tf_op jit(solution)/shard_map/ppermute | solution.py:68
  191.9 16.0 %collective-permute-start.29 = (bf16[4,3,80,128]{3,2,1,0:T(8,128)(2,1)S(1)}, bf16[4,3,80,128]{3,2,1,0:T(8,128)(2,1)S(1)}, u32[]{:S(2)}, u32[]{:S(2)}) collective-permute-start(bf16[4,3,80,128]{3,2,1,0:T(8,128)(2,1)S(1)} %get-tuple-element.158.refs_4_), channel_id=1, source_target_pairs={{1,0},{2,1},{3,2},{5,4},{6,5},{7,6},{9,8},{10,9},{11,10},{13,12},{... | collective-permute-start | bytes 737288 | tf_op jit(solution)/shard_map/ppermute | solution.py:68
  193.6 14.3 %collective-permute-start.32 = (bf16[96,1536]{1,0:T(8,128)(2,1)S(1)}, bf16[96,1536]{1,0:T(8,128)(2,1)S(1)}, u32[]{:S(2)}, u32[]{:S(2)}) collective-permute-start(bf16[96,1536]{1,0:T(8,128)(2,1)S(1)} %get-tuple-element.161.refs_4_), channel_id=1, source_target_pairs={{0,16},{4,20},{8,24},{12,28},{16,0},{20,4},{24,8},{28,12},{1,17},{... | collective-permute-start | bytes 884744 | tf_op jit(solution)/shard_map/ppermute | solution.py:59
  195.2 12.8 %collective-permute-start.33 = (bf16[96,1536]{1,0:T(8,128)(2,1)S(1)}, bf16[96,1536]{1,0:T(8,128)(2,1)S(1)}, u32[]{:S(2)}, u32[]{:S(2)}) collective-permute-start(bf16[96,1536]{1,0:T(8,128)(2,1)S(1)} %get-tuple-element.162.refs_5_), channel_id=1, source_target_pairs={{0,8},{4,12},{8,0},{12,4},{16,24},{20,28},{24,16},{28,20},{1,9},{5... | collective-permute-start | bytes 884744 | tf_op jit(solution)/shard_map/ppermute | solution.py:59
  208.1 20.9 %collective-permute-start.35 = (bf16[192,768]{1,0:T(8,128)(2,1)S(1)}, bf16[192,768]{1,0:T(8,128)(2,1)S(1)}, u32[]{:S(2)}, u32[]{:S(2)}) collective-permute-start(bf16[192,768]{1,0:T(8,128)(2,1)S(1)} %get-tuple-element.167.refs_14_), channel_id=1, source_target_pairs={{0,3},{1,0},{2,1},{3,2},{4,7},{5,4},{6,5},{7,6},{8,11},{9,8},{10,9... | collective-permute-start | bytes 884744 | tf_op jit(solution)/shard_map/ppermute | solution.py:63
  213.8 24.6 %collective-permute-start.36 = (bf16[192,768]{1,0:T(8,128)(2,1)S(1)}, bf16[192,768]{1,0:T(8,128)(2,1)S(1)}, u32[]{:S(2)}, u32[]{:S(2)}) collective-permute-start(bf16[192,768]{1,0:T(8,128)(2,1)S(1)} %get-tuple-element.168.refs_15_), channel_id=1, source_target_pairs={{0,2},{1,3},{2,0},{3,1},{4,6},{5,7},{6,4},{7,5},{8,10},{9,11},{10,... | collective-permute-start | bytes 884744 | tf_op jit(solution)/shard_map/ppermute | solution.py:63
  213.8 24.6 %collective-permute-start.37 = (bf16[192,768]{1,0:T(8,128)(2,1)S(1)}, bf16[192,768]{1,0:T(8,128)(2,1)S(1)}, u32[]{:S(2)}, u32[]{:S(2)}) collective-permute-start(bf16[192,768]{1,0:T(8,128)(2,1)S(1)} %get-tuple-element.169.refs_16_), channel_id=1, source_target_pairs={{0,1},{1,2},{2,3},{3,0},{4,5},{5,6},{6,7},{7,4},{8,9},{9,10},{10,1... | collective-permute-start | bytes 884744 | tf_op jit(solution)/shard_map/ppermute | solution.py:63
  238.5 4.6 %collective-permute-start.38 = (bf16[392,1536]{1,0:T(8,128)(2,1)S(1)}, bf16[392,1536]{1,0:T(8,128)(2,1)S(1)}, u32[]{:S(2)}, u32[]{:S(2)}) collective-permute-start(bf16[392,1536]{1,0:T(8,128)(2,1)S(1)} %get-tuple-element.182), channel_id=1, source_target_pairs={{0,4},{4,0},{8,12},{12,8},{16,20},{20,16},{24,28},{28,24},{1,5},{5... | collective-permute-start | bytes 3612680 | tf_op jit(solution)/shard_map/ppermute | solution.py:59
  238.6 4.6 %collective-permute-start.34 = (bf16[384,1536]{1,0:T(8,128)(2,1)S(1)}, bf16[384,1536]{1,0:T(8,128)(2,1)S(1)}, u32[]{:S(2)}, u32[]{:S(2)}) collective-permute-start(bf16[384,1536]{1,0:T(8,128)(2,1)S(1)} %get-tuple-element.178), channel_id=1, source_target_pairs={{0,4},{4,0},{8,12},{12,8},{16,20},{20,16},{24,28},{28,24},{1,5},{5... | collective-permute-start | bytes 3538952 | tf_op jit(solution)/shard_map/ppermute | solution.py:59
  243.7 16.7 %collective-permute-start.40 = (bf16[400,768]{1,0:T(8,128)(2,1)S(1)}, bf16[400,768]{1,0:T(8,128)(2,1)S(1)}, u32[]{:S(2)}, u32[]{:S(2)}) collective-permute-start(bf16[400,768]{1,0:T(8,128)(2,1)S(1)} %get-tuple-element.185.refs_5_), channel_id=1, source_target_pairs={{0,16},{4,20},{8,24},{12,28},{16,0},{20,4},{24,8},{28,12},{1,17},{... | collective-permute-start | bytes 1843208 | tf_op jit(solution)/shard_map/ppermute | solution.py:59
  245.2 15.1 %collective-permute-start.39 = (bf16[384,768]{1,0:T(8,128)(2,1)S(1)}, bf16[384,768]{1,0:T(8,128)(2,1)S(1)}, u32[]{:S(2)}, u32[]{:S(2)}) collective-permute-start(bf16[384,768]{1,0:T(8,128)(2,1)S(1)} %get-tuple-element.184.refs_4_), channel_id=1, source_target_pairs={{0,8},{4,12},{8,0},{12,4},{16,24},{20,28},{24,16},{28,20},{1,9},{5... | collective-permute-start | bytes 1769480 | tf_op jit(solution)/shard_map/ppermute | solution.py:59
  261.7 10.5 %collective-permute-start.42 = (bf16[208,768]{1,0:T(8,128)(2,1)S(1)}, bf16[208,768]{1,0:T(8,128)(2,1)S(1)}, u32[]{:S(2)}, u32[]{:S(2)}) collective-permute-start(bf16[208,768]{1,0:T(8,128)(2,1)S(1)} %get-tuple-element.192), channel_id=1, source_target_pairs={{0,8},{4,12},{8,0},{12,4},{16,24},{20,28},{24,16},{28,20},{1,9},{5... | collective-permute-start | bytes 958472 | tf_op jit(solution)/shard_map/ppermute | solution.py:59
  262.1 9.9 %collective-permute-start.41 = (bf16[192,768]{1,0:T(8,128)(2,1)S(1)}, bf16[192,768]{1,0:T(8,128)(2,1)S(1)}, u32[]{:S(2)}, u32[]{:S(2)}) collective-permute-start(bf16[192,768]{1,0:T(8,128)(2,1)S(1)} %get-tuple-element.191), channel_id=1, source_target_pairs={{0,16},{4,20},{8,24},{12,28},{16,0},{20,4},{24,8},{28,12},{1,17},{... | collective-permute-start | bytes 884744 | tf_op jit(solution)/shard_map/ppermute | solution.py:59
  262.7 13.7 %collective-permute-start.47 = (bf16[192,768]{1,0:T(8,128)(2,1)S(1)}, bf16[192,768]{1,0:T(8,128)(2,1)S(1)}, u32[]{:S(2)}, u32[]{:S(2)}) collective-permute-start(bf16[192,768]{1,0:T(8,128)(2,1)S(1)} %shard_map.278.refs_0_.refs_1_), channel_id=1, source_target_pairs={{0,16},{4,20},{8,24},{12,28},{16,0},{20,4},{24,8},{28,12},{1,17},{... | collective-permute-start | bytes 884744 | tf_op jit(solution)/shard_map/ppermute | solution.py:59
  264.1 12.4 %collective-permute-start.46 = (bf16[192,768]{1,0:T(8,128)(2,1)S(1)}, bf16[192,768]{1,0:T(8,128)(2,1)S(1)}, u32[]{:S(2)}, u32[]{:S(2)}) collective-permute-start(bf16[192,768]{1,0:T(8,128)(2,1)S(1)} %shard_map.278.refs_0_.refs_1_), channel_id=1, source_target_pairs={{0,8},{4,12},{8,0},{12,4},{16,24},{20,28},{24,16},{28,20},{1,9},{5... | collective-permute-start | bytes 884744 | tf_op jit(solution)/shard_map/ppermute | solution.py:59
  276.5 7.0 %collective-permute-start.48 = (bf16[192,768]{1,0:T(8,128)(2,1)S(1)}, bf16[192,768]{1,0:T(8,128)(2,1)S(1)}, u32[]{:S(2)}, u32[]{:S(2)}) collective-permute-start(bf16[192,768]{1,0:T(8,128)(2,1)S(1)} %collective-permute-done.46.refs_1_.refs_2_), channel_id=1, source_target_pairs={{0,16},{4,20},{8,24},{12,28},{16,0},{20,4},{24,8},{28,12},{1,17},{... | collective-permute-start | bytes 884744 | tf_op jit(solution)/shard_map/ppermute | solution.py:59
  277.6 5.3 %collective-permute-start.43 = (bf16[104,768]{1,0:T(8,128)(2,1)S(1)}, bf16[104,768]{1,0:T(8,128)(2,1)S(1)}, u32[]{:S(2)}, u32[]{:S(2)}) collective-permute-start(bf16[104,768]{1,0:T(8,128)(2,1)S(1)} %get-tuple-element.195), channel_id=1, source_target_pairs={{0,3},{1,0},{2,1},{3,2},{4,7},{5,4},{6,5},{7,6},{8,11},{9,8},{10,9... | collective-permute-start | bytes 479240 | tf_op jit(solution)/shard_map/ppermute | solution.py:63
  283.6 3.0 collective-permute-start.49
  283.7 12.8 %collective-permute-start.44 = (bf16[104,768]{1,0:T(8,128)(2,1)S(1)}, bf16[104,768]{1,0:T(8,128)(2,1)S(1)}, u32[]{:S(2)}, u32[]{:S(2)}) collective-permute-start(bf16[104,768]{1,0:T(8,128)(2,1)S(1)} %get-tuple-element.196), channel_id=1, source_target_pairs={{0,2},{1,3},{2,0},{3,1},{4,6},{5,7},{6,4},{7,5},{8,10},{9,11},{10,... | collective-permute-start | bytes 479240 | tf_op jit(solution)/shard_map/ppermute | solution.py:63
  284.5 12.0 %collective-permute-start.45 = (bf16[104,768]{1,0:T(8,128)(2,1)S(1)}, bf16[104,768]{1,0:T(8,128)(2,1)S(1)}, u32[]{:S(2)}, u32[]{:S(2)}) collective-permute-start(bf16[104,768]{1,0:T(8,128)(2,1)S(1)} %get-tuple-element.197), channel_id=1, source_target_pairs={{0,1},{1,2},{2,3},{3,0},{4,5},{5,6},{6,7},{7,4},{8,9},{9,10},{10,1... | collective-permute-start | bytes 479240 | tf_op jit(solution)/shard_map/ppermute | solution.py:63
  296.6 7.7 %collective-permute-start.52 = (bf16[96,768]{1,0:T(8,128)(2,1)S(1)}, bf16[96,768]{1,0:T(8,128)(2,1)S(1)}, u32[]{:S(2)}, u32[]{:S(2)}) collective-permute-start(bf16[96,768]{1,0:T(8,128)(2,1)S(1)} %shard_map.285.refs_0_.refs_1_), channel_id=1, source_target_pairs={{0,24},{4,28},{8,16},{12,20},{16,8},{20,12},{24,0},{28,4},{1,25},{... | collective-permute-start | bytes 442376 | tf_op jit(solution)/shard_map/ppermute | solution.py:59
  298.2 8.3 %collective-permute-start.51 = (bf16[96,768]{1,0:T(8,128)(2,1)S(1)}, bf16[96,768]{1,0:T(8,128)(2,1)S(1)}, u32[]{:S(2)}, u32[]{:S(2)}) collective-permute-start(bf16[96,768]{1,0:T(8,128)(2,1)S(1)} %shard_map.285.refs_0_.refs_1_), channel_id=1, source_target_pairs={{0,16},{4,20},{8,24},{12,28},{16,0},{20,4},{24,8},{28,12},{1,17},{... | collective-permute-start | bytes 442376 | tf_op jit(solution)/shard_map/ppermute | solution.py:59
  299.3 7.2 %collective-permute-start.50 = (bf16[96,768]{1,0:T(8,128)(2,1)S(1)}, bf16[96,768]{1,0:T(8,128)(2,1)S(1)}, u32[]{:S(2)}, u32[]{:S(2)}) collective-permute-start(bf16[96,768]{1,0:T(8,128)(2,1)S(1)} %shard_map.285.refs_0_.refs_1_), channel_id=1, source_target_pairs={{0,8},{4,12},{8,0},{12,4},{16,24},{20,28},{24,16},{28,20},{1,9},{5... | collective-permute-start | bytes 442376 | tf_op jit(solution)/shard_map/ppermute | solution.py:59
  306.6 2.1 collective-permute-start.53
  (40 other events, 178.4 us)
where the time goes:
time: 317 us; the launch traced here: 312 us
  waiting for transfers between devices  118 us (37%)
  Pallas kernels  105 us (33%)
  starting transfers between devices  61.8 us (19%)
  local copies, waits for them, and re-layouts  17.5 us (6%)
  between operations  6.99 us (2%)
    pallas_call x34, Pallas kernels, call(): pl.pallas_call(waiting_body, out_shape=outs, in_specs=list(specs) + [ANY]...  105 us
    ppermute x36, waiting for transfers between devices, swap(): return lax.ppermute(value, 'dp', [(d, d ^ mask) for d in range(self.dp)])  74.7 us
    ppermute x12, waiting for transfers between devices, turn(): lax.ppermute(value, 'tensor', [(k, (k + step) % size) for k in range(size)])  41.5 us
    ppermute x36, starting transfers between devices, swap(): return lax.ppermute(value, 'dp', [(d, d ^ mask) for d in range(self.dp)])  30.8 us
    ppermute x12, starting transfers between devices, turn(): lax.ppermute(value, 'tensor', [(k, (k + step) % size) for k in range(size)])  17.8 us
    ppermute x6, starting transfers between devices, onward(): return lax.ppermute(value, 'tensor', pairs)  13.1 us
    unnamed x107, local copies, waits for them, and re-layouts  12.8 us
  transfers between devices with their start and end apart: 54, of which 29 were waited for; matrix products, arithmetic and copies ran while one was open for 1% of the time, Pallas kernels for 27%

commit v1 on v0

--- a/solution.py
+++ b/solution.py
@@ -686,7 +686,7 @@
     mixed, state, mix_weight = call(
         mix_kernel,
         (shaped((tensor, count, wide), BF16), states, shaped((tensor, width, width), BF16)),
-        [SMEM, VMEM, VMEM, VMEM] + [ANY] * 6, [sems(32)], after=(mask, mask_t), limit=9, cost=8,
+        [SMEM, VMEM, VMEM, VMEM] + [ANY] * 6, [sems(32)], limit=9, cost=8,
     )(info, tokens, bias_qkv, key_table, *mix_buffers)
     per_head = shaped((tensor, 3, count, 2 * HEAD), F32)
     arrived = [places.onward(state, s) for s in range(1, tensor)]
@@ -785,19 +785,18 @@
         mix_last_kernel, (shaped((rows + 8, width), BF16),) * tensor, [VMEM] * 5,
     )(keep0, keep1, *got, vector_rows)
     mix_own = turn_back(places, mix_last)
-    feed_x, feed_y = later((feed_x, feed_y), mix_last)
-    feed_xy = later(places.swap(feed_x, Y), mix_own[1])
-    feed_all = spread_cores(places, [feed_low, feed_x, feed_y, feed_xy])
+    feed_x, feed_y = later((feed_x, feed_y), mix_own[1])
+    feed_all = spread_cores(places, [feed_low, feed_x, feed_y, places.swap(feed_x, Y)])
 
     held = pltpu.VMEM((width, width), F32)
     d_w_in, d_w_two = call(
         finish_feed_kernel, (shaped((width, width), F32),) * 2, [SMEM] + [VMEM] * 5, [held], limit=10, cost=4,
     )(info, *feed_all)
-    mix_own = later(mix_own, d_w_in)
     mix_rows = added(places, mix_own, rows)
+    mix_four = later(spread_chips(places, mix_rows), d_w_in)
     d_w_qkv, d_w_out = call(
         finish_mix_kernel, (shaped((wide, width), F32), shaped((192, width), F32)), [SMEM] + [VMEM] * 5, [held], limit=7, cost=3,
-    )(info, *spread_cores(places, spread_chips(places, mix_rows)))
+    )(info, *spread_cores(places, mix_four))
 
     ends = jnp.stack([part[rows:] for part in mix_own])
     ends = lax.dynamic_slice_in_dim(jnp.concatenate([ends, ends]), tensor - places.z, tensor, 0)

time: 317 us -> 306 us (0.965)
  waiting for transfers between devices: 118 us -> 114 us
  starting transfers between devices: 61.8 us -> 58.3 us
    ppermute x12, waiting for transfers between devices: 41.5 us -> 36.3 us  [turn(): lax.ppermute(value, 'tensor', [(k, (k + step) % size) for k in range(size)])]
    unnamed x107 -> x103, local copies, waits for them, and re-layouts: 12.8 us -> 10.5 us
  transfers between devices with their start and end apart: 54 -> 54, of which waited for: 29 -> 29; matrix products, arithmetic and copies ran while one was open for 1% -> 2% of each run, Pallas kernels for 27% -> 27%
where the time goes in v1:
time: 306 us; the launch traced here: 301 us
  waiting for transfers between devices  114 us (37%)
  Pallas kernels  103 us (34%)
  starting transfers between devices  58.3 us (19%)
  local copies, waits for them, and re-layouts  15.2 us (5%)
  between operations  6.99 us (2%)
    pallas_call x34, Pallas kernels, call(): pl.pallas_call(waiting_body, out_shape=outs, in_specs=list(specs) + [ANY]...  103 us
    ppermute x36, waiting for transfers between devices, swap(): return lax.ppermute(value, 'dp', [(d, d ^ mask) for d in range(self.dp)])  76.6 us
    ppermute x12, waiting for transfers between devices, turn(): lax.ppermute(value, 'tensor', [(k, (k + step) % size) for k in range(size)])  36.3 us
    ppermute x36, starting transfers between devices, swap(): return lax.ppermute(value, 'dp', [(d, d ^ mask) for d in range(self.dp)])  29 us
    ppermute x12, starting transfers between devices, turn(): lax.ppermute(value, 'tensor', [(k, (k + step) % size) for k in range(size)])  17.5 us
    ppermute x6, starting transfers between devices, onward(): return lax.ppermute(value, 'tensor', pairs)  11.8 us
    unnamed x103, local copies, waits for them, and re-layouts  10.5 us
  transfers between devices with their start and end apart: 54, of which 29 were waited for; matrix products, arithmetic and copies ran while one was open for 2% of the time, Pallas kernels for 27%

profile of v1, /device:TPU:0, one launch (start us, length us, event | category | flops | bytes accessed | tf_op | source)
XLA Modules:
  0.0 300.6 jit_solution(18249250183773430106)
XLA Ops:
  2.9 5.1 %collective-permute-start.2 = (bf16[104,768]{1,0:T(8,128)(2,1)S(1)}, bf16[104,768]{1,0:T(8,128)(2,1)S(1)}, u32[]{:S(2)}, u32[]{:S(2)}) collective-permute-start(bf16[104,768]{1,0:T(8,128)(2,1)S(1)} %pad_maximum_fusion.1.refs_0_), channel_id=1, source_target_pairs={{0,3},{1,0},{2,1},{3,2},{4,7},{5,4},{6,5},{7,6},{8,11},{9,8},{10,9... | collective-permute-start | bytes 479240 | tf_op jit(solution)/shard_map/ppermute | solution.py:63
  9.1 3.5 %collective-permute-done.2.refs_3_ = bf16[104,768]{1,0:T(8,128)(2,1)S(1)} collective-permute-done((bf16[104,768]{1,0:T(8,128)(2,1)S(1)}, bf16[104,768]{1,0:T(8,128)(2,1)S(1)}, u32[]{:S(2)}, u32[]{:S(2)}) %collective-permute-start.2) | collective-permute-done | bytes 159776 | tf_op jit(solution)/shard_map/ppermute | solution.py:63
  12.6 9.0 %collective-permute-done.1.refs_2_ = bf16[104,768]{1,0:T(8,128)(2,1)S(1)} collective-permute-done((bf16[104,768]{1,0:T(8,128)(2,1)S(1)}, bf16[104,768]{1,0:T(8,128)(2,1)S(1)}, u32[]{:S(2)}, u32[]{:S(2)}) %collective-permute-start.1) | collective-permute-done | bytes 159776 | tf_op jit(solution)/shard_map/ppermute | solution.py:63
  22.8 1.5 collective-permute-start.3
  24.3 1.5 collective-permute-start.4
  25.9 5.4 %collective-permute-done.3.refs_1_ = bf16[2,96,768]{2,1,0:T(8,128)(2,1)S(1)} collective-permute-done((bf16[2,96,768]{2,1,0:T(8,128)(2,1)S(1)}, bf16[2,96,768]{2,1,0:T(8,128)(2,1)S(1)}, u32[]{:S(2)}, u32[]{:S(2)}) %collective-permute-start.3) | collective-permute-done | bytes 294944 | tf_op jit(solution)/shard_map/ppermute | solution.py:59
  31.3 1.2 collective-permute-done.4.refs_3_
  32.6 1.6 collective-permute-start.5
  35.7 2.6 collective-permute-start.10
  38.7 7.5 %collective-permute-done.5.refs_0_.refs_5_ = bf16[2,2,96,768]{3,2,1,0:T(8,128)(2,1)S(1)} collective-permute-done((bf16[2,2,96,768]{3,2,1,0:T(8,128)(2,1)S(1)}, bf16[2,2,96,768]{3,2,1,0:T(8,128)(2,1)S(1)}, u32[]{:S(2)}, u32[]{:S(2)}) %collective-permute-start.5) | collective-permute-done | bytes 589856 | tf_op jit(solution)/shard_map/ppermute | solution.py:59
  46.2 1.3 collective-permute-done.6.refs_1_.refs_7_
  47.5 2.2 shard_map.257
  56.2 9.1 %collective-permute-done.11.refs_3_ = bf16[192,768]{1,0:T(8,128)(2,1)S(1)} collective-permute-done((bf16[192,768]{1,0:T(8,128)(2,1)S(1)}, bf16[192,768]{1,0:T(8,128)(2,1)S(1)}, u32[]{:S(2)}, u32[]{:S(2)}) %collective-permute-start.11) | collective-permute-done | bytes 294944 | tf_op jit(solution)/shard_map/ppermute | solution.py:63
  68.0 8.2 %shard_map.258 = (bf16[4,512,576]{2,1,0:T(8,128)(2,1)S(1)}, bf16[4,3,80,128]{3,2,1,0:T(8,128)(2,1)S(1)}, bf16[4,768,768]{2,1,0:T(8,128)(2,1)S(1)}) custom-call(s32[8]{0:T(128)S(1)} %stack.69.refs_0_, bf16[512,768]{1,0:T(8,128)(2,1)S(1)} %copy-done.14, f32[4,1,576]{2,1,0:T(1,128)S(1)} %copy-done.38, f32[512,128]{1,0:T(8,128)S(1)} %get-tuple-element.230.refs_3_.refs_9_, ...), custom_call_target="tpu_custom_call" | custom-call | flops 1840000000 | bytes 1 | tf_op jit(solution)/shard_map/pallas_call | solution.py:36
  76.2 4.1 %collective-permute-start.16 = (bf16[4,3,80,128]{3,2,1,0:T(8,128)(2,1)S(1)}, bf16[4,3,80,128]{3,2,1,0:T(8,128)(2,1)S(1)}, u32[]{:S(2)}, u32[]{:S(2)}) collective-permute-start(bf16[4,3,80,128]{3,2,1,0:T(8,128)(2,1)S(1)} %get-tuple-element.120.refs_4_), channel_id=1, source_target_pairs={{0,3},{4,7},{8,11},{12,15},{16,19},{20,23},{24,27},{28,31}} | collective-permute-start | bytes 737288 | tf_op jit(solution)/shard_map/ppermute | solution.py:68
  80.4 1.3 collective-permute-start.15
  81.7 2.5 collective-permute-start.14
  84.2 1.5 fusion
  85.9 1.6 collective-permute-start.17
  87.5 1.5 collective-permute-start.18
  89.0 5.2 %shard_map.261.refs_1_ = f32[4,3,512,128]{3,2,1,0:T(8,128)S(1)} custom-call(bf16[4,512,576]{2,1,0:T(8,128)(2,1)S(1)} %get-tuple-element.116.refs_0_.refs_5_.refs_4_.refs_1_, f32[512,512]{1,0:T(8,128)S(1)} %get-tuple-element.228.refs_1_.refs_2_, bf16[2,2,192,768]{3,2,1,0:T(8,128)(2,1)S(1)} %get-tuple-element.126.refs_2_.refs_0_.refs_7_.refs_4_.refs_6_, ...), custom_call_target="tpu_custom_call" | custom-call | flops 1610000000 | bytes 1 | tf_op jit(solution)/shard_map/pallas_call | solution.py:36
  94.2 1.5 collective-permute-done.14.refs_2_
  95.7 6.5 %shard_map.262 = (bf16[4,512,192]{2,1,0:T(8,128)(2,1)S(1)}, bf16[4,3,80,128]{3,2,1,0:T(8,128)(2,1)S(1)}, f32[4,512,128]{2,1,0:T(8,128)S(1)}, bf16[512,768]{1,0:T...) custom-call(s32[8]{0:T(128)S(1)} %stack.69.refs_0_, f32[4,3,512,128]{3,2,1,0:T(8,128)S(1)} %shard_map.261.refs_1_, ...), custom_call_target="tpu_custom_call" | custom-call | flops 23000000512 | bytes 1 | tf_op jit(solution)/shard_map/pallas_call | solution.py:36
  102.2 1.2 copy-done.19
  105.2 7.5 %collective-permute-done.17.refs_0_.refs_8_.refs_5_.refs_7_ = bf16[2,2,192,768]{3,2,1,0:T(8,128)(2,1)S(1)} collective-permute-done((bf16[2,2,192,768]{3,2,1,0:T(8,128)(2,1)S(1)}, bf16[2,2,192,768]{3,2,1,0:T(8,128)(2,1)S(1)}, u32[]{:S(2)}, u32[]{:S(2)}) %collective-permute-start.17) | collective-permute-done | bytes 1179680 | tf_op jit(solution)/shard_map/ppermute | solution.py:59
  112.7 1.2 collective-permute-done.18.refs_1_.refs_10_.refs_7_.refs_9_
  115.0 3.8 %collective-permute-done.20.refs_12_.refs_9_.refs_11_ = bf16[2,2,2,192,768]{4,3,2,1,0:T(8,128)(2,1)S(1)} collective-permute-done((bf16[2,2,2,192,768]{4,3,2,1,0:T(8,128)(2,1)S(1)}, bf16[2,2,2,192,768]{4,3,2,1,0:T(8,128)(2,1)S(1)}, u32[]{:S(2)}, u32[]{:S(2)}) %collective-permute-start.20) | collective-permute-done | bytes 2359328 | tf_op jit(solution)/shard_map/ppermute | solution.py:59
  118.7 3.4 %collective-permute-done.19.refs_11_.refs_8_.refs_10_ = bf16[2,2,2,192,768]{4,3,2,1,0:T(8,128)(2,1)S(1)} collective-permute-done((bf16[2,2,2,192,768]{4,3,2,1,0:T(8,128)(2,1)S(1)}, bf16[2,2,2,192,768]{4,3,2,1,0:T(8,128)(2,1)S(1)}, u32[]{:S(2)}, u32[]{:S(2)}) %collective-permute-start.19) | collective-permute-done | bytes 2359328 | tf_op jit(solution)/shard_map/ppermute | solution.py:59
  122.1 15.8 %shard_map.265 = (bf16[4,512,768]{2,1,0:T(8,128)(2,1)S(1)}, bf16[512,768]{1,0:T(8,128)(2,1)}, bf16[512,768]{1,0:T(8,128)(2,1)S(1)}, f32[512,768]{1,0:T(8,128)S(1...) custom-call(s32[8]{0:T(128)S(1)} %stack.69.refs_0_, ...), custom_call_target="tpu_custom_call" | custom-call | flops 4369999872 | bytes 1 | tf_op jit(solution)/shard_map/pallas_call | solution.py:36
  139.8 1.3 copy-done.3
  141.1 1.7 copy-done.8
  142.7 8.1 %shard_map.266 = (bf16[4,512,768]{2,1,0:T(8,128)(2,1)S(1)}, f32[4,8,768]{2,1,0:T(8,128)S(1)}, bf16[384,3072]{1,0:T(8,128)(2,1)S(1)}, bf16[384,3072]{1,0:T(8,128)(2,1)S(1)}) custom-call(s32[8]{0:T(128)S(1)} %stack.69.refs_0_, bf16[512,768]{1,0:T(8,128)(2,1)S(1)} %get-tuple-element.124.refs_1_, bf16[512,768]{1,0:T(8,128)(2,1)S(1)} %get-tuple-element.131.refs_2_, ...), custom_call_target="tpu_custom_call" | custom-call | flops 3220000000 | bytes 1 | tf_op jit(solution)/shard_map/pallas_call | solution.py:36
  151.9 1.5 collective-permute-start.23
  154.1 5.8 %shard_map.268 = (f32[512,768]{1,0:T(8,128)S(1)}, bf16[512,768]{1,0:T(8,128)(2,1)S(1)}, f32[8,768]{1,0:T(8,128)S(1)}) custom-call(s32[8]{0:T(128)S(1)} %stack.69.refs_0_, bf16[4,512,768]{2,1,0:T(8,128)(2,1)S(1)} %get-tuple-element.133.refs_1_, f32[512,768]{1,0:T(8,128)S(1)} %copy-done.22, f32[512,768]{1,0:T(8,128)S(1)} %copy-done.20, ...), custom_call_target="tpu_custom_call" | custom-call | flops 2530000128 | bytes 1 | tf_op jit(solution)/shard_map/pallas_call | solution.py:36
  159.9 7.4 %collective-permute-done.23.refs_2_ = bf16[192,1536]{1,0:T(8,128)(2,1)S(1)} collective-permute-done((bf16[192,1536]{1,0:T(8,128)(2,1)S(1)}, bf16[192,1536]{1,0:T(8,128)(2,1)S(1)}, u32[]{:S(2)}, u32[]{:S(2)}) %collective-permute-start.23) | collective-permute-done | bytes 589856 | tf_op jit(solution)/shard_map/ppermute | solution.py:59
  167.3 1.1 collective-permute-done.24.refs_3_
  170.4 1.5 collective-permute-start.27
  171.9 1.4 collective-permute-start.28
  173.4 10.7 %shard_map.271 = (bf16[4,3,512,128]{3,2,1,0:T(8,128)(2,1)S(1)}, bf16[4,3,80,128]{3,2,1,0:T(8,128)(2,1)S(1)}) custom-call(bf16[512,768]{1,0:T(8,128)(2,1)S(1)} %get-tuple-element.142.refs_4_.refs_0_.refs_12_, bf16[4,768,768]{2,1,0:T(8,128)(2,1)S(1)} %get-tuple-element.123.refs_8_.refs_1_.refs_2_, bf16[4,512,192]{2,1,0:T(8,128)(2,1)S(1)} %copy-done.6, ...), custom_call_target="tpu_custom_call" | custom-call | flops 2530000128 | bytes 1 | tf_op jit(solution)/shard_map/pallas_call | solution.py:36
  184.1 1.3 collective-permute-start.31
  185.4 4.8 %collective-permute-done.27.refs_2_ = bf16[96,1536]{1,0:T(8,128)(2,1)S(1)} collective-permute-done((bf16[96,1536]{1,0:T(8,128)(2,1)S(1)}, bf16[96,1536]{1,0:T(8,128)(2,1)S(1)}, u32[]{:S(2)}, u32[]{:S(2)}) %collective-permute-start.27) | collective-permute-done | bytes 294944 | tf_op jit(solution)/shard_map/ppermute | solution.py:59
  190.2 1.3 collective-permute-start.30
  191.5 1.3 collective-permute-start.29
  193.8 1.4 collective-permute-start.33
  195.2 11.3 %shard_map.274.refs_6_.refs_2_ = f32[4,512,576]{2,1,0:T(8,128)S(1)} custom-call(bf16[4,512,576]{2,1,0:T(8,128)(2,1)S(1)} %get-tuple-element.116.refs_0_.refs_5_.refs_4_.refs_1_, bf16[4,3,512,128]{3,2,1,0:T(8,128)(2,1)S(1)} %get-tuple-element.152.refs_1_.refs_3_, f32[512,512]{1,0:T(8,128)S(1)} %copy-done.13, f32[512,512]{1,0:T(8,128)S(1)} %copy-done.25, ...), custom_call_target="tpu_custom_call" | custom-call | flops 3450000128 | bytes 1 | tf_op jit(solution)/shard_map/pallas_call | solution.py:36
  206.8 5.7 %collective-permute-start.35 = (bf16[192,768]{1,0:T(8,128)(2,1)S(1)}, bf16[192,768]{1,0:T(8,128)(2,1)S(1)}, u32[]{:S(2)}, u32[]{:S(2)}) collective-permute-start(bf16[192,768]{1,0:T(8,128)(2,1)S(1)} %get-tuple-element.166.refs_14_), channel_id=1, source_target_pairs={{0,3},{1,0},{2,1},{3,2},{4,7},{5,4},{6,5},{7,6},{8,11},{9,8},{10,9... | collective-permute-start | bytes 884744 | tf_op jit(solution)/shard_map/ppermute | solution.py:63
  213.1 7.0 %shard_map.276 = (bf16[2,512,768]{2,1,0:T(8,128)(2,1)S(1)}, f32[2,8,768]{2,1,0:T(8,128)S(1)}, bf16[384,1536]{1,0:T(8,128)(2,1)S(1)}, bf16[384,1536]{1,0:T(8,128)(2,1)S(1)}) custom-call(s32[8]{0:T(128)S(1)} %stack.69.refs_0_, bf16[4,512,576]{2,1,0:T(8,128)(2,1)S(1)} %get-tuple-element.116.refs_0_.refs_5_.refs_4_.refs_1_, ...), custom_call_target="tpu_custom_call" | custom-call | flops 2530000128 | bytes 1 | tf_op jit(solution)/shard_map/pallas_call | solution.py:36
  220.1 7.4 %shard_map.277 = (bf16[2,512,768]{2,1,0:T(8,128)(2,1)S(1)}, f32[2,8,768]{2,1,0:T(8,128)}, bf16[384,1536]{1,0:T(8,128)(2,1)S(1)}, bf16[392,1536]{1,0:T(8,128)(2,1)S(1)}, bf16[16,768]{1,0:T(8,128)(2,1)S(1)}) custom-call(s32[8]{0:T(128)S(1)} %stack.69.refs_0_, bf16[4,512,576]{2,1,0:T(8,128)(2,1)S(1)} %get-tuple-element.116.refs_0_.refs_5_.refs_4_.refs_1_, ...), custom_call_target="tpu_custom_call" | custom-call | flops 2530000128 | bytes 1 | tf_op jit(solution)/shard_map/pallas_call | solution.py:36
  227.6 10.4 %collective-permute-done.36.refs_2_ = bf16[192,768]{1,0:T(8,128)(2,1)S(1)} collective-permute-done((bf16[192,768]{1,0:T(8,128)(2,1)S(1)}, bf16[192,768]{1,0:T(8,128)(2,1)S(1)}, u32[]{:S(2)}, u32[]{:S(2)}) %collective-permute-start.36) | collective-permute-done | bytes 294944 | tf_op jit(solution)/shard_map/ppermute | solution.py:63
  238.7 4.1 %collective-permute-done.34.refs_1_ = bf16[384,1536]{1,0:T(8,128)(2,1)S(1)} collective-permute-done((bf16[384,1536]{1,0:T(8,128)(2,1)S(1)}, bf16[384,1536]{1,0:T(8,128)(2,1)S(1)}, u32[]{:S(2)}, u32[]{:S(2)}) %collective-permute-start.34) | collective-permute-done | bytes 1179680 | tf_op jit(solution)/shard_map/ppermute | solution.py:59
  243.9 3.5 %shard_map.280.refs_5_ = bf16[512,768]{1,0:T(8,128)(2,1)} custom-call(bf16[2,512,768]{2,1,0:T(8,128)(2,1)S(1)} %get-tuple-element.169.refs_0_, bf16[2,512,768]{2,1,0:T(8,128)(2,1)S(1)} %get-tuple-element.174.refs_4_.refs_1_, bf16[4,768,768]{2,1,0:T(8,128)(2,1)S(1)} %get-tuple-element.123.refs_8_.refs_1_.refs_2_, f32[512,768]{1,0:T(8,128)S(1)} %get-tuple-element.175.refs_3_, ...), custom_call_target="tpu_custom_call" | custom-call | flops 1380000000 | bytes 1 | tf_op jit(solution)/shard_map/pallas_call | solution.py:36
  247.4 11.6 %collective-permute-done.39.refs_2_ = bf16[384,768]{1,0:T(8,128)(2,1)S(1)} collective-permute-done((bf16[384,768]{1,0:T(8,128)(2,1)S(1)}, bf16[384,768]{1,0:T(8,128)(2,1)S(1)}, u32[]{:S(2)}, u32[]{:S(2)}) %collective-permute-start.39) | collective-permute-done | bytes 589856 | tf_op jit(solution)/shard_map/ppermute | solution.py:59
  260.7 1.4 collective-permute-start.41
  262.8 1.9 collective-permute-start.49
  264.7 6.0 %collective-permute-done.41.refs_2_ = bf16[192,768]{1,0:T(8,128)(2,1)S(1)} collective-permute-done((bf16[192,768]{1,0:T(8,128)(2,1)S(1)}, bf16[192,768]{1,0:T(8,128)(2,1)S(1)}, u32[]{:S(2)}, u32[]{:S(2)}) %collective-permute-start.41) | collective-permute-done | bytes 294944 | tf_op jit(solution)/shard_map/ppermute | solution.py:59
  271.3 4.0 %collective-permute-done.50.refs_2_.refs_3_ = bf16[192,768]{1,0:T(8,128)(2,1)S(1)} collective-permute-done((bf16[192,768]{1,0:T(8,128)(2,1)S(1)}, bf16[192,768]{1,0:T(8,128)(2,1)S(1)}, u32[]{:S(2)}, u32[]{:S(2)}) %collective-permute-start.50) | collective-permute-done | bytes 294944 | tf_op jit(solution)/shard_map/ppermute | solution.py:59
  276.6 1.2 collective-permute-start.51
  277.8 1.2 collective-permute-start.44
  279.0 1.2 collective-permute-start.45
  280.2 3.1 %collective-permute-done.51.refs_3_.refs_4_ = bf16[192,768]{1,0:T(8,128)(2,1)S(1)} collective-permute-done((bf16[192,768]{1,0:T(8,128)(2,1)S(1)}, bf16[192,768]{1,0:T(8,128)(2,1)S(1)}, u32[]{:S(2)}, u32[]{:S(2)}) %collective-permute-start.51) | collective-permute-done | bytes 294944 | tf_op jit(solution)/shard_map/ppermute | solution.py:59
  283.5 3.4 %collective-permute-done.44.refs_2_ = bf16[104,768]{1,0:T(8,128)(2,1)S(1)} collective-permute-done((bf16[104,768]{1,0:T(8,128)(2,1)S(1)}, bf16[104,768]{1,0:T(8,128)(2,1)S(1)}, u32[]{:S(2)}, u32[]{:S(2)}) %collective-permute-start.44) | collective-permute-done | bytes 159776 | tf_op jit(solution)/shard_map/ppermute | solution.py:63
  286.9 1.8 collective-permute-start.48
  290.5 3.6 %shard_map.285 = (f32[768,768]{1,0:T(8,128)}, f32[768,768]{1,0:T(8,128)}) custom-call(s32[8]{0:T(128)S(1)} %stack.69.refs_0_, bf16[192,768]{1,0:T(8,128)(2,1)S(1)} %shard_map.278.refs_0_.refs_1_, bf16[192,768]{1,0:T(8,128)(2,1)S(1)} %collective-permute-done.49.refs_1_.refs_2_, bf16[192,768]{1,0:T(8,128)(2,1)S(1)} %collective-permute-done.50.refs_2_.refs_3_, ...), custom_call_target="tpu_custom_call" | custom-call | flops 920000000 | bytes 1 | tf_op jit(solution)/shard_map/pallas_call | solution.py:36
  297.6 2.8 shard_map.287
  (213 shorter events, 32.2 us)
Async XLA Ops:
  2.9 9.7 %collective-permute-start.2 = (bf16[104,768]{1,0:T(8,128)(2,1)S(1)}, bf16[104,768]{1,0:T(8,128)(2,1)S(1)}, u32[]{:S(2)}, u32[]{:S(2)}) collective-permute-start(bf16[104,768]{1,0:T(8,128)(2,1)S(1)} %pad_maximum_fusion.1.refs_0_), channel_id=1, source_target_pairs={{0,3},{1,0},{2,1},{3,2},{4,7},{5,4},{6,5},{7,6},{8,11},{9,8},{10,9... | collective-permute-start | bytes 479240 | tf_op jit(solution)/shard_map/ppermute | solution.py:63
  8.0 13.5 %collective-permute-start.1 = (bf16[104,768]{1,0:T(8,128)(2,1)S(1)}, bf16[104,768]{1,0:T(8,128)(2,1)S(1)}, u32[]{:S(2)}, u32[]{:S(2)}) collective-permute-start(bf16[104,768]{1,0:T(8,128)(2,1)S(1)} %pad_maximum_fusion.1.refs_0_), channel_id=1, source_target_pairs={{0,2},{1,3},{2,0},{3,1},{4,6},{5,7},{6,4},{7,5},{8,10},{9,11},{10,... | collective-permute-start | bytes 479240 | tf_op jit(solution)/shard_map/ppermute | solution.py:63
  8.1 13.5 %collective-permute-start = (bf16[104,768]{1,0:T(8,128)(2,1)S(1)}, bf16[104,768]{1,0:T(8,128)(2,1)S(1)}, u32[]{:S(2)}, u32[]{:S(2)}) collective-permute-start(bf16[104,768]{1,0:T(8,128)(2,1)S(1)} %pad_maximum_fusion.1.refs_0_), channel_id=1, source_target_pairs={{0,1},{1,2},{2,3},{3,0},{4,5},{5,6},{6,7},{7,4},{8,9},{9,10},{10,1... | collective-permute-start | bytes 479240 | tf_op jit(solution)/shard_map/ppermute | solution.py:63
  22.8 15.5 %copy-start.41 = (s32[1,8]{1,0:T(1,128)S(1)}, s32[1,8]{1,0:T(1,128)}, u32[]{:S(2)}) copy-start(s32[1,8]{1,0:T(1,128)} %param.16) | copy-start | bytes 100
  22.8 8.4 %collective-permute-start.3 = (bf16[2,96,768]{2,1,0:T(8,128)(2,1)S(1)}, bf16[2,96,768]{2,1,0:T(8,128)(2,1)S(1)}, u32[]{:S(2)}, u32[]{:S(2)}) collective-permute-start(bf16[2,96,768]{2,1,0:T(8,128)(2,1)S(1)} %get-tuple-element.112.refs_0_), channel_id=1, source_target_pairs={{0,8},{4,12},{8,0},{12,4},{16,24},{20,28},{24,16},{28,20},{1,9},{5... | collective-permute-start | bytes 884744 | tf_op jit(solution)/shard_map/ppermute | solution.py:59
  24.3 8.2 %collective-permute-start.4 = (bf16[2,96,768]{2,1,0:T(8,128)(2,1)S(1)}, bf16[2,96,768]{2,1,0:T(8,128)(2,1)S(1)}, u32[]{:S(2)}, u32[]{:S(2)}) collective-permute-start(bf16[2,96,768]{2,1,0:T(8,128)(2,1)S(1)} %get-tuple-element.113.refs_2_), channel_id=1, source_target_pairs={{0,16},{4,20},{8,24},{12,28},{16,0},{20,4},{24,8},{28,12},{1,17},{... | collective-permute-start | bytes 884744 | tf_op jit(solution)/shard_map/ppermute | solution.py:59
  32.6 13.6 %collective-permute-start.5 = (bf16[2,2,96,768]{3,2,1,0:T(8,128)(2,1)S(1)}, bf16[2,2,96,768]{3,2,1,0:T(8,128)(2,1)S(1)}, u32[]{:S(2)}, u32[]{:S(2)}) collective-permute-start(bf16[2,2,96,768]{3,2,1,0:T(8,128)(2,1)S(1)} %get-tuple-element.114.refs_0_.refs_4_), channel_id=1, source_target_pairs={{0,16},{4,20},{8,24},{12,28},{16,0},{20,4},{24,8},{28,12},{1,17},{... | collective-permute-start | bytes 1769480 | tf_op jit(solution)/shard_map/ppermute | solution.py:59
  34.2 13.4 %collective-permute-start.6 = (bf16[2,2,96,768]{3,2,1,0:T(8,128)(2,1)S(1)}, bf16[2,2,96,768]{3,2,1,0:T(8,128)(2,1)}, u32[]{:S(2)}, u32[]{:S(2)}) collective-permute-start(bf16[2,2,96,768]{3,2,1,0:T(8,128)(2,1)S(1)} %get-tuple-element.115.refs_1_.refs_6_.refs_5_), channel_id=1, source_target_pairs={{0,8},{4,12},{8,0},{12,4},{16,24},{20,28},{24,16},{28,20},{1,9},{5... | collective-permute-start | bytes 1769480 | tf_op jit(solution)/shard_map/ppermute | solution.py:59
  35.7 20.3 %collective-permute-start.10 = (bf16[192,768]{1,0:T(8,128)(2,1)S(1)}, bf16[192,768]{1,0:T(8,128)(2,1)S(1)}, u32[]{:S(2)}, u32[]{:S(2)}) collective-permute-start(bf16[192,768]{1,0:T(8,128)(2,1)S(1)} %pad_maximum_fusion.refs_0_), channel_id=1, source_target_pairs={{0,2},{1,3},{2,0},{3,1},{4,6},{5,7},{6,4},{7,5},{8,10},{9,11},{10,... | collective-permute-start | bytes 884744 | tf_op jit(solution)/shard_map/ppermute | solution.py:63
  38.3 17.7 %collective-permute-start.9 = (bf16[192,768]{1,0:T(8,128)(2,1)S(1)}, bf16[192,768]{1,0:T(8,128)(2,1)}, u32[]{:S(2)}, u32[]{:S(2)}) collective-permute-start(bf16[192,768]{1,0:T(8,128)(2,1)S(1)} %pad_maximum_fusion.refs_0_), channel_id=1, source_target_pairs={{0,1},{1,2},{2,3},{3,0},{4,5},{5,6},{6,7},{7,4},{8,9},{9,10},{10,1... | collective-permute-start | bytes 884744 | tf_op jit(solution)/shard_map/ppermute | solution.py:63
  38.6 29.3 %collective-permute-start.7 = (bf16[2,2,2,96,768]{4,3,2,1,0:T(8,128)(2,1)S(1)}, bf16[2,2,2,96,768]{4,3,2,1,0:T(8,128)(2,1)}, u32[]{:S(2)}, u32[]{:S(2)}) collective-permute-start(bf16[2,2,2,96,768]{4,3,2,1,0:T(8,128)(2,1)S(1)} %shard_map.256), channel_id=1, source_target_pairs={{0,4},{4,0},{8,12},{12,8},{16,20},{20,16},{24,28},{28,24},{1,5},{5... | collective-permute-start | bytes 3538952 | tf_op jit(solution)/shard_map/ppermute | solution.py:59
  49.7 18.2 %collective-permute-start.8 = (bf16[2,2,2,96,768]{4,3,2,1,0:T(8,128)(2,1)}, bf16[2,2,2,96,768]{4,3,2,1,0:T(8,128)(2,1)}, u32[]{:S(2)}, u32[]{:S(2)}) collective-permute-start(bf16[2,2,2,96,768]{4,3,2,1,0:T(8,128)(2,1)} %shard_map.257), channel_id=1, source_target_pairs={{0,4},{4,0},{8,12},{12,8},{16,20},{20,16},{24,28},{28,24},{1,5},{5... | collective-permute-start | bytes 3538952 | tf_op jit(solution)/shard_map/ppermute | solution.py:59
  56.0 9.4 %collective-permute-start.11 = (bf16[192,768]{1,0:T(8,128)(2,1)S(1)}, bf16[192,768]{1,0:T(8,128)(2,1)S(1)}, u32[]{:S(2)}, u32[]{:S(2)}) collective-permute-start(bf16[192,768]{1,0:T(8,128)(2,1)S(1)} %pad_maximum_fusion.refs_0_), channel_id=1, source_target_pairs={{0,3},{1,0},{2,1},{3,2},{4,7},{5,4},{6,5},{7,6},{8,11},{9,8},{10,9... | collective-permute-start | bytes 884744 | tf_op jit(solution)/shard_map/ppermute | solution.py:63
  56.0 11.9 %copy-start.14 = (bf16[512,768]{1,0:T(8,128)(2,1)S(1)}, bf16[512,768]{1,0:T(8,128)(2,1)}, u32[]{:S(2)}) copy-start(bf16[512,768]{1,0:T(8,128)(2,1)} %refs_10_.3) | copy-start | bytes 2359300
  56.0 11.9 %copy-start.29 = (bf16[2,2,96,768]{3,2,1,0:T(8,128)(2,1)S(1)}, bf16[2,2,96,768]{3,2,1,0:T(8,128)(2,1)}, u32[]{:S(2)}) copy-start(bf16[2,2,96,768]{3,2,1,0:T(8,128)(2,1)} %copy-done.28) | copy-start | bytes 1769476
  56.0 11.9 %copy-start.38 = (f32[4,1,576]{2,1,0:T(1,128)S(1)}, f32[4,1,576]{2,1,0:T(1,128)}, u32[]{:S(2)}) copy-start(f32[4,1,576]{2,1,0:T(1,128)} %copy-done.37) | copy-start | bytes 27652
  66.4 19.3 %collective-permute-start.12 = (bf16[2,192,768]{2,1,0:T(8,128)(2,1)S(1)}, bf16[2,192,768]{2,1,0:T(8,128)(2,1)S(1)}, u32[]{:S(2)}, u32[]{:S(2)}) collective-permute-start(bf16[2,192,768]{2,1,0:T(8,128)(2,1)S(1)} %get-tuple-element.118.refs_0_), channel_id=1, source_target_pairs={{0,8},{4,12},{8,0},{12,4},{16,24},{20,28},{24,16},{28,20},{1,9},{5... | collective-permute-start | bytes 1769480 | tf_op jit(solution)/shard_map/ppermute | solution.py:59
  67.1 18.7 %collective-permute-start.13 = (bf16[2,192,768]{2,1,0:T(8,128)(2,1)S(1)}, bf16[2,192,768]{2,1,0:T(8,128)(2,1)S(1)}, u32[]{:S(2)}, u32[]{:S(2)}) collective-permute-start(bf16[2,192,768]{2,1,0:T(8,128)(2,1)S(1)} %get-tuple-element.119.refs_2_), channel_id=1, source_target_pairs={{0,16},{4,20},{8,24},{12,28},{16,0},{20,4},{24,8},{28,12},{1,17},{... | collective-permute-start | bytes 1769480 | tf_op jit(solution)/shard_map/ppermute | solution.py:59
  68.0 16.2 %copy-start.40 = (s32[512]{0:T(512)S(1)}, s32[512]{0:T(512)}, u32[]{:S(2)}) copy-start(s32[512]{0:T(512)} %copy-done.39) | copy-start | bytes 6148
  76.2 9.5 %copy-start.44 = (bf16[768]{0:T(1024)(128)(2,1)S(1)}, bf16[768]{0:T(1024)(128)(2,1)}, u32[]{:S(2)}) copy-start(bf16[768]{0:T(1024)(128)(2,1)} %param.22) | copy-start | bytes 4612
  76.2 17.9 %collective-permute-start.16 = (bf16[4,3,80,128]{3,2,1,0:T(8,128)(2,1)S(1)}, bf16[4,3,80,128]{3,2,1,0:T(8,128)(2,1)S(1)}, u32[]{:S(2)}, u32[]{:S(2)}) collective-permute-start(bf16[4,3,80,128]{3,2,1,0:T(8,128)(2,1)S(1)} %get-tuple-element.120.refs_4_), channel_id=1, source_target_pairs={{0,3},{4,7},{8,11},{12,15},{16,19},{20,23},{24,27},{28,31}} | collective-permute-start | bytes 737288 | tf_op jit(solution)/shard_map/ppermute | solution.py:68
  80.4 13.8 %collective-permute-start.15 = (bf16[4,3,80,128]{3,2,1,0:T(8,128)(2,1)S(1)}, bf16[4,3,80,128]{3,2,1,0:T(8,128)(2,1)S(1)}, u32[]{:S(2)}, u32[]{:S(2)}) collective-permute-start(bf16[4,3,80,128]{3,2,1,0:T(8,128)(2,1)S(1)} %get-tuple-element.120.refs_4_), channel_id=1, source_target_pairs={{0,2},{1,3},{4,6},{5,7},{8,10},{9,11},{12,14},{13,15},{16,18},{17,... | collective-permute-start | bytes 737288 | tf_op jit(solution)/shard_map/ppermute | solution.py:68
  81.7 14.0 %collective-permute-start.14 = (bf16[4,3,80,128]{3,2,1,0:T(8,128)(2,1)S(1)}, bf16[4,3,80,128]{3,2,1,0:T(8,128)(2,1)S(1)}, u32[]{:S(2)}, u32[]{:S(2)}) collective-permute-start(bf16[4,3,80,128]{3,2,1,0:T(8,128)(2,1)S(1)} %get-tuple-element.120.refs_4_), channel_id=1, source_target_pairs={{0,1},{1,2},{2,3},{4,5},{5,6},{6,7},{8,9},{9,10},{10,11},{12,13},{... | collective-permute-start | bytes 737288 | tf_op jit(solution)/shard_map/ppermute | solution.py:68
  85.9 26.8 %collective-permute-start.17 = (bf16[2,2,192,768]{3,2,1,0:T(8,128)(2,1)S(1)}, bf16[2,2,192,768]{3,2,1,0:T(8,128)(2,1)S(1)}, u32[]{:S(2)}, u32[]{:S(2)}) collective-permute-start(bf16[2,2,192,768]{3,2,1,0:T(8,128)(2,1)S(1)} %get-tuple-element.126.refs_2_.refs_0_.refs_7_.refs_4_.refs_6_), channel_id=1, source_target_pairs={{0,16},{4,20},{8,24},{12,28},{16,0},{20,4},{24,8},{28,12},{1,17},{... | collective-permute-start | bytes 3538952 | tf_op jit(solution)/shard_map/ppermute | solution.py:59
  87.5 26.4 %collective-permute-start.18 = (bf16[2,2,192,768]{3,2,1,0:T(8,128)(2,1)S(1)}, bf16[2,2,192,768]{3,2,1,0:T(8,128)(2,1)S(1)}, u32[]{:S(2)}, u32[]{:S(2)}) collective-permute-start(bf16[2,2,192,768]{3,2,1,0:T(8,128)(2,1)S(1)} %get-tuple-element.128.refs_3_.refs_1_.refs_9_.refs_6_.refs_8_), channel_id=1, source_target_pairs={{0,8},{4,12},{8,0},{12,4},{16,24},{20,28},{24,16},{28,20},{1,9},{5... | collective-permute-start | bytes 3538952 | tf_op jit(solution)/shard_map/ppermute | solution.py:59
  114.1 4.6 %collective-permute-start.20 = (bf16[2,2,2,192,768]{4,3,2,1,0:T(8,128)(2,1)S(1)}, bf16[2,2,2,192,768]{4,3,2,1,0:T(8,128)(2,1)S(1)}, u32[]{:S(2)}, u32[]{:S(2)}) collective-permute-start(bf16[2,2,2,192,768]{4,3,2,1,0:T(8,128)(2,1)S(1)} %shard_map.264), channel_id=1, source_target_pairs={{0,4},{4,0},{8,12},{12,8},{16,20},{20,16},{24,28},{28,24},{1,5},{5... | collective-permute-start | bytes 7077896 | tf_op jit(solution)/shard_map/ppermute | solution.py:59
  114.4 7.7 %collective-permute-start.19 = (bf16[2,2,2,192,768]{4,3,2,1,0:T(8,128)(2,1)S(1)}, bf16[2,2,2,192,768]{4,3,2,1,0:T(8,128)(2,1)S(1)}, u32[]{:S(2)}, u32[]{:S(2)}) collective-permute-start(bf16[2,2,2,192,768]{4,3,2,1,0:T(8,128)(2,1)S(1)} %shard_map.263), channel_id=1, source_target_pairs={{0,4},{4,0},{8,12},{12,8},{16,20},{20,16},{24,28},{28,24},{1,5},{5... | collective-permute-start | bytes 7077896 | tf_op jit(solution)/shard_map/ppermute | solution.py:59
  118.7 19.1 %copy-start.7 = (bf16[2,2,2,192,768]{4,3,2,1,0:T(8,128)(2,1)}, bf16[2,2,2,192,768]{4,3,2,1,0:T(8,128)(2,1)S(1)}, u32[]{:S(2)}) copy-start(bf16[2,2,2,192,768]{4,3,2,1,0:T(8,128)(2,1)S(1)} %collective-permute-done.20.refs_12_.refs_9_.refs_11_) | copy-start | bytes 7077892
  122.1 17.7 %copy-start.10 = (bf16[2,2,2,192,768]{4,3,2,1,0:T(8,128)(2,1)}, bf16[2,2,2,192,768]{4,3,2,1,0:T(8,128)(2,1)S(1)}, u32[]{:S(2)}) copy-start(bf16[2,2,2,192,768]{4,3,2,1,0:T(8,128)(2,1)S(1)} %collective-permute-done.19.refs_11_.refs_8_.refs_10_) | copy-start | bytes 7077892
  139.7 11.7 %collective-permute-start.21 = (bf16[384,3072]{1,0:T(8,128)(2,1)}, bf16[384,3072]{1,0:T(8,128)(2,1)S(1)}, u32[]{:S(2)}, u32[]{:S(2)}) collective-permute-start(bf16[384,3072]{1,0:T(8,128)(2,1)} %get-tuple-element.138), channel_id=1, source_target_pairs={{0,4},{4,0},{8,12},{12,8},{16,20},{20,16},{24,28},{28,24},{1,5},{5... | collective-permute-start | bytes 7077896 | tf_op jit(solution)/shard_map/ppermute | solution.py:59
  142.7 11.2 %copy-start.20 = (f32[512,768]{1,0:T(8,128)S(1)}, f32[512,768]{1,0:T(8,128)}, u32[]{:S(2)}) copy-start(f32[512,768]{1,0:T(8,128)} %copy-done.19) | copy-start | bytes 4718596
  142.7 11.2 %copy-start.22 = (f32[512,768]{1,0:T(8,128)S(1)}, f32[512,768]{1,0:T(8,128)}, u32[]{:S(2)}) copy-start(f32[512,768]{1,0:T(8,128)} %copy-done.21) | copy-start | bytes 4718596
  150.9 17.8 %collective-permute-start.22 = (bf16[384,3072]{1,0:T(8,128)(2,1)S(1)}, bf16[384,3072]{1,0:T(8,128)(2,1)S(1)}, u32[]{:S(2)}, u32[]{:S(2)}) collective-permute-start(bf16[384,3072]{1,0:T(8,128)(2,1)S(1)} %get-tuple-element.139.refs_2_), channel_id=1, source_target_pairs={{0,4},{4,0},{8,12},{12,8},{16,20},{20,16},{24,28},{28,24},{1,5},{5... | collective-permute-start | bytes 7077896 | tf_op jit(solution)/shard_map/ppermute | solution.py:59
  151.9 15.4 %collective-permute-start.23 = (bf16[192,1536]{1,0:T(8,128)(2,1)S(1)}, bf16[192,1536]{1,0:T(8,128)(2,1)S(1)}, u32[]{:S(2)}, u32[]{:S(2)}) collective-permute-start(bf16[192,1536]{1,0:T(8,128)(2,1)S(1)} %get-tuple-element.140.refs_12_), channel_id=1, source_target_pairs={{0,8},{4,12},{8,0},{12,4},{16,24},{20,28},{24,16},{28,20},{1,9},{5... | collective-permute-start | bytes 1769480 | tf_op jit(solution)/shard_map/ppermute | solution.py:59
  153.4 15.1 %collective-permute-start.24 = (bf16[192,1536]{1,0:T(8,128)(2,1)S(1)}, bf16[192,1536]{1,0:T(8,128)(2,1)S(1)}, u32[]{:S(2)}, u32[]{:S(2)}) collective-permute-start(bf16[192,1536]{1,0:T(8,128)(2,1)S(1)} %get-tuple-element.141.refs_13_), channel_id=1, source_target_pairs={{0,16},{4,20},{8,24},{12,28},{16,0},{20,4},{24,8},{28,12},{1,17},{... | collective-permute-start | bytes 1769480 | tf_op jit(solution)/shard_map/ppermute | solution.py:59
  169.3 23.6 %collective-permute-start.25 = (bf16[192,1536]{1,0:T(8,128)(2,1)S(1)}, bf16[192,1536]{1,0:T(8,128)(2,1)S(1)}, u32[]{:S(2)}, u32[]{:S(2)}) collective-permute-start(bf16[192,1536]{1,0:T(8,128)(2,1)S(1)} %get-tuple-element.150.refs_6_), channel_id=1, source_target_pairs={{0,8},{4,12},{8,0},{12,4},{16,24},{20,28},{24,16},{28,20},{1,9},{5... | collective-permute-start | bytes 1769480 | tf_op jit(solution)/shard_map/ppermute | solution.py:59
  169.9 23.0 %collective-permute-start.26 = (bf16[192,1536]{1,0:T(8,128)(2,1)S(1)}, bf16[192,1536]{1,0:T(8,128)(2,1)S(1)}, u32[]{:S(2)}, u32[]{:S(2)}) collective-permute-start(bf16[192,1536]{1,0:T(8,128)(2,1)S(1)} %get-tuple-element.151.refs_7_), channel_id=1, source_target_pairs={{0,16},{4,20},{8,24},{12,28},{16,0},{20,4},{24,8},{28,12},{1,17},{... | collective-permute-start | bytes 1769480 | tf_op jit(solution)/shard_map/ppermute | solution.py:59
  170.4 19.8 %collective-permute-start.27 = (bf16[96,1536]{1,0:T(8,128)(2,1)S(1)}, bf16[96,1536]{1,0:T(8,128)(2,1)S(1)}, u32[]{:S(2)}, u32[]{:S(2)}) collective-permute-start(bf16[96,1536]{1,0:T(8,128)(2,1)S(1)} %get-tuple-element.148.refs_2_), channel_id=1, source_target_pairs={{0,16},{4,20},{8,24},{12,28},{16,0},{20,4},{24,8},{28,12},{1,17},{... | collective-permute-start | bytes 884744 | tf_op jit(solution)/shard_map/ppermute | solution.py:59
  171.9 19.5 %collective-permute-start.28 = (bf16[96,1536]{1,0:T(8,128)(2,1)S(1)}, bf16[96,1536]{1,0:T(8,128)(2,1)S(1)}, u32[]{:S(2)}, u32[]{:S(2)}) collective-permute-start(bf16[96,1536]{1,0:T(8,128)(2,1)S(1)} %get-tuple-element.149.refs_3_), channel_id=1, source_target_pairs={{0,8},{4,12},{8,0},{12,4},{16,24},{20,28},{24,16},{28,20},{1,9},{5... | collective-permute-start | bytes 884744 | tf_op jit(solution)/shard_map/ppermute | solution.py:59
  184.1 22.4 %collective-permute-start.31 = (bf16[4,3,80,128]{3,2,1,0:T(8,128)(2,1)S(1)}, bf16[4,3,80,128]{3,2,1,0:T(8,128)(2,1)S(1)}, u32[]{:S(2)}, u32[]{:S(2)}) collective-permute-start(bf16[4,3,80,128]{3,2,1,0:T(8,128)(2,1)S(1)} %get-tuple-element.157.refs_4_), channel_id=1, source_target_pairs={{3,0},{7,4},{11,8},{15,12},{19,16},{23,20},{27,24},{31,28}} | collective-permute-start | bytes 737288 | tf_op jit(solution)/shard_map/ppermute | solution.py:68
  190.2 16.4 %collective-permute-start.30 = (bf16[4,3,80,128]{3,2,1,0:T(8,128)(2,1)S(1)}, bf16[4,3,80,128]{3,2,1,0:T(8,128)(2,1)S(1)}, u32[]{:S(2)}, u32[]{:S(2)}) collective-permute-start(bf16[4,3,80,128]{3,2,1,0:T(8,128)(2,1)S(1)} %get-tuple-element.157.refs_4_), channel_id=1, source_target_pairs={{2,0},{3,1},{6,4},{7,5},{10,8},{11,9},{14,12},{15,13},{18,16},{19,... | collective-permute-start | bytes 737288 | tf_op jit(solution)/shard_map/ppermute | solution.py:68
  191.5 15.1 %collective-permute-start.29 = (bf16[4,3,80,128]{3,2,1,0:T(8,128)(2,1)S(1)}, bf16[4,3,80,128]{3,2,1,0:T(8,128)(2,1)S(1)}, u32[]{:S(2)}, u32[]{:S(2)}) collective-permute-start(bf16[4,3,80,128]{3,2,1,0:T(8,128)(2,1)S(1)} %get-tuple-element.157.refs_4_), channel_id=1, source_target_pairs={{1,0},{2,1},{3,2},{5,4},{6,5},{7,6},{9,8},{10,9},{11,10},{13,12},{... | collective-permute-start | bytes 737288 | tf_op jit(solution)/shard_map/ppermute | solution.py:68
  193.2 13.4 %collective-permute-start.32 = (bf16[96,1536]{1,0:T(8,128)(2,1)S(1)}, bf16[96,1536]{1,0:T(8,128)(2,1)S(1)}, u32[]{:S(2)}, u32[]{:S(2)}) collective-permute-start(bf16[96,1536]{1,0:T(8,128)(2,1)S(1)} %get-tuple-element.160.refs_4_), channel_id=1, source_target_pairs={{0,16},{4,20},{8,24},{12,28},{16,0},{20,4},{24,8},{28,12},{1,17},{... | collective-permute-start | bytes 884744 | tf_op jit(solution)/shard_map/ppermute | solution.py:59
  193.8 12.8 %collective-permute-start.33 = (bf16[96,1536]{1,0:T(8,128)(2,1)S(1)}, bf16[96,1536]{1,0:T(8,128)(2,1)S(1)}, u32[]{:S(2)}, u32[]{:S(2)}) collective-permute-start(bf16[96,1536]{1,0:T(8,128)(2,1)S(1)} %get-tuple-element.161.refs_5_), channel_id=1, source_target_pairs={{0,8},{4,12},{8,0},{12,4},{16,24},{20,28},{24,16},{28,20},{1,9},{5... | collective-permute-start | bytes 884744 | tf_op jit(solution)/shard_map/ppermute | solution.py:59
  206.8 20.8 %collective-permute-start.35 = (bf16[192,768]{1,0:T(8,128)(2,1)S(1)}, bf16[192,768]{1,0:T(8,128)(2,1)S(1)}, u32[]{:S(2)}, u32[]{:S(2)}) collective-permute-start(bf16[192,768]{1,0:T(8,128)(2,1)S(1)} %get-tuple-element.166.refs_14_), channel_id=1, source_target_pairs={{0,3},{1,0},{2,1},{3,2},{4,7},{5,4},{6,5},{7,6},{8,11},{9,8},{10,9... | collective-permute-start | bytes 884744 | tf_op jit(solution)/shard_map/ppermute | solution.py:63
  212.4 25.5 %collective-permute-start.36 = (bf16[192,768]{1,0:T(8,128)(2,1)S(1)}, bf16[192,768]{1,0:T(8,128)(2,1)S(1)}, u32[]{:S(2)}, u32[]{:S(2)}) collective-permute-start(bf16[192,768]{1,0:T(8,128)(2,1)S(1)} %get-tuple-element.167.refs_15_), channel_id=1, source_target_pairs={{0,2},{1,3},{2,0},{3,1},{4,6},{5,7},{6,4},{7,5},{8,10},{9,11},{10,... | collective-permute-start | bytes 884744 | tf_op jit(solution)/shard_map/ppermute | solution.py:63
  212.4 25.5 %collective-permute-start.37 = (bf16[192,768]{1,0:T(8,128)(2,1)S(1)}, bf16[192,768]{1,0:T(8,128)(2,1)S(1)}, u32[]{:S(2)}, u32[]{:S(2)}) collective-permute-start(bf16[192,768]{1,0:T(8,128)(2,1)S(1)} %get-tuple-element.168.refs_16_), channel_id=1, source_target_pairs={{0,1},{1,2},{2,3},{3,0},{4,5},{5,6},{6,7},{7,4},{8,9},{9,10},{10,1... | collective-permute-start | bytes 884744 | tf_op jit(solution)/shard_map/ppermute | solution.py:63
  238.1 4.6 %collective-permute-start.38 = (bf16[392,1536]{1,0:T(8,128)(2,1)S(1)}, bf16[392,1536]{1,0:T(8,128)(2,1)S(1)}, u32[]{:S(2)}, u32[]{:S(2)}) collective-permute-start(bf16[392,1536]{1,0:T(8,128)(2,1)S(1)} %get-tuple-element.181), channel_id=1, source_target_pairs={{0,4},{4,0},{8,12},{12,8},{16,20},{20,16},{24,28},{28,24},{1,5},{5... | collective-permute-start | bytes 3612680 | tf_op jit(solution)/shard_map/ppermute | solution.py:59
  238.2 4.6 %collective-permute-start.34 = (bf16[384,1536]{1,0:T(8,128)(2,1)S(1)}, bf16[384,1536]{1,0:T(8,128)(2,1)S(1)}, u32[]{:S(2)}, u32[]{:S(2)}) collective-permute-start(bf16[384,1536]{1,0:T(8,128)(2,1)S(1)} %get-tuple-element.177), channel_id=1, source_target_pairs={{0,4},{4,0},{8,12},{12,8},{16,20},{20,16},{24,28},{28,24},{1,5},{5... | collective-permute-start | bytes 3538952 | tf_op jit(solution)/shard_map/ppermute | solution.py:59
  243.2 16.0 %collective-permute-start.40 = (bf16[400,768]{1,0:T(8,128)(2,1)S(1)}, bf16[400,768]{1,0:T(8,128)(2,1)S(1)}, u32[]{:S(2)}, u32[]{:S(2)}) collective-permute-start(bf16[400,768]{1,0:T(8,128)(2,1)S(1)} %get-tuple-element.184.refs_5_), channel_id=1, source_target_pairs={{0,16},{4,20},{8,24},{12,28},{16,0},{20,4},{24,8},{28,12},{1,17},{... | collective-permute-start | bytes 1843208 | tf_op jit(solution)/shard_map/ppermute | solution.py:59
  243.9 15.1 %collective-permute-start.39 = (bf16[384,768]{1,0:T(8,128)(2,1)S(1)}, bf16[384,768]{1,0:T(8,128)(2,1)S(1)}, u32[]{:S(2)}, u32[]{:S(2)}) collective-permute-start(bf16[384,768]{1,0:T(8,128)(2,1)S(1)} %get-tuple-element.183.refs_4_), channel_id=1, source_target_pairs={{0,8},{4,12},{8,0},{12,4},{16,24},{20,28},{24,16},{28,20},{1,9},{5... | collective-permute-start | bytes 1769480 | tf_op jit(solution)/shard_map/ppermute | solution.py:59
  260.6 10.5 %collective-permute-start.42 = (bf16[208,768]{1,0:T(8,128)(2,1)S(1)}, bf16[208,768]{1,0:T(8,128)(2,1)S(1)}, u32[]{:S(2)}, u32[]{:S(2)}) collective-permute-start(bf16[208,768]{1,0:T(8,128)(2,1)S(1)} %get-tuple-element.191), channel_id=1, source_target_pairs={{0,8},{4,12},{8,0},{12,4},{16,24},{20,28},{24,16},{28,20},{1,9},{5... | collective-permute-start | bytes 958472 | tf_op jit(solution)/shard_map/ppermute | solution.py:59
  260.7 9.9 %collective-permute-start.41 = (bf16[192,768]{1,0:T(8,128)(2,1)S(1)}, bf16[192,768]{1,0:T(8,128)(2,1)S(1)}, u32[]{:S(2)}, u32[]{:S(2)}) collective-permute-start(bf16[192,768]{1,0:T(8,128)(2,1)S(1)} %get-tuple-element.190), channel_id=1, source_target_pairs={{0,16},{4,20},{8,24},{12,28},{16,0},{20,4},{24,8},{28,12},{1,17},{... | collective-permute-start | bytes 884744 | tf_op jit(solution)/shard_map/ppermute | solution.py:59
  262.2 13.1 %collective-permute-start.50 = (bf16[192,768]{1,0:T(8,128)(2,1)S(1)}, bf16[192,768]{1,0:T(8,128)(2,1)S(1)}, u32[]{:S(2)}, u32[]{:S(2)}) collective-permute-start(bf16[192,768]{1,0:T(8,128)(2,1)S(1)} %shard_map.278.refs_0_.refs_1_), channel_id=1, source_target_pairs={{0,16},{4,20},{8,24},{12,28},{16,0},{20,4},{24,8},{28,12},{1,17},{... | collective-permute-start | bytes 884744 | tf_op jit(solution)/shard_map/ppermute | solution.py:59
  262.8 13.0 %collective-permute-start.49 = (bf16[192,768]{1,0:T(8,128)(2,1)S(1)}, bf16[192,768]{1,0:T(8,128)(2,1)S(1)}, u32[]{:S(2)}, u32[]{:S(2)}) collective-permute-start(bf16[192,768]{1,0:T(8,128)(2,1)S(1)} %shard_map.278.refs_0_.refs_1_), channel_id=1, source_target_pairs={{0,8},{4,12},{8,0},{12,4},{16,24},{20,28},{24,16},{28,20},{1,9},{5... | collective-permute-start | bytes 884744 | tf_op jit(solution)/shard_map/ppermute | solution.py:59
  271.3 5.3 %collective-permute-start.43 = (bf16[104,768]{1,0:T(8,128)(2,1)S(1)}, bf16[104,768]{1,0:T(8,128)(2,1)S(1)}, u32[]{:S(2)}, u32[]{:S(2)}) collective-permute-start(bf16[104,768]{1,0:T(8,128)(2,1)S(1)} %get-tuple-element.194), channel_id=1, source_target_pairs={{0,3},{1,0},{2,1},{3,2},{4,7},{5,4},{6,5},{7,6},{8,11},{9,8},{10,9... | collective-permute-start | bytes 479240 | tf_op jit(solution)/shard_map/ppermute | solution.py:63
  276.6 6.7 %collective-permute-start.51 = (bf16[192,768]{1,0:T(8,128)(2,1)S(1)}, bf16[192,768]{1,0:T(8,128)(2,1)S(1)}, u32[]{:S(2)}, u32[]{:S(2)}) collective-permute-start(bf16[192,768]{1,0:T(8,128)(2,1)S(1)} %collective-permute-done.49.refs_1_.refs_2_), channel_id=1, source_target_pairs={{0,16},{4,20},{8,24},{12,28},{16,0},{20,4},{24,8},{28,12},{1,17},{... | collective-permute-start | bytes 884744 | tf_op jit(solution)/shard_map/ppermute | solution.py:59
  277.8 9.0 %collective-permute-start.44 = (bf16[104,768]{1,0:T(8,128)(2,1)S(1)}, bf16[104,768]{1,0:T(8,128)(2,1)S(1)}, u32[]{:S(2)}, u32[]{:S(2)}) collective-permute-start(bf16[104,768]{1,0:T(8,128)(2,1)S(1)} %get-tuple-element.195), channel_id=1, source_target_pairs={{0,2},{1,3},{2,0},{3,1},{4,6},{5,7},{6,4},{7,5},{8,10},{9,11},{10,... | collective-permute-start | bytes 479240 | tf_op jit(solution)/shard_map/ppermute | solution.py:63
  279.0 7.8 %collective-permute-start.45 = (bf16[104,768]{1,0:T(8,128)(2,1)S(1)}, bf16[104,768]{1,0:T(8,128)(2,1)S(1)}, u32[]{:S(2)}, u32[]{:S(2)}) collective-permute-start(bf16[104,768]{1,0:T(8,128)(2,1)S(1)} %get-tuple-element.196), channel_id=1, source_target_pairs={{0,1},{1,2},{2,3},{3,0},{4,5},{5,6},{6,7},{7,4},{8,9},{9,10},{10,1... | collective-permute-start | bytes 479240 | tf_op jit(solution)/shard_map/ppermute | solution.py:63
  283.4 7.1 %collective-permute-start.52 = (bf16[4,192,768]{2,1,0:T(8,128)(2,1)S(1)}, bf16[4,192,768]{2,1,0:T(8,128)(2,1)S(1)}, u32[]{:S(2)}, u32[]{:S(2)}) collective-permute-start(bf16[4,192,768]{2,1,0:T(8,128)(2,1)S(1)} %shard_map.284), channel_id=1, source_target_pairs={{0,4},{4,0},{8,12},{12,8},{16,20},{20,16},{24,28},{28,24},{1,5},{5... | collective-permute-start | bytes 3538952 | tf_op jit(solution)/shard_map/ppermute | solution.py:59
  286.9 7.2 %collective-permute-start.48 = (bf16[96,768]{1,0:T(8,128)(2,1)S(1)}, bf16[96,768]{1,0:T(8,128)(2,1)S(1)}, u32[]{:S(2)}, u32[]{:S(2)}) collective-permute-start(bf16[96,768]{1,0:T(8,128)(2,1)S(1)} %shard_map.283.refs_0_.refs_1_), channel_id=1, source_target_pairs={{0,24},{4,28},{8,16},{12,20},{16,8},{20,12},{24,0},{28,4},{1,25},{... | collective-permute-start | bytes 442376 | tf_op jit(solution)/shard_map/ppermute | solution.py:59
  288.7 6.3 %collective-permute-start.47 = (bf16[96,768]{1,0:T(8,128)(2,1)S(1)}, bf16[96,768]{1,0:T(8,128)(2,1)S(1)}, u32[]{:S(2)}, u32[]{:S(2)}) collective-permute-start(bf16[96,768]{1,0:T(8,128)(2,1)S(1)} %shard_map.283.refs_0_.refs_1_), channel_id=1, source_target_pairs={{0,16},{4,20},{8,24},{12,28},{16,0},{20,4},{24,8},{28,12},{1,17},{... | collective-permute-start | bytes 442376 | tf_op jit(solution)/shard_map/ppermute | solution.py:59
  289.9 5.6 %collective-permute-start.46 = (bf16[96,768]{1,0:T(8,128)(2,1)S(1)}, bf16[96,768]{1,0:T(8,128)(2,1)S(1)}, u32[]{:S(2)}, u32[]{:S(2)}) collective-permute-start(bf16[96,768]{1,0:T(8,128)(2,1)S(1)} %shard_map.283.refs_0_.refs_1_), channel_id=1, source_target_pairs={{0,8},{4,12},{8,0},{12,4},{16,24},{20,28},{24,16},{28,20},{1,9},{5... | collective-permute-start | bytes 442376 | tf_op jit(solution)/shard_map/ppermute | solution.py:59
  295.6 2.1 collective-permute-start.53
  (38 other events, 151.2 us)

commit v2 on v1

--- a/solution.py
+++ b/solution.py
@@ -712,13 +712,13 @@
         feed_kernel,
         (hidden_like, shaped((count, width), BF16), shaped((count, width), BF16),
          shaped((count, width), F32), vectors, grad_like, grad_like),
-        [SMEM] + [VMEM] * 6 + [ANY] * 6, [square, square, pltpu.VMEM(hidden_like.shape, BF16), turned, ordered, total_scratch, sems(32)], limit=33, cost=19,
+        [SMEM] + [VMEM] * 6 + [ANY] * 6, [square, square, pltpu.VMEM(hidden_like.shape, BF16), turned, ordered, total_scratch, sems(32)], limit=31, cost=19,
     )(info, first, bias_in, line(b_two), line(gain_two), line(shift_two), cotangent, *feed_buffers)
 
     got = places.swap(two_send, CORE)
     d_hidden, d_bias_in, in_keep, in_send = call(
         feed_back_kernel, (hidden_like, shaped((tensor, 8, width), F32), grad_like, grad_like),
-        [SMEM] + [VMEM] * 3 + [ANY] * 6, [square, turned, ordered, sems(16)], limit=19, cost=14,
+        [SMEM] + [VMEM] * 3 + [ANY] * 6, [square, turned, ordered, sems(16)], limit=18, cost=14,
     )(info, first, d_second, slope, *feed_buffers)
     wide_halves = halves_like(2 * rows, 2 * width)
     keep0, send0, keep1, send1 = call(first_halves_kernel, wide_halves, [VMEM] * 2, after=(in_send,))(two_keep, got)
@@ -736,7 +736,7 @@
     got_in = swap_all(places, (in_send0, in_send1), (X, Y))
     d_sums, d_carried = call(
         heads_back_kernel, (shaped((tensor, 3, count, 2 * HEAD), BF16), states), [VMEM] * 6,
-        after=(in_send0, in_send1), limit=10, cost=11,
+        after=(in_send0, in_send1), limit=9, cost=11,
     )(d_branch, mix_weight, attended, dens, mixed, query_table)
     arrived_back = [places.onward(d_carried, -s) for s in range(1, tensor)]
     end = shaped((rows, 2 * width), BF16)
@@ -745,7 +745,7 @@
         next_halves_kernel, halves_like(rows, 2 * width), [VMEM] * 4, after=two_ends)(in0, in1, *got_in)
     got_in = swap_all(places, (in_send0, in_send1), (Y, X))
     local = call(
-        local_back_kernel, shaped((tensor, count, wide), F32), [VMEM] * 4, after=(in_send0, in_send1), limit=10, cost=15,
+        local_back_kernel, shaped((tensor, count, wide), F32), [VMEM] * 4, after=(in_send0, in_send1), limit=9, cost=15,
     )(mixed, d_sums, mask, mask_t)
     feed_last = call(
         feed_last_kernel, (shaped((2 * rows, width), BF16),) * tensor, [VMEM] * 6, after=(local, *arrived_back),
@@ -757,13 +757,13 @@
     mix_inputs = (info, mixed, local, d_sums, carried, *arrived_back, query_table, key_table, tokens, attended, d_branch)
     d_mixed_a, d_bias_a, keep_a, send_a = call(
         functools.partial(mix_back_kernel, 0), mix_outs + (mix_like,), [SMEM] + [VMEM] * 12, mix_scratch,
-        after=feed_last, limit=19, cost=11,
+        after=feed_last, limit=17, cost=11,
     )(*mix_inputs)
     got_a = places.swap(send_a, CORE)
     d_mixed_b, d_bias_b, keep_b, send_b, vector_rows = call(
         functools.partial(mix_back_kernel, 2),
         mix_outs + (shaped((4 * rows + 8, 2 * width), BF16), shaped((16, width), BF16)), [SMEM] + [VMEM] * 16,
-        mix_scratch, limit=19, cost=11,
+        mix_scratch, limit=17, cost=11,
     )(*mix_inputs, vectors_one, vectors_two, d_bias_in, d_bias_a)
     feed_rows = added(places, feed_own, 2 * rows, after=(d_mixed_b,))
     got_a, got_b = later(got_a, feed_rows), places.swap(later(send_b, feed_rows), CORE)

time: 306 us -> 304 us (level)
  other arithmetic: 2.95 us -> 6.67 us
    unnamed x103 -> x89, local copies, waits for them, and re-layouts: 10.5 us -> 7.19 us
  transfers between devices with their start and end apart: 54 -> 54, of which waited for: 29 -> 29; matrix products, arithmetic and copies ran while one was open for 2% -> 3% of each run, Pallas kernels for 27% -> 27%
where the time goes in v2:
time: 304 us; the launch traced here: 299 us
  waiting for transfers between devices  114 us (38%)
  Pallas kernels  101 us (33%)
  starting transfers between devices  58.4 us (19%)
  local copies, waits for them, and re-layouts  12.5 us (4%)
  between operations  6.9 us (2%)
  other arithmetic  6.67 us (2%)
    pallas_call x34, Pallas kernels, call(): pl.pallas_call(waiting_body, out_shape=outs, in_specs=list(specs) + [ANY]...  101 us
    ppermute x36, waiting for transfers between devices, swap(): return lax.ppermute(value, 'dp', [(d, d ^ mask) for d in range(self.dp)])  76.4 us
    ppermute x12, waiting for transfers between devices, turn(): lax.ppermute(value, 'tensor', [(k, (k + step) % size) for k in range(size)])  35.8 us
    ppermute x36, starting transfers between devices, swap(): return lax.ppermute(value, 'dp', [(d, d ^ mask) for d in range(self.dp)])  28.9 us
    ppermute x12, starting transfers between devices, turn(): lax.ppermute(value, 'tensor', [(k, (k + step) % size) for k in range(size)])  17.5 us
    ppermute x6, starting transfers between devices, onward(): return lax.ppermute(value, 'tensor', pairs)  12 us
    unnamed x89, local copies, waits for them, and re-layouts  7.19 us
  transfers between devices with their start and end apart: 54, of which 29 were waited for; matrix products, arithmetic and copies ran while one was open for 3% of the time, Pallas kernels for 27%

profile of v2, /device:TPU:0, one launch (start us, length us, event | category | flops | bytes accessed | tf_op | source)
XLA Modules:
  0.0 299.4 jit_solution(13977620119786133882)
XLA Ops:
  2.9 5.1 %collective-permute-start.2 = (bf16[104,768]{1,0:T(8,128)(2,1)S(1)}, bf16[104,768]{1,0:T(8,128)(2,1)S(1)}, u32[]{:S(2)}, u32[]{:S(2)}) collective-permute-start(bf16[104,768]{1,0:T(8,128)(2,1)S(1)} %pad_maximum_fusion.1.refs_0_), channel_id=1, source_target_pairs={{0,3},{1,0},{2,1},{3,2},{4,7},{5,4},{6,5},{7,6},{8,11},{9,8},{10,9... | collective-permute-start | bytes 479240 | tf_op jit(solution)/shard_map/ppermute | solution.py:63
  9.1 3.5 %collective-permute-done.2.refs_3_ = bf16[104,768]{1,0:T(8,128)(2,1)S(1)} collective-permute-done((bf16[104,768]{1,0:T(8,128)(2,1)S(1)}, bf16[104,768]{1,0:T(8,128)(2,1)S(1)}, u32[]{:S(2)}, u32[]{:S(2)}) %collective-permute-start.2) | collective-permute-done | bytes 159776 | tf_op jit(solution)/shard_map/ppermute | solution.py:63
  12.6 9.0 %collective-permute-done.1.refs_2_ = bf16[104,768]{1,0:T(8,128)(2,1)S(1)} collective-permute-done((bf16[104,768]{1,0:T(8,128)(2,1)S(1)}, bf16[104,768]{1,0:T(8,128)(2,1)S(1)}, u32[]{:S(2)}, u32[]{:S(2)}) %collective-permute-start.1) | collective-permute-done | bytes 159776 | tf_op jit(solution)/shard_map/ppermute | solution.py:63
  22.2 1.5 collective-permute-start.3
  23.7 1.5 collective-permute-start.4
  25.3 5.4 %collective-permute-done.3.refs_1_ = bf16[2,96,768]{2,1,0:T(8,128)(2,1)S(1)} collective-permute-done((bf16[2,96,768]{2,1,0:T(8,128)(2,1)S(1)}, bf16[2,96,768]{2,1,0:T(8,128)(2,1)S(1)}, u32[]{:S(2)}, u32[]{:S(2)}) %collective-permute-start.3) | collective-permute-done | bytes 294944 | tf_op jit(solution)/shard_map/ppermute | solution.py:59
  30.7 1.2 collective-permute-done.4.refs_3_
  32.0 1.6 collective-permute-start.5
  35.1 2.6 collective-permute-start.10
  39.2 6.4 %collective-permute-done.5.refs_0_.refs_5_ = bf16[2,2,96,768]{3,2,1,0:T(8,128)(2,1)S(1)} collective-permute-done((bf16[2,2,96,768]{3,2,1,0:T(8,128)(2,1)S(1)}, bf16[2,2,96,768]{3,2,1,0:T(8,128)(2,1)S(1)}, u32[]{:S(2)}, u32[]{:S(2)}) %collective-permute-start.5) | collective-permute-done | bytes 589856 | tf_op jit(solution)/shard_map/ppermute | solution.py:59
  45.6 1.3 collective-permute-done.6.refs_1_.refs_7_
  46.9 2.2 shard_map.257
  58.6 8.7 %collective-permute-done.11.refs_3_ = bf16[192,768]{1,0:T(8,128)(2,1)S(1)} collective-permute-done((bf16[192,768]{1,0:T(8,128)(2,1)S(1)}, bf16[192,768]{1,0:T(8,128)(2,1)S(1)}, u32[]{:S(2)}, u32[]{:S(2)}) %collective-permute-start.11) | collective-permute-done | bytes 294944 | tf_op jit(solution)/shard_map/ppermute | solution.py:63
  69.9 8.2 %shard_map.258 = (bf16[4,512,576]{2,1,0:T(8,128)(2,1)S(1)}, bf16[4,3,80,128]{3,2,1,0:T(8,128)(2,1)S(1)}, bf16[4,768,768]{2,1,0:T(8,128)(2,1)S(1)}) custom-call(s32[8]{0:T(128)S(1)} %stack.69.refs_0_, bf16[512,768]{1,0:T(8,128)(2,1)S(1)} %copy-done.11, f32[4,1,576]{2,1,0:T(1,128)S(1)} %copy-done.29, f32[512,128]{1,0:T(8,128)S(1)} %get-tuple-element.230.refs_3_.refs_9_, ...), custom_call_target="tpu_custom_call" | custom-call | flops 1840000000 | bytes 1 | tf_op jit(solution)/shard_map/pallas_call | solution.py:36
  78.2 4.1 %collective-permute-start.16 = (bf16[4,3,80,128]{3,2,1,0:T(8,128)(2,1)S(1)}, bf16[4,3,80,128]{3,2,1,0:T(8,128)(2,1)S(1)}, u32[]{:S(2)}, u32[]{:S(2)}) collective-permute-start(bf16[4,3,80,128]{3,2,1,0:T(8,128)(2,1)S(1)} %get-tuple-element.120.refs_4_), channel_id=1, source_target_pairs={{0,3},{4,7},{8,11},{12,15},{16,19},{20,23},{24,27},{28,31}} | collective-permute-start | bytes 737288 | tf_op jit(solution)/shard_map/ppermute | solution.py:68
  82.3 1.3 collective-permute-start.15
  83.6 2.6 collective-permute-start.14
  86.3 1.5 fusion
  88.1 1.6 collective-permute-start.17
  89.6 1.5 collective-permute-start.18
  91.1 5.0 %shard_map.261.refs_1_ = f32[4,3,512,128]{3,2,1,0:T(8,128)S(1)} custom-call(bf16[4,512,576]{2,1,0:T(8,128)(2,1)S(1)} %get-tuple-element.116.refs_0_.refs_5_.refs_4_.refs_1_, f32[512,512]{1,0:T(8,128)S(1)} %get-tuple-element.228.refs_1_.refs_2_, bf16[2,2,192,768]{3,2,1,0:T(8,128)(2,1)S(1)} %get-tuple-element.126.refs_2_.refs_0_.refs_7_.refs_4_.refs_6_, ...), custom_call_target="tpu_custom_call" | custom-call | flops 1610000000 | bytes 1 | tf_op jit(solution)/shard_map/pallas_call | solution.py:36
  96.2 1.5 collective-permute-done.14.refs_2_
  97.7 6.6 %shard_map.262 = (bf16[4,512,192]{2,1,0:T(8,128)(2,1)S(1)}, bf16[4,3,80,128]{3,2,1,0:T(8,128)(2,1)S(1)}, f32[4,512,128]{2,1,0:T(8,128)S(1)}, bf16[512,768]{1,0:T...) custom-call(s32[8]{0:T(128)S(1)} %stack.69.refs_0_, f32[4,3,512,128]{3,2,1,0:T(8,128)S(1)} %shard_map.261.refs_1_, ...), custom_call_target="tpu_custom_call" | custom-call | flops 23000000512 | bytes 1 | tf_op jit(solution)/shard_map/pallas_call | solution.py:36
  104.3 1.2 copy-done.16
  106.5 8.3 %collective-permute-done.17.refs_0_.refs_8_.refs_5_.refs_7_ = bf16[2,2,192,768]{3,2,1,0:T(8,128)(2,1)S(1)} collective-permute-done((bf16[2,2,192,768]{3,2,1,0:T(8,128)(2,1)S(1)}, bf16[2,2,192,768]{3,2,1,0:T(8,128)(2,1)S(1)}, u32[]{:S(2)}, u32[]{:S(2)}) %collective-permute-start.17) | collective-permute-done | bytes 1179680 | tf_op jit(solution)/shard_map/ppermute | solution.py:59
  114.8 1.2 collective-permute-done.18.refs_1_.refs_10_.refs_7_.refs_9_
  117.1 3.8 %collective-permute-done.20.refs_12_.refs_9_.refs_11_ = bf16[2,2,2,192,768]{4,3,2,1,0:T(8,128)(2,1)S(1)} collective-permute-done((bf16[2,2,2,192,768]{4,3,2,1,0:T(8,128)(2,1)S(1)}, bf16[2,2,2,192,768]{4,3,2,1,0:T(8,128)(2,1)S(1)}, u32[]{:S(2)}, u32[]{:S(2)}) %collective-permute-start.20) | collective-permute-done | bytes 2359328 | tf_op jit(solution)/shard_map/ppermute | solution.py:59
  120.9 3.4 %collective-permute-done.19.refs_11_.refs_8_.refs_10_ = bf16[2,2,2,192,768]{4,3,2,1,0:T(8,128)(2,1)S(1)} collective-permute-done((bf16[2,2,2,192,768]{4,3,2,1,0:T(8,128)(2,1)S(1)}, bf16[2,2,2,192,768]{4,3,2,1,0:T(8,128)(2,1)S(1)}, u32[]{:S(2)}, u32[]{:S(2)}) %collective-permute-start.19) | collective-permute-done | bytes 2359328 | tf_op jit(solution)/shard_map/ppermute | solution.py:59
  124.2 14.4 %shard_map.265 = (bf16[4,512,768]{2,1,0:T(8,128)(2,1)S(1)}, bf16[512,768]{1,0:T(8,128)(2,1)}, bf16[512,768]{1,0:T(8,128)(2,1)S(1)}, f32[512,768]{1,0:T(8,128)S(1...) custom-call(s32[8]{0:T(128)S(1)} %stack.69.refs_0_, ...), custom_call_target="tpu_custom_call" | custom-call | flops 4369999872 | bytes 1 | tf_op jit(solution)/shard_map/pallas_call | solution.py:36
  138.6 1.1 copy-done.18
  139.9 1.7 copy-done.3
  141.6 8.2 %shard_map.266 = (bf16[4,512,768]{2,1,0:T(8,128)(2,1)S(1)}, f32[4,8,768]{2,1,0:T(8,128)S(1)}, bf16[384,3072]{1,0:T(8,128)(2,1)S(1)}, bf16[384,3072]{1,0:T(8,128)(2,1)S(1)}) custom-call(s32[8]{0:T(128)S(1)} %stack.69.refs_0_, bf16[512,768]{1,0:T(8,128)(2,1)S(1)} %get-tuple-element.124.refs_1_, bf16[512,768]{1,0:T(8,128)(2,1)S(1)} %get-tuple-element.131.refs_2_, ...), custom_call_target="tpu_custom_call" | custom-call | flops 3220000000 | bytes 1 | tf_op jit(solution)/shard_map/pallas_call | solution.py:36
  150.7 1.5 collective-permute-start.23
  153.0 5.8 %shard_map.268 = (f32[512,768]{1,0:T(8,128)S(1)}, bf16[512,768]{1,0:T(8,128)(2,1)S(1)}, f32[8,768]{1,0:T(8,128)S(1)}) custom-call(s32[8]{0:T(128)S(1)} %stack.69.refs_0_, bf16[4,512,768]{2,1,0:T(8,128)(2,1)S(1)} %get-tuple-element.133.refs_1_, f32[512,768]{1,0:T(8,128)S(1)} %copy-done.19, f32[512,768]{1,0:T(8,128)S(1)} %copy-done.17, ...), custom_call_target="tpu_custom_call" | custom-call | flops 2530000128 | bytes 1 | tf_op jit(solution)/shard_map/pallas_call | solution.py:36
  158.8 7.3 %collective-permute-done.23.refs_2_ = bf16[192,1536]{1,0:T(8,128)(2,1)S(1)} collective-permute-done((bf16[192,1536]{1,0:T(8,128)(2,1)S(1)}, bf16[192,1536]{1,0:T(8,128)(2,1)S(1)}, u32[]{:S(2)}, u32[]{:S(2)}) %collective-permute-start.23) | collective-permute-done | bytes 589856 | tf_op jit(solution)/shard_map/ppermute | solution.py:59
  166.1 1.2 collective-permute-done.24.refs_3_
  169.3 1.5 collective-permute-start.27
  170.8 1.5 collective-permute-start.28
  172.3 10.7 %shard_map.271 = (bf16[4,3,512,128]{3,2,1,0:T(8,128)(2,1)S(1)}, bf16[4,3,80,128]{3,2,1,0:T(8,128)(2,1)S(1)}) custom-call(bf16[512,768]{1,0:T(8,128)(2,1)S(1)} %get-tuple-element.142.refs_4_.refs_0_.refs_12_, bf16[4,768,768]{2,1,0:T(8,128)(2,1)S(1)} %get-tuple-element.123.refs_8_.refs_1_.refs_2_, ...), custom_call_target="tpu_custom_call" | custom-call | flops 2530000128 | bytes 1 | tf_op jit(solution)/shard_map/pallas_call | solution.py:36
  183.0 1.3 collective-permute-start.31
  184.3 4.8 %collective-permute-done.27.refs_2_ = bf16[96,1536]{1,0:T(8,128)(2,1)S(1)} collective-permute-done((bf16[96,1536]{1,0:T(8,128)(2,1)S(1)}, bf16[96,1536]{1,0:T(8,128)(2,1)S(1)}, u32[]{:S(2)}, u32[]{:S(2)}) %collective-permute-start.27) | collective-permute-done | bytes 294944 | tf_op jit(solution)/shard_map/ppermute | solution.py:59
  189.1 1.3 collective-permute-start.30
  190.4 1.3 collective-permute-start.29
  192.6 1.4 collective-permute-start.33
  194.0 11.3 %shard_map.274.refs_6_.refs_2_ = f32[4,512,576]{2,1,0:T(8,128)S(1)} custom-call(bf16[4,512,576]{2,1,0:T(8,128)(2,1)S(1)} %get-tuple-element.116.refs_0_.refs_5_.refs_4_.refs_1_, bf16[4,3,512,128]{3,2,1,0:T(8,128)(2,1)S(1)} %get-tuple-element.152.refs_1_.refs_3_, f32[512,512]{1,0:T(8,128)S(1)} %copy-done.10, f32[512,512]{1,0:T(8,128)S(1)} %copy-done.22, ...), custom_call_target="tpu_custom_call" | custom-call | flops 3450000128 | bytes 1 | tf_op jit(solution)/shard_map/pallas_call | solution.py:36
  205.5 5.7 %collective-permute-start.35 = (bf16[192,768]{1,0:T(8,128)(2,1)S(1)}, bf16[192,768]{1,0:T(8,128)(2,1)S(1)}, u32[]{:S(2)}, u32[]{:S(2)}) collective-permute-start(bf16[192,768]{1,0:T(8,128)(2,1)S(1)} %get-tuple-element.166.refs_14_), channel_id=1, source_target_pairs={{0,3},{1,0},{2,1},{3,2},{4,7},{5,4},{6,5},{7,6},{8,11},{9,8},{10,9... | collective-permute-start | bytes 884744 | tf_op jit(solution)/shard_map/ppermute | solution.py:63
  211.9 7.0 %shard_map.276 = (bf16[2,512,768]{2,1,0:T(8,128)(2,1)S(1)}, f32[2,8,768]{2,1,0:T(8,128)S(1)}, bf16[384,1536]{1,0:T(8,128)(2,1)S(1)}, bf16[384,1536]{1,0:T(8,128)(2,1)S(1)}) custom-call(s32[8]{0:T(128)S(1)} %stack.69.refs_0_, bf16[4,512,576]{2,1,0:T(8,128)(2,1)S(1)} %get-tuple-element.116.refs_0_.refs_5_.refs_4_.refs_1_, ...), custom_call_target="tpu_custom_call" | custom-call | flops 2530000128 | bytes 1 | tf_op jit(solution)/shard_map/pallas_call | solution.py:36
  218.9 7.4 %shard_map.277 = (bf16[2,512,768]{2,1,0:T(8,128)(2,1)S(1)}, f32[2,8,768]{2,1,0:T(8,128)}, bf16[384,1536]{1,0:T(8,128)(2,1)S(1)}, bf16[392,1536]{1,0:T(8,128)(2,1)S(1)}, bf16[16,768]{1,0:T(8,128)(2,1)S(1)}) custom-call(s32[8]{0:T(128)S(1)} %stack.69.refs_0_, bf16[4,512,576]{2,1,0:T(8,128)(2,1)S(1)} %get-tuple-element.116.refs_0_.refs_5_.refs_4_.refs_1_, ...), custom_call_target="tpu_custom_call" | custom-call | flops 2530000128 | bytes 1 | tf_op jit(solution)/shard_map/pallas_call | solution.py:36
  226.4 10.5 %collective-permute-done.36.refs_2_ = bf16[192,768]{1,0:T(8,128)(2,1)S(1)} collective-permute-done((bf16[192,768]{1,0:T(8,128)(2,1)S(1)}, bf16[192,768]{1,0:T(8,128)(2,1)S(1)}, u32[]{:S(2)}, u32[]{:S(2)}) %collective-permute-start.36) | collective-permute-done | bytes 294944 | tf_op jit(solution)/shard_map/ppermute | solution.py:63
  237.5 4.1 %collective-permute-done.34.refs_1_ = bf16[384,1536]{1,0:T(8,128)(2,1)S(1)} collective-permute-done((bf16[384,1536]{1,0:T(8,128)(2,1)S(1)}, bf16[384,1536]{1,0:T(8,128)(2,1)S(1)}, u32[]{:S(2)}, u32[]{:S(2)}) %collective-permute-start.34) | collective-permute-done | bytes 1179680 | tf_op jit(solution)/shard_map/ppermute | solution.py:59
  242.7 3.5 %shard_map.280.refs_5_ = bf16[512,768]{1,0:T(8,128)(2,1)} custom-call(bf16[2,512,768]{2,1,0:T(8,128)(2,1)S(1)} %get-tuple-element.169.refs_0_, bf16[2,512,768]{2,1,0:T(8,128)(2,1)S(1)} %get-tuple-element.174.refs_4_.refs_1_, bf16[4,768,768]{2,1,0:T(8,128)(2,1)S(1)} %get-tuple-element.123.refs_8_.refs_1_.refs_2_, f32[512,768]{1,0:T(8,128)S(1)} %get-tuple-element.175.refs_3_, ...), custom_call_target="tpu_custom_call" | custom-call | flops 1380000000 | bytes 1 | tf_op jit(solution)/shard_map/pallas_call | solution.py:36
  246.2 11.5 %collective-permute-done.39.refs_2_ = bf16[384,768]{1,0:T(8,128)(2,1)S(1)} collective-permute-done((bf16[384,768]{1,0:T(8,128)(2,1)S(1)}, bf16[384,768]{1,0:T(8,128)(2,1)S(1)}, u32[]{:S(2)}, u32[]{:S(2)}) %collective-permute-start.39) | collective-permute-done | bytes 589856 | tf_op jit(solution)/shard_map/ppermute | solution.py:59
  259.5 1.5 collective-permute-start.41
  261.6 1.9 collective-permute-start.49
  263.6 6.0 %collective-permute-done.41.refs_2_ = bf16[192,768]{1,0:T(8,128)(2,1)S(1)} collective-permute-done((bf16[192,768]{1,0:T(8,128)(2,1)S(1)}, bf16[192,768]{1,0:T(8,128)(2,1)S(1)}, u32[]{:S(2)}, u32[]{:S(2)}) %collective-permute-start.41) | collective-permute-done | bytes 294944 | tf_op jit(solution)/shard_map/ppermute | solution.py:59
  270.2 4.0 %collective-permute-done.50.refs_2_.refs_3_ = bf16[192,768]{1,0:T(8,128)(2,1)S(1)} collective-permute-done((bf16[192,768]{1,0:T(8,128)(2,1)S(1)}, bf16[192,768]{1,0:T(8,128)(2,1)S(1)}, u32[]{:S(2)}, u32[]{:S(2)}) %collective-permute-start.50) | collective-permute-done | bytes 294944 | tf_op jit(solution)/shard_map/ppermute | solution.py:59
  275.5 1.2 collective-permute-start.51
  277.7 1.3 collective-permute-start.45
  279.1 3.1 %collective-permute-done.51.refs_3_.refs_4_ = bf16[192,768]{1,0:T(8,128)(2,1)S(1)} collective-permute-done((bf16[192,768]{1,0:T(8,128)(2,1)S(1)}, bf16[192,768]{1,0:T(8,128)(2,1)S(1)}, u32[]{:S(2)}, u32[]{:S(2)}) %collective-permute-start.51) | collective-permute-done | bytes 294944 | tf_op jit(solution)/shard_map/ppermute | solution.py:59
  282.3 3.3 %collective-permute-done.44.refs_2_ = bf16[104,768]{1,0:T(8,128)(2,1)S(1)} collective-permute-done((bf16[104,768]{1,0:T(8,128)(2,1)S(1)}, bf16[104,768]{1,0:T(8,128)(2,1)S(1)}, u32[]{:S(2)}, u32[]{:S(2)}) %collective-permute-start.44) | collective-permute-done | bytes 159776 | tf_op jit(solution)/shard_map/ppermute | solution.py:63
  285.7 1.8 collective-permute-start.48
  287.6 1.2 collective-permute-start.47
  289.3 3.6 %shard_map.285 = (f32[768,768]{1,0:T(8,128)}, f32[768,768]{1,0:T(8,128)}) custom-call(s32[8]{0:T(128)S(1)} %stack.69.refs_0_, bf16[192,768]{1,0:T(8,128)(2,1)S(1)} %shard_map.278.refs_0_.refs_1_, bf16[192,768]{1,0:T(8,128)(2,1)S(1)} %collective-permute-done.49.refs_1_.refs_2_, bf16[192,768]{1,0:T(8,128)(2,1)S(1)} %collective-permute-done.50.refs_2_.refs_3_, ...), custom_call_target="tpu_custom_call" | custom-call | flops 920000000 | bytes 1 | tf_op jit(solution)/shard_map/pallas_call | solution.py:36
  296.5 2.8 shard_map.287
  (199 shorter events, 33.1 us)
Async XLA Ops:
  2.9 9.7 %collective-permute-start.2 = (bf16[104,768]{1,0:T(8,128)(2,1)S(1)}, bf16[104,768]{1,0:T(8,128)(2,1)S(1)}, u32[]{:S(2)}, u32[]{:S(2)}) collective-permute-start(bf16[104,768]{1,0:T(8,128)(2,1)S(1)} %pad_maximum_fusion.1.refs_0_), channel_id=1, source_target_pairs={{0,3},{1,0},{2,1},{3,2},{4,7},{5,4},{6,5},{7,6},{8,11},{9,8},{10,9... | collective-permute-start | bytes 479240 | tf_op jit(solution)/shard_map/ppermute | solution.py:63
  8.0 13.5 %collective-permute-start.1 = (bf16[104,768]{1,0:T(8,128)(2,1)S(1)}, bf16[104,768]{1,0:T(8,128)(2,1)S(1)}, u32[]{:S(2)}, u32[]{:S(2)}) collective-permute-start(bf16[104,768]{1,0:T(8,128)(2,1)S(1)} %pad_maximum_fusion.1.refs_0_), channel_id=1, source_target_pairs={{0,2},{1,3},{2,0},{3,1},{4,6},{5,7},{6,4},{7,5},{8,10},{9,11},{10,... | collective-permute-start | bytes 479240 | tf_op jit(solution)/shard_map/ppermute | solution.py:63
  8.1 13.5 %collective-permute-start = (bf16[104,768]{1,0:T(8,128)(2,1)S(1)}, bf16[104,768]{1,0:T(8,128)(2,1)S(1)}, u32[]{:S(2)}, u32[]{:S(2)}) collective-permute-start(bf16[104,768]{1,0:T(8,128)(2,1)S(1)} %pad_maximum_fusion.1.refs_0_), channel_id=1, source_target_pairs={{0,1},{1,2},{2,3},{3,0},{4,5},{5,6},{6,7},{7,4},{8,9},{9,10},{10,1... | collective-permute-start | bytes 479240 | tf_op jit(solution)/shard_map/ppermute | solution.py:63
  22.2 15.5 %copy-start.34 = (s32[1,8]{1,0:T(1,128)S(1)}, s32[1,8]{1,0:T(1,128)}, u32[]{:S(2)}) copy-start(s32[1,8]{1,0:T(1,128)} %param.16) | copy-start | bytes 100
  22.2 8.4 %collective-permute-start.3 = (bf16[2,96,768]{2,1,0:T(8,128)(2,1)S(1)}, bf16[2,96,768]{2,1,0:T(8,128)(2,1)S(1)}, u32[]{:S(2)}, u32[]{:S(2)}) collective-permute-start(bf16[2,96,768]{2,1,0:T(8,128)(2,1)S(1)} %get-tuple-element.112.refs_0_), channel_id=1, source_target_pairs={{0,8},{4,12},{8,0},{12,4},{16,24},{20,28},{24,16},{28,20},{1,9},{5... | collective-permute-start | bytes 884744 | tf_op jit(solution)/shard_map/ppermute | solution.py:59
  23.7 8.2 %collective-permute-start.4 = (bf16[2,96,768]{2,1,0:T(8,128)(2,1)S(1)}, bf16[2,96,768]{2,1,0:T(8,128)(2,1)S(1)}, u32[]{:S(2)}, u32[]{:S(2)}) collective-permute-start(bf16[2,96,768]{2,1,0:T(8,128)(2,1)S(1)} %get-tuple-element.113.refs_2_), channel_id=1, source_target_pairs={{0,16},{4,20},{8,24},{12,28},{16,0},{20,4},{24,8},{28,12},{1,17},{... | collective-permute-start | bytes 884744 | tf_op jit(solution)/shard_map/ppermute | solution.py:59
  32.0 13.6 %collective-permute-start.5 = (bf16[2,2,96,768]{3,2,1,0:T(8,128)(2,1)S(1)}, bf16[2,2,96,768]{3,2,1,0:T(8,128)(2,1)S(1)}, u32[]{:S(2)}, u32[]{:S(2)}) collective-permute-start(bf16[2,2,96,768]{3,2,1,0:T(8,128)(2,1)S(1)} %get-tuple-element.114.refs_0_.refs_4_), channel_id=1, source_target_pairs={{0,16},{4,20},{8,24},{12,28},{16,0},{20,4},{24,8},{28,12},{1,17},{... | collective-permute-start | bytes 1769480 | tf_op jit(solution)/shard_map/ppermute | solution.py:59
  33.6 13.4 %collective-permute-start.6 = (bf16[2,2,96,768]{3,2,1,0:T(8,128)(2,1)S(1)}, bf16[2,2,96,768]{3,2,1,0:T(8,128)(2,1)}, u32[]{:S(2)}, u32[]{:S(2)}) collective-permute-start(bf16[2,2,96,768]{3,2,1,0:T(8,128)(2,1)S(1)} %get-tuple-element.115.refs_1_.refs_6_.refs_5_), channel_id=1, source_target_pairs={{0,8},{4,12},{8,0},{12,4},{16,24},{20,28},{24,16},{28,20},{1,9},{5... | collective-permute-start | bytes 1769480 | tf_op jit(solution)/shard_map/ppermute | solution.py:59
  35.1 23.5 %collective-permute-start.10 = (bf16[192,768]{1,0:T(8,128)(2,1)S(1)}, bf16[192,768]{1,0:T(8,128)(2,1)S(1)}, u32[]{:S(2)}, u32[]{:S(2)}) collective-permute-start(bf16[192,768]{1,0:T(8,128)(2,1)S(1)} %pad_maximum_fusion.refs_0_), channel_id=1, source_target_pairs={{0,2},{1,3},{2,0},{3,1},{4,6},{5,7},{6,4},{7,5},{8,10},{9,11},{10,... | collective-permute-start | bytes 884744 | tf_op jit(solution)/shard_map/ppermute | solution.py:63
  37.7 20.9 %collective-permute-start.9 = (bf16[192,768]{1,0:T(8,128)(2,1)S(1)}, bf16[192,768]{1,0:T(8,128)(2,1)}, u32[]{:S(2)}, u32[]{:S(2)}) collective-permute-start(bf16[192,768]{1,0:T(8,128)(2,1)S(1)} %pad_maximum_fusion.refs_0_), channel_id=1, source_target_pairs={{0,1},{1,2},{2,3},{3,0},{4,5},{5,6},{6,7},{7,4},{8,9},{9,10},{10,1... | collective-permute-start | bytes 884744 | tf_op jit(solution)/shard_map/ppermute | solution.py:63
  39.1 30.8 %collective-permute-start.7 = (bf16[2,2,2,96,768]{4,3,2,1,0:T(8,128)(2,1)S(1)}, bf16[2,2,2,96,768]{4,3,2,1,0:T(8,128)(2,1)}, u32[]{:S(2)}, u32[]{:S(2)}) collective-permute-start(bf16[2,2,2,96,768]{4,3,2,1,0:T(8,128)(2,1)S(1)} %shard_map.256), channel_id=1, source_target_pairs={{0,4},{4,0},{8,12},{12,8},{16,20},{20,16},{24,28},{28,24},{1,5},{5... | collective-permute-start | bytes 3538952 | tf_op jit(solution)/shard_map/ppermute | solution.py:59
  49.1 20.8 %collective-permute-start.8 = (bf16[2,2,2,96,768]{4,3,2,1,0:T(8,128)(2,1)}, bf16[2,2,2,96,768]{4,3,2,1,0:T(8,128)(2,1)}, u32[]{:S(2)}, u32[]{:S(2)}) collective-permute-start(bf16[2,2,2,96,768]{4,3,2,1,0:T(8,128)(2,1)} %shard_map.257), channel_id=1, source_target_pairs={{0,4},{4,0},{8,12},{12,8},{16,20},{20,16},{24,28},{28,24},{1,5},{5... | collective-permute-start | bytes 3538952 | tf_op jit(solution)/shard_map/ppermute | solution.py:59
  57.8 11.7 %copy-start.30 = (f32[512]{0:T(512)S(1)}, f32[512]{0:T(512)}, u32[]{:S(2)}) copy-start(f32[512]{0:T(512)} %get-tuple-element.225) | copy-start | bytes 6148
  57.8 11.7 %copy-start.31 = (f32[512]{0:T(512)S(1)}, f32[512]{0:T(512)}, u32[]{:S(2)}) copy-start(f32[512]{0:T(512)} %sin.11) | copy-start | bytes 6148
  57.8 9.5 %collective-permute-start.11 = (bf16[192,768]{1,0:T(8,128)(2,1)S(1)}, bf16[192,768]{1,0:T(8,128)(2,1)S(1)}, u32[]{:S(2)}, u32[]{:S(2)}) collective-permute-start(bf16[192,768]{1,0:T(8,128)(2,1)S(1)} %pad_maximum_fusion.refs_0_), channel_id=1, source_target_pairs={{0,3},{1,0},{2,1},{3,2},{4,7},{5,4},{6,5},{7,6},{8,11},{9,8},{10,9... | collective-permute-start | bytes 884744 | tf_op jit(solution)/shard_map/ppermute | solution.py:63
  58.6 11.3 %copy-start.11 = (bf16[512,768]{1,0:T(8,128)(2,1)S(1)}, bf16[512,768]{1,0:T(8,128)(2,1)}, u32[]{:S(2)}) copy-start(bf16[512,768]{1,0:T(8,128)(2,1)} %refs_10_.3) | copy-start | bytes 2359300
  58.6 11.3 %copy-start.29 = (f32[4,1,576]{2,1,0:T(1,128)S(1)}, f32[4,1,576]{2,1,0:T(1,128)}, u32[]{:S(2)}) copy-start(f32[4,1,576]{2,1,0:T(1,128)} %copy-done.28) | copy-start | bytes 27652
  68.4 19.5 %collective-permute-start.12 = (bf16[2,192,768]{2,1,0:T(8,128)(2,1)S(1)}, bf16[2,192,768]{2,1,0:T(8,128)(2,1)S(1)}, u32[]{:S(2)}, u32[]{:S(2)}) collective-permute-start(bf16[2,192,768]{2,1,0:T(8,128)(2,1)S(1)} %get-tuple-element.118.refs_0_), channel_id=1, source_target_pairs={{0,8},{4,12},{8,0},{12,4},{16,24},{20,28},{24,16},{28,20},{1,9},{5... | collective-permute-start | bytes 1769480 | tf_op jit(solution)/shard_map/ppermute | solution.py:59
  69.0 18.9 %collective-permute-start.13 = (bf16[2,192,768]{2,1,0:T(8,128)(2,1)S(1)}, bf16[2,192,768]{2,1,0:T(8,128)(2,1)S(1)}, u32[]{:S(2)}, u32[]{:S(2)}) collective-permute-start(bf16[2,192,768]{2,1,0:T(8,128)(2,1)S(1)} %get-tuple-element.119.refs_2_), channel_id=1, source_target_pairs={{0,16},{4,20},{8,24},{12,28},{16,0},{20,4},{24,8},{28,12},{1,17},{... | collective-permute-start | bytes 1769480 | tf_op jit(solution)/shard_map/ppermute | solution.py:59
  69.9 27.8 %copy-start.7 = (f32[512,128]{1,0:T(8,128)}, f32[512,128]{1,0:T(8,128)S(1)}, u32[]{:S(2)}) copy-start(f32[512,128]{1,0:T(8,128)S(1)} %get-tuple-element.229.refs_6_.refs_5_.refs_8_) | copy-start | bytes 786436
  69.9 16.4 %copy-start.33 = (s32[512]{0:T(512)S(1)}, s32[512]{0:T(512)}, u32[]{:S(2)}) copy-start(s32[512]{0:T(512)} %copy-done.32) | copy-start | bytes 6148
  78.2 18.0 %collective-permute-start.16 = (bf16[4,3,80,128]{3,2,1,0:T(8,128)(2,1)S(1)}, bf16[4,3,80,128]{3,2,1,0:T(8,128)(2,1)S(1)}, u32[]{:S(2)}, u32[]{:S(2)}) collective-permute-start(bf16[4,3,80,128]{3,2,1,0:T(8,128)(2,1)S(1)} %get-tuple-element.120.refs_4_), channel_id=1, source_target_pairs={{0,3},{4,7},{8,11},{12,15},{16,19},{20,23},{24,27},{28,31}} | collective-permute-start | bytes 737288 | tf_op jit(solution)/shard_map/ppermute | solution.py:68
  82.3 13.8 %collective-permute-start.15 = (bf16[4,3,80,128]{3,2,1,0:T(8,128)(2,1)S(1)}, bf16[4,3,80,128]{3,2,1,0:T(8,128)(2,1)S(1)}, u32[]{:S(2)}, u32[]{:S(2)}) collective-permute-start(bf16[4,3,80,128]{3,2,1,0:T(8,128)(2,1)S(1)} %get-tuple-element.120.refs_4_), channel_id=1, source_target_pairs={{0,2},{1,3},{4,6},{5,7},{8,10},{9,11},{12,14},{13,15},{16,18},{17,... | collective-permute-start | bytes 737288 | tf_op jit(solution)/shard_map/ppermute | solution.py:68
  83.6 14.0 %collective-permute-start.14 = (bf16[4,3,80,128]{3,2,1,0:T(8,128)(2,1)S(1)}, bf16[4,3,80,128]{3,2,1,0:T(8,128)(2,1)S(1)}, u32[]{:S(2)}, u32[]{:S(2)}) collective-permute-start(bf16[4,3,80,128]{3,2,1,0:T(8,128)(2,1)S(1)} %get-tuple-element.120.refs_4_), channel_id=1, source_target_pairs={{0,1},{1,2},{2,3},{4,5},{5,6},{6,7},{8,9},{9,10},{10,11},{12,13},{... | collective-permute-start | bytes 737288 | tf_op jit(solution)/shard_map/ppermute | solution.py:68
  88.1 26.7 %collective-permute-start.17 = (bf16[2,2,192,768]{3,2,1,0:T(8,128)(2,1)S(1)}, bf16[2,2,192,768]{3,2,1,0:T(8,128)(2,1)S(1)}, u32[]{:S(2)}, u32[]{:S(2)}) collective-permute-start(bf16[2,2,192,768]{3,2,1,0:T(8,128)(2,1)S(1)} %get-tuple-element.126.refs_2_.refs_0_.refs_7_.refs_4_.refs_6_), channel_id=1, source_target_pairs={{0,16},{4,20},{8,24},{12,28},{16,0},{20,4},{24,8},{28,12},{1,17},{... | collective-permute-start | bytes 3538952 | tf_op jit(solution)/shard_map/ppermute | solution.py:59
  89.6 26.4 %collective-permute-start.18 = (bf16[2,2,192,768]{3,2,1,0:T(8,128)(2,1)S(1)}, bf16[2,2,192,768]{3,2,1,0:T(8,128)(2,1)S(1)}, u32[]{:S(2)}, u32[]{:S(2)}) collective-permute-start(bf16[2,2,192,768]{3,2,1,0:T(8,128)(2,1)S(1)} %get-tuple-element.128.refs_3_.refs_1_.refs_9_.refs_6_.refs_8_), channel_id=1, source_target_pairs={{0,8},{4,12},{8,0},{12,4},{16,24},{20,28},{24,16},{28,20},{1,9},{5... | collective-permute-start | bytes 3538952 | tf_op jit(solution)/shard_map/ppermute | solution.py:59
  116.3 4.6 %collective-permute-start.20 = (bf16[2,2,2,192,768]{4,3,2,1,0:T(8,128)(2,1)S(1)}, bf16[2,2,2,192,768]{4,3,2,1,0:T(8,128)(2,1)S(1)}, u32[]{:S(2)}, u32[]{:S(2)}) collective-permute-start(bf16[2,2,2,192,768]{4,3,2,1,0:T(8,128)(2,1)S(1)} %shard_map.264), channel_id=1, source_target_pairs={{0,4},{4,0},{8,12},{12,8},{16,20},{20,16},{24,28},{28,24},{1,5},{5... | collective-permute-start | bytes 7077896 | tf_op jit(solution)/shard_map/ppermute | solution.py:59
  116.5 7.7 %collective-permute-start.19 = (bf16[2,2,2,192,768]{4,3,2,1,0:T(8,128)(2,1)S(1)}, bf16[2,2,2,192,768]{4,3,2,1,0:T(8,128)(2,1)S(1)}, u32[]{:S(2)}, u32[]{:S(2)}) collective-permute-start(bf16[2,2,2,192,768]{4,3,2,1,0:T(8,128)(2,1)S(1)} %shard_map.263), channel_id=1, source_target_pairs={{0,4},{4,0},{8,12},{12,8},{16,20},{20,16},{24,28},{28,24},{1,5},{5... | collective-permute-start | bytes 7077896 | tf_op jit(solution)/shard_map/ppermute | solution.py:59
  120.9 17.8 %copy-start.2 = (bf16[2,2,2,192,768]{4,3,2,1,0:T(8,128)(2,1)}, bf16[2,2,2,192,768]{4,3,2,1,0:T(8,128)(2,1)S(1)}, u32[]{:S(2)}) copy-start(bf16[2,2,2,192,768]{4,3,2,1,0:T(8,128)(2,1)S(1)} %collective-permute-done.20.refs_12_.refs_9_.refs_11_) | copy-start | bytes 7077892
  124.2 15.7 %copy-start.5 = (bf16[2,2,2,192,768]{4,3,2,1,0:T(8,128)(2,1)}, bf16[2,2,2,192,768]{4,3,2,1,0:T(8,128)(2,1)S(1)}, u32[]{:S(2)}) copy-start(bf16[2,2,2,192,768]{4,3,2,1,0:T(8,128)(2,1)S(1)} %collective-permute-done.19.refs_11_.refs_8_.refs_10_) | copy-start | bytes 7077892
  139.8 10.4 %collective-permute-start.21 = (bf16[384,3072]{1,0:T(8,128)(2,1)S(1)}, bf16[384,3072]{1,0:T(8,128)(2,1)S(1)}, u32[]{:S(2)}, u32[]{:S(2)}) collective-permute-start(bf16[384,3072]{1,0:T(8,128)(2,1)S(1)} %get-tuple-element.138), channel_id=1, source_target_pairs={{0,4},{4,0},{8,12},{12,8},{16,20},{20,16},{24,28},{28,24},{1,5},{5... | collective-permute-start | bytes 7077896 | tf_op jit(solution)/shard_map/ppermute | solution.py:59
  141.6 11.2 %copy-start.19 = (f32[512,768]{1,0:T(8,128)S(1)}, f32[512,768]{1,0:T(8,128)}, u32[]{:S(2)}) copy-start(f32[512,768]{1,0:T(8,128)} %copy-done.18) | copy-start | bytes 4718596
  149.7 17.9 %collective-permute-start.22 = (bf16[384,3072]{1,0:T(8,128)(2,1)S(1)}, bf16[384,3072]{1,0:T(8,128)(2,1)S(1)}, u32[]{:S(2)}, u32[]{:S(2)}) collective-permute-start(bf16[384,3072]{1,0:T(8,128)(2,1)S(1)} %get-tuple-element.139.refs_2_), channel_id=1, source_target_pairs={{0,4},{4,0},{8,12},{12,8},{16,20},{20,16},{24,28},{28,24},{1,5},{5... | collective-permute-start | bytes 7077896 | tf_op jit(solution)/shard_map/ppermute | solution.py:59
  150.7 15.4 %collective-permute-start.23 = (bf16[192,1536]{1,0:T(8,128)(2,1)S(1)}, bf16[192,1536]{1,0:T(8,128)(2,1)S(1)}, u32[]{:S(2)}, u32[]{:S(2)}) collective-permute-start(bf16[192,1536]{1,0:T(8,128)(2,1)S(1)} %get-tuple-element.140.refs_12_), channel_id=1, source_target_pairs={{0,8},{4,12},{8,0},{12,4},{16,24},{20,28},{24,16},{28,20},{1,9},{5... | collective-permute-start | bytes 1769480 | tf_op jit(solution)/shard_map/ppermute | solution.py:59
  152.2 15.1 %collective-permute-start.24 = (bf16[192,1536]{1,0:T(8,128)(2,1)S(1)}, bf16[192,1536]{1,0:T(8,128)(2,1)S(1)}, u32[]{:S(2)}, u32[]{:S(2)}) collective-permute-start(bf16[192,1536]{1,0:T(8,128)(2,1)S(1)} %get-tuple-element.141.refs_13_), channel_id=1, source_target_pairs={{0,16},{4,20},{8,24},{12,28},{16,0},{20,4},{24,8},{28,12},{1,17},{... | collective-permute-start | bytes 1769480 | tf_op jit(solution)/shard_map/ppermute | solution.py:59
  168.1 23.6 %collective-permute-start.25 = (bf16[192,1536]{1,0:T(8,128)(2,1)S(1)}, bf16[192,1536]{1,0:T(8,128)(2,1)S(1)}, u32[]{:S(2)}, u32[]{:S(2)}) collective-permute-start(bf16[192,1536]{1,0:T(8,128)(2,1)S(1)} %get-tuple-element.150.refs_6_), channel_id=1, source_target_pairs={{0,8},{4,12},{8,0},{12,4},{16,24},{20,28},{24,16},{28,20},{1,9},{5... | collective-permute-start | bytes 1769480 | tf_op jit(solution)/shard_map/ppermute | solution.py:59
  168.8 23.0 %collective-permute-start.26 = (bf16[192,1536]{1,0:T(8,128)(2,1)S(1)}, bf16[192,1536]{1,0:T(8,128)(2,1)S(1)}, u32[]{:S(2)}, u32[]{:S(2)}) collective-permute-start(bf16[192,1536]{1,0:T(8,128)(2,1)S(1)} %get-tuple-element.151.refs_7_), channel_id=1, source_target_pairs={{0,16},{4,20},{8,24},{12,28},{16,0},{20,4},{24,8},{28,12},{1,17},{... | collective-permute-start | bytes 1769480 | tf_op jit(solution)/shard_map/ppermute | solution.py:59
  169.3 19.8 %collective-permute-start.27 = (bf16[96,1536]{1,0:T(8,128)(2,1)S(1)}, bf16[96,1536]{1,0:T(8,128)(2,1)S(1)}, u32[]{:S(2)}, u32[]{:S(2)}) collective-permute-start(bf16[96,1536]{1,0:T(8,128)(2,1)S(1)} %get-tuple-element.148.refs_2_), channel_id=1, source_target_pairs={{0,16},{4,20},{8,24},{12,28},{16,0},{20,4},{24,8},{28,12},{1,17},{... | collective-permute-start | bytes 884744 | tf_op jit(solution)/shard_map/ppermute | solution.py:59
  170.8 19.6 %collective-permute-start.28 = (bf16[96,1536]{1,0:T(8,128)(2,1)S(1)}, bf16[96,1536]{1,0:T(8,128)(2,1)S(1)}, u32[]{:S(2)}, u32[]{:S(2)}) collective-permute-start(bf16[96,1536]{1,0:T(8,128)(2,1)S(1)} %get-tuple-element.149.refs_3_), channel_id=1, source_target_pairs={{0,8},{4,12},{8,0},{12,4},{16,24},{20,28},{24,16},{28,20},{1,9},{5... | collective-permute-start | bytes 884744 | tf_op jit(solution)/shard_map/ppermute | solution.py:59
  183.0 22.3 %collective-permute-start.31 = (bf16[4,3,80,128]{3,2,1,0:T(8,128)(2,1)S(1)}, bf16[4,3,80,128]{3,2,1,0:T(8,128)(2,1)S(1)}, u32[]{:S(2)}, u32[]{:S(2)}) collective-permute-start(bf16[4,3,80,128]{3,2,1,0:T(8,128)(2,1)S(1)} %get-tuple-element.157.refs_4_), channel_id=1, source_target_pairs={{3,0},{7,4},{11,8},{15,12},{19,16},{23,20},{27,24},{31,28}} | collective-permute-start | bytes 737288 | tf_op jit(solution)/shard_map/ppermute | solution.py:68
  189.1 16.2 %collective-permute-start.30 = (bf16[4,3,80,128]{3,2,1,0:T(8,128)(2,1)S(1)}, bf16[4,3,80,128]{3,2,1,0:T(8,128)(2,1)S(1)}, u32[]{:S(2)}, u32[]{:S(2)}) collective-permute-start(bf16[4,3,80,128]{3,2,1,0:T(8,128)(2,1)S(1)} %get-tuple-element.157.refs_4_), channel_id=1, source_target_pairs={{2,0},{3,1},{6,4},{7,5},{10,8},{11,9},{14,12},{15,13},{18,16},{19,... | collective-permute-start | bytes 737288 | tf_op jit(solution)/shard_map/ppermute | solution.py:68
  190.4 15.0 %collective-permute-start.29 = (bf16[4,3,80,128]{3,2,1,0:T(8,128)(2,1)S(1)}, bf16[4,3,80,128]{3,2,1,0:T(8,128)(2,1)S(1)}, u32[]{:S(2)}, u32[]{:S(2)}) collective-permute-start(bf16[4,3,80,128]{3,2,1,0:T(8,128)(2,1)S(1)} %get-tuple-element.157.refs_4_), channel_id=1, source_target_pairs={{1,0},{2,1},{3,2},{5,4},{6,5},{7,6},{9,8},{10,9},{11,10},{13,12},{... | collective-permute-start | bytes 737288 | tf_op jit(solution)/shard_map/ppermute | solution.py:68
  192.0 13.3 %collective-permute-start.32 = (bf16[96,1536]{1,0:T(8,128)(2,1)S(1)}, bf16[96,1536]{1,0:T(8,128)(2,1)S(1)}, u32[]{:S(2)}, u32[]{:S(2)}) collective-permute-start(bf16[96,1536]{1,0:T(8,128)(2,1)S(1)} %get-tuple-element.160.refs_4_), channel_id=1, source_target_pairs={{0,16},{4,20},{8,24},{12,28},{16,0},{20,4},{24,8},{28,12},{1,17},{... | collective-permute-start | bytes 884744 | tf_op jit(solution)/shard_map/ppermute | solution.py:59
  192.6 12.8 %collective-permute-start.33 = (bf16[96,1536]{1,0:T(8,128)(2,1)S(1)}, bf16[96,1536]{1,0:T(8,128)(2,1)S(1)}, u32[]{:S(2)}, u32[]{:S(2)}) collective-permute-start(bf16[96,1536]{1,0:T(8,128)(2,1)S(1)} %get-tuple-element.161.refs_5_), channel_id=1, source_target_pairs={{0,8},{4,12},{8,0},{12,4},{16,24},{20,28},{24,16},{28,20},{1,9},{5... | collective-permute-start | bytes 884744 | tf_op jit(solution)/shard_map/ppermute | solution.py:59
  205.5 20.8 %collective-permute-start.35 = (bf16[192,768]{1,0:T(8,128)(2,1)S(1)}, bf16[192,768]{1,0:T(8,128)(2,1)S(1)}, u32[]{:S(2)}, u32[]{:S(2)}) collective-permute-start(bf16[192,768]{1,0:T(8,128)(2,1)S(1)} %get-tuple-element.166.refs_14_), channel_id=1, source_target_pairs={{0,3},{1,0},{2,1},{3,2},{4,7},{5,4},{6,5},{7,6},{8,11},{9,8},{10,9... | collective-permute-start | bytes 884744 | tf_op jit(solution)/shard_map/ppermute | solution.py:63
  211.2 25.6 %collective-permute-start.36 = (bf16[192,768]{1,0:T(8,128)(2,1)S(1)}, bf16[192,768]{1,0:T(8,128)(2,1)S(1)}, u32[]{:S(2)}, u32[]{:S(2)}) collective-permute-start(bf16[192,768]{1,0:T(8,128)(2,1)S(1)} %get-tuple-element.167.refs_15_), channel_id=1, source_target_pairs={{0,2},{1,3},{2,0},{3,1},{4,6},{5,7},{6,4},{7,5},{8,10},{9,11},{10,... | collective-permute-start | bytes 884744 | tf_op jit(solution)/shard_map/ppermute | solution.py:63
  211.2 25.6 %collective-permute-start.37 = (bf16[192,768]{1,0:T(8,128)(2,1)S(1)}, bf16[192,768]{1,0:T(8,128)(2,1)S(1)}, u32[]{:S(2)}, u32[]{:S(2)}) collective-permute-start(bf16[192,768]{1,0:T(8,128)(2,1)S(1)} %get-tuple-element.168.refs_16_), channel_id=1, source_target_pairs={{0,1},{1,2},{2,3},{3,0},{4,5},{5,6},{6,7},{7,4},{8,9},{9,10},{10,1... | collective-permute-start | bytes 884744 | tf_op jit(solution)/shard_map/ppermute | solution.py:63
  237.0 4.6 %collective-permute-start.38 = (bf16[392,1536]{1,0:T(8,128)(2,1)S(1)}, bf16[392,1536]{1,0:T(8,128)(2,1)S(1)}, u32[]{:S(2)}, u32[]{:S(2)}) collective-permute-start(bf16[392,1536]{1,0:T(8,128)(2,1)S(1)} %get-tuple-element.181), channel_id=1, source_target_pairs={{0,4},{4,0},{8,12},{12,8},{16,20},{20,16},{24,28},{28,24},{1,5},{5... | collective-permute-start | bytes 3612680 | tf_op jit(solution)/shard_map/ppermute | solution.py:59
  237.0 4.6 %collective-permute-start.34 = (bf16[384,1536]{1,0:T(8,128)(2,1)S(1)}, bf16[384,1536]{1,0:T(8,128)(2,1)S(1)}, u32[]{:S(2)}, u32[]{:S(2)}) collective-permute-start(bf16[384,1536]{1,0:T(8,128)(2,1)S(1)} %get-tuple-element.177), channel_id=1, source_target_pairs={{0,4},{4,0},{8,12},{12,8},{16,20},{20,16},{24,28},{28,24},{1,5},{5... | collective-permute-start | bytes 3538952 | tf_op jit(solution)/shard_map/ppermute | solution.py:59
  242.1 16.0 %collective-permute-start.40 = (bf16[400,768]{1,0:T(8,128)(2,1)S(1)}, bf16[400,768]{1,0:T(8,128)(2,1)S(1)}, u32[]{:S(2)}, u32[]{:S(2)}) collective-permute-start(bf16[400,768]{1,0:T(8,128)(2,1)S(1)} %get-tuple-element.184.refs_5_), channel_id=1, source_target_pairs={{0,16},{4,20},{8,24},{12,28},{16,0},{20,4},{24,8},{28,12},{1,17},{... | collective-permute-start | bytes 1843208 | tf_op jit(solution)/shard_map/ppermute | solution.py:59
  242.7 15.1 %collective-permute-start.39 = (bf16[384,768]{1,0:T(8,128)(2,1)S(1)}, bf16[384,768]{1,0:T(8,128)(2,1)S(1)}, u32[]{:S(2)}, u32[]{:S(2)}) collective-permute-start(bf16[384,768]{1,0:T(8,128)(2,1)S(1)} %get-tuple-element.183.refs_4_), channel_id=1, source_target_pairs={{0,8},{4,12},{8,0},{12,4},{16,24},{20,28},{24,16},{28,20},{1,9},{5... | collective-permute-start | bytes 1769480 | tf_op jit(solution)/shard_map/ppermute | solution.py:59
  259.5 10.5 %collective-permute-start.42 = (bf16[208,768]{1,0:T(8,128)(2,1)S(1)}, bf16[208,768]{1,0:T(8,128)(2,1)S(1)}, u32[]{:S(2)}, u32[]{:S(2)}) collective-permute-start(bf16[208,768]{1,0:T(8,128)(2,1)S(1)} %get-tuple-element.191), channel_id=1, source_target_pairs={{0,8},{4,12},{8,0},{12,4},{16,24},{20,28},{24,16},{28,20},{1,9},{5... | collective-permute-start | bytes 958472 | tf_op jit(solution)/shard_map/ppermute | solution.py:59
  259.5 10.0 %collective-permute-start.41 = (bf16[192,768]{1,0:T(8,128)(2,1)S(1)}, bf16[192,768]{1,0:T(8,128)(2,1)S(1)}, u32[]{:S(2)}, u32[]{:S(2)}) collective-permute-start(bf16[192,768]{1,0:T(8,128)(2,1)S(1)} %get-tuple-element.190), channel_id=1, source_target_pairs={{0,16},{4,20},{8,24},{12,28},{16,0},{20,4},{24,8},{28,12},{1,17},{... | collective-permute-start | bytes 884744 | tf_op jit(solution)/shard_map/ppermute | solution.py:59
  261.0 13.1 %collective-permute-start.50 = (bf16[192,768]{1,0:T(8,128)(2,1)S(1)}, bf16[192,768]{1,0:T(8,128)(2,1)S(1)}, u32[]{:S(2)}, u32[]{:S(2)}) collective-permute-start(bf16[192,768]{1,0:T(8,128)(2,1)S(1)} %shard_map.278.refs_0_.refs_1_), channel_id=1, source_target_pairs={{0,16},{4,20},{8,24},{12,28},{16,0},{20,4},{24,8},{28,12},{1,17},{... | collective-permute-start | bytes 884744 | tf_op jit(solution)/shard_map/ppermute | solution.py:59
  261.6 13.0 %collective-permute-start.49 = (bf16[192,768]{1,0:T(8,128)(2,1)S(1)}, bf16[192,768]{1,0:T(8,128)(2,1)S(1)}, u32[]{:S(2)}, u32[]{:S(2)}) collective-permute-start(bf16[192,768]{1,0:T(8,128)(2,1)S(1)} %shard_map.278.refs_0_.refs_1_), channel_id=1, source_target_pairs={{0,8},{4,12},{8,0},{12,4},{16,24},{20,28},{24,16},{28,20},{1,9},{5... | collective-permute-start | bytes 884744 | tf_op jit(solution)/shard_map/ppermute | solution.py:59
  270.1 5.3 %collective-permute-start.43 = (bf16[104,768]{1,0:T(8,128)(2,1)S(1)}, bf16[104,768]{1,0:T(8,128)(2,1)S(1)}, u32[]{:S(2)}, u32[]{:S(2)}) collective-permute-start(bf16[104,768]{1,0:T(8,128)(2,1)S(1)} %get-tuple-element.194), channel_id=1, source_target_pairs={{0,3},{1,0},{2,1},{3,2},{4,7},{5,4},{6,5},{7,6},{8,11},{9,8},{10,9... | collective-permute-start | bytes 479240 | tf_op jit(solution)/shard_map/ppermute | solution.py:63
  275.5 6.7 %collective-permute-start.51 = (bf16[192,768]{1,0:T(8,128)(2,1)S(1)}, bf16[192,768]{1,0:T(8,128)(2,1)S(1)}, u32[]{:S(2)}, u32[]{:S(2)}) collective-permute-start(bf16[192,768]{1,0:T(8,128)(2,1)S(1)} %collective-permute-done.49.refs_1_.refs_2_), channel_id=1, source_target_pairs={{0,16},{4,20},{8,24},{12,28},{16,0},{20,4},{24,8},{28,12},{1,17},{... | collective-permute-start | bytes 884744 | tf_op jit(solution)/shard_map/ppermute | solution.py:59
  276.7 9.0 %collective-permute-start.44 = (bf16[104,768]{1,0:T(8,128)(2,1)S(1)}, bf16[104,768]{1,0:T(8,128)(2,1)S(1)}, u32[]{:S(2)}, u32[]{:S(2)}) collective-permute-start(bf16[104,768]{1,0:T(8,128)(2,1)S(1)} %get-tuple-element.195), channel_id=1, source_target_pairs={{0,2},{1,3},{2,0},{3,1},{4,6},{5,7},{6,4},{7,5},{8,10},{9,11},{10,... | collective-permute-start | bytes 479240 | tf_op jit(solution)/shard_map/ppermute | solution.py:63
  277.7 7.9 %collective-permute-start.45 = (bf16[104,768]{1,0:T(8,128)(2,1)S(1)}, bf16[104,768]{1,0:T(8,128)(2,1)S(1)}, u32[]{:S(2)}, u32[]{:S(2)}) collective-permute-start(bf16[104,768]{1,0:T(8,128)(2,1)S(1)} %get-tuple-element.196), channel_id=1, source_target_pairs={{0,1},{1,2},{2,3},{3,0},{4,5},{5,6},{6,7},{7,4},{8,9},{9,10},{10,1... | collective-permute-start | bytes 479240 | tf_op jit(solution)/shard_map/ppermute | solution.py:63
  282.3 7.1 %collective-permute-start.52 = (bf16[4,192,768]{2,1,0:T(8,128)(2,1)S(1)}, bf16[4,192,768]{2,1,0:T(8,128)(2,1)S(1)}, u32[]{:S(2)}, u32[]{:S(2)}) collective-permute-start(bf16[4,192,768]{2,1,0:T(8,128)(2,1)S(1)} %shard_map.284), channel_id=1, source_target_pairs={{0,4},{4,0},{8,12},{12,8},{16,20},{20,16},{24,28},{28,24},{1,5},{5... | collective-permute-start | bytes 3538952 | tf_op jit(solution)/shard_map/ppermute | solution.py:59
  285.7 7.2 %collective-permute-start.48 = (bf16[96,768]{1,0:T(8,128)(2,1)S(1)}, bf16[96,768]{1,0:T(8,128)(2,1)S(1)}, u32[]{:S(2)}, u32[]{:S(2)}) collective-permute-start(bf16[96,768]{1,0:T(8,128)(2,1)S(1)} %shard_map.283.refs_0_.refs_1_), channel_id=1, source_target_pairs={{0,24},{4,28},{8,16},{12,20},{16,8},{20,12},{24,0},{28,4},{1,25},{... | collective-permute-start | bytes 442376 | tf_op jit(solution)/shard_map/ppermute | solution.py:59
  287.6 6.3 %collective-permute-start.47 = (bf16[96,768]{1,0:T(8,128)(2,1)S(1)}, bf16[96,768]{1,0:T(8,128)(2,1)S(1)}, u32[]{:S(2)}, u32[]{:S(2)}) collective-permute-start(bf16[96,768]{1,0:T(8,128)(2,1)S(1)} %shard_map.283.refs_0_.refs_1_), channel_id=1, source_target_pairs={{0,16},{4,20},{8,24},{12,28},{16,0},{20,4},{24,8},{28,12},{1,17},{... | collective-permute-start | bytes 442376 | tf_op jit(solution)/shard_map/ppermute | solution.py:59
  288.7 5.7 %collective-permute-start.46 = (bf16[96,768]{1,0:T(8,128)(2,1)S(1)}, bf16[96,768]{1,0:T(8,128)(2,1)S(1)}, u32[]{:S(2)}, u32[]{:S(2)}) collective-permute-start(bf16[96,768]{1,0:T(8,128)(2,1)S(1)} %shard_map.283.refs_0_.refs_1_), channel_id=1, source_target_pairs={{0,8},{4,12},{8,0},{12,4},{16,24},{20,28},{24,16},{28,20},{1,9},{5... | collective-permute-start | bytes 442376 | tf_op jit(solution)/shard_map/ppermute | solution.py:59
  294.4 2.1 collective-permute-start.53
  (31 other events, 129.7 us)
